TPU v7x, 32 devices: a whole 2x2x4 slice. The times are simulated.
32 devices in a mesh: blk: 4 (over y, x), sta: 8 (over z, core).
Axes of the slice: x: 2, y: 2, z: 4, core: 2. Of those that a mesh axis runs over, the one named last changes fastest.
Arguments:
- waveforms: bfloat16 [48, 2048], P('sta', 'blk')
- templates: bfloat16 [48, 409600], P('sta', 'blk')
- available: int32 [16, 1024], P(None, 'blk'), may hold values from 0 to 1, as said below
- usable: int32 [48], replicated, may hold values from 0 to 1
Outputs:
- detection: float32 [1024, 2048], P(('blk', 'sta'))
Inputs may be any that keep to these rules, and one draw needn't show every extreme that they name: Each template is available on one run of consecutive stations and nowhere else.
All inputs are finite; a program needn't handle non-finite values.
Results may differ from a plain program's by a relative error of at most 0.003.
Values may be sent and summed in bfloat16 or wider, within the bound.
No kernel may reach another device: no remote copies, remote signals or barrier semaphores. Data moves between devices by JAX's collectives and lax.ppermute only.
A program may use at most 128 MiB of HBM per device.

v0:
```python
import math

import jax
import jax.numpy as jnp
from jax import lax
from jax.sharding import PartitionSpec as P

TLEN = 400


FLOOR_SHARE = 0.1
EPSILON = 1e-06


def from_behind(array, axis, by):
    length = lax.axis_size(axis)
    pairs = [(i, i + by) for i in range(length) if 0 <= i + by < length]
    return lax.ppermute(array, axis, pairs)


def shifted(array, axis, by):
    length = lax.axis_size(axis)
    return lax.ppermute(array, axis, [(i, (i + by) % length) for i in range(length)])


def correlate(signal, kernels):
    length = kernels.shape[2]
    width = signal.shape[1] - length + 1
    offsets = (
        jnp.arange(width, dtype=jnp.int32)[:, None] + jnp.arange(length, dtype=jnp.int32)[None, :]
    )
    windows = jnp.take(signal, offsets, axis=1)
    return jnp.einsum("gtj,gpj->gpt", windows, kernels, preferred_element_type=jnp.float32)


def unit_templates(raw, weight):
    channels_here = raw.shape[0]
    block_rows = weight.shape[1]
    shaped = raw.astype(jnp.float32).reshape(channels_here, block_rows, TLEN)
    centred = shaped - jnp.mean(shaped, axis=2, keepdims=True)
    squared = jnp.sum(centred * centred, axis=2, keepdims=True)
    scaled = centred * lax.rsqrt(squared + EPSILON) * weight[:, :, None]
    return scaled.astype(jnp.bfloat16).reshape(channels_here, block_rows * TLEN)


def inverse_energy(extended):
    squares = extended.astype(jnp.float32) ** 2
    running = jnp.cumsum(squares, axis=1)
    running = jnp.concatenate([jnp.zeros((squares.shape[0], 1), jnp.float32), running], axis=1)
    width = extended.shape[1] - TLEN + 1
    energy = running[:, TLEN:] - running[:, :width]
    return lax.rsqrt(jnp.maximum(energy, FLOOR_SHARE * TLEN))


def block_sums(extended, inverse, pieces):
    piece_rows = pieces.shape[1] // TLEN
    kernels = pieces.reshape(pieces.shape[0], piece_rows, TLEN)
    matched = correlate(extended, kernels)
    return jnp.sum(matched * inverse[:, None, :], axis=0)


def local(waveforms, templates, available, usable):
    blocks = lax.axis_size("blk")
    shares = lax.axis_size("sta")
    my_block = lax.axis_index("blk")
    my_share = lax.axis_index("sta")
    channels_here = waveforms.shape[0]
    stations_here = channels_here // 3
    block_rows = available.shape[1]
    own_rows = block_rows // shares
    seg_width = waveforms.shape[1]
    mine_avail = lax.dynamic_slice_in_dim(available, my_share * stations_here, stations_here, 0)
    mine_usable = lax.dynamic_slice_in_dim(usable, my_share * channels_here, channels_here, 0)
    weight = (
        jnp.repeat(mine_avail, 3, axis=0).astype(jnp.float32)
        * mine_usable.astype(jnp.float32)[:, None]
    )
    own_pieces = unit_templates(templates, weight)
    station_usable = jnp.sum(usable.reshape(-1, 3), axis=1).astype(jnp.float32)
    owned_avail = lax.dynamic_slice_in_dim(available, my_share * own_rows, own_rows, 1).astype(
        jnp.float32
    )
    counted = jnp.sum(owned_avail * station_usable[:, None], axis=0)
    tail = from_behind(waveforms[:, : TLEN - 1], "blk", -1)
    extended = jnp.concatenate([waveforms, tail], axis=1)
    inverse = inverse_energy(extended)

    def stack_block(pieces):
        summed = block_sums(extended, inverse, pieces)
        return lax.psum_scatter(summed, "sta", scatter_dimension=0, tiled=True)

    def place(buffer, value, which):
        return lax.dynamic_update_slice_in_dim(buffer, value[None], which, 0)

    buffer = jnp.zeros((blocks, own_rows, seg_width), jnp.float32)
    buffer = place(buffer, stack_block(own_pieces), my_block)
    moving = own_pieces
    for hop_index in range(1, blocks):
        moving = shifted(moving, "blk", 1)
        buffer = place(buffer, stack_block(moving), (my_block - hop_index) % blocks)
    gathered = lax.all_to_all(buffer, "blk", split_axis=0, concat_axis=2, tiled=True)
    stacked = gathered[0]
    return math.sqrt(TLEN) * stacked * lax.rsqrt(jnp.maximum(counted, 1.0))[:, None]


def solution(mesh):
    return jax.shard_map(
        local,
        mesh=mesh,
        in_specs=(P("sta", "blk"), P("sta", "blk"), P(None, "blk"), P()),
        out_specs=P(("blk", "sta"), None),
        check_vma=False,
    )
```

profile of v0, /device:TPU:0, one launch (start us, length us, event | category | flops | bytes accessed | tf_op | source)
XLA Modules:
  0.0 1028.3 jit_solution(17871238405603491927)
XLA Ops:
  7.8 4.9 reshape.76
  13.8 2.0 mul.105
  15.7 5.8 mul.111
  21.6 2.0 mul.99
  23.6 5.9 mul.109
  29.4 1.9 sub.25
  31.3 5.9 sub.28
  37.2 6.3 multiply_convert_fusion
  43.5 3.6 collective-permute-start.1
  48.8 2.5 copy.37
  51.3 3.0 reshape.93
  54.3 2.1 broadcast_clamp_fusion
  58.8 774.0 %gather_fusion = bf16[204800,6]{1,0:T(8,128)(2,1)} fusion(bf16[6,911]{0,1:T(8,128)(2,1)S(1)} %copy.38, s32[204800]{0:T(1024)} %broadcast_clamp_fusion), kind=kCustom, calls=%fused_computation.clone | custom fusion | bytes 5734400 | tf_op jit(solution)/shard_map/jit(_take)/gather | solution.py:32
  832.8 46.5 %copy.39 = bf16[512,400,6]{0,1,2:T(8,128)(2,1)} copy(bf16[512,400,6]{2,1,0:T(8,128)(2,1)} %bitcast.48) | data formatting | bytes 4915200 | tf_op jit(solution)/shard_map/jit(_take)/gather | solution.py:32
  879.4 3.7 multiply_reduce_fusion.3
  883.2 3.0 collective-permute-start.2
  886.2 3.3 reshape.98
  889.5 4.3 reshape.79
  893.8 4.0 multiply_reduce_fusion.2
  897.9 23.7 %collective-permute-done.2 = bf16[6,102400]{1,0:T(8,128)(2,1)S(1)} collective-permute-done((bf16[6,102400]{1,0:T(8,128)(2,1)}, bf16[6,102400]{1,0:T(8,128)(2,1)S(1)}, u32[]{:S(2)}, u32[]{:S(2)}) %collective-permute-start.2) | collective-permute-done | bytes 1228832 | tf_op jit(solution)/shard_map/ppermute | solution.py:23
  921.7 1.7 collective-permute-start.3
  923.4 1.8 reshape.100
  925.2 4.3 reshape.80
  929.5 4.1 multiply_reduce_fusion.1
  933.7 25.4 %collective-permute-done.3 = bf16[6,102400]{1,0:T(8,128)(2,1)} collective-permute-done((bf16[6,102400]{1,0:T(8,128)(2,1)S(1)}, bf16[6,102400]{1,0:T(8,128)(2,1)}, u32[]{:S(2)}, u32[]{:S(2)}) %collective-permute-start.3) | collective-permute-done | bytes 1228832 | tf_op jit(solution)/shard_map/ppermute | solution.py:23
  959.0 3.3 reshape.102
  962.3 3.5 reshape.81
  965.8 3.6 multiply_reduce_fusion
  973.5 5.4 reduce-scatter.9.cloned.1.call-done
  980.3 29.9 %reduce-scatter.11.cloned.1.call-done = f32[32,512]{1,0:T(8,128)} async-done(((f32[256,512]{1,0:T(8,128)}), f32[32,512]{1,0:T(8,128)}) %reduce-scatter.11.cloned.1.call-update) | async-done | bytes 65552 | tf_op jit(solution)/shard_map/reduce_scatter | solution.py:90
  1011.7 3.7 all-to-all-start
  1015.4 5.4 all-to-all-done
  (56 shorter events, 14.7 us)
Async XLA Ops:
  6.5 963.2 %reduce-scatter.5.cloned.1.call-start = ((), (), s32[]{:S(2)}) async-start(), calls=%async_computation.5 | async-start | bytes 589824 | tf_op jit(solution)/shard_map/reduce_scatter | solution.py:90
  6.5 49.9 %collective-permute-start = (bf16[6,399]{1,0:T(8,128)(2,1)}, bf16[6,399]{1,0:T(8,128)(2,1)S(1)}, u32[]{:S(2)}, u32[]{:S(2)}) collective-permute-start(bf16[6,399]{1,0:T(8,128)(2,1)} %bitcast.56), channel_id=1, source_target_pairs={{8,0},{16,8},{24,16},{9,1},{17,9},{25,17},{10,2},{18,10},{26,18},{... | collective-permute-start | bytes 14372 | tf_op jit(solution)/shard_map/ppermute | solution.py:18
  12.7 0.9 copy-start.2
  12.7 0.9 copy-start.3
  43.5 839.7 %collective-permute-start.1 = (bf16[6,102400]{1,0:T(8,128)(2,1)}, bf16[6,102400]{1,0:T(8,128)(2,1)}, u32[]{:S(2)}, u32[]{:S(2)}) collective-permute-start(bf16[6,102400]{1,0:T(8,128)(2,1)} %multiply_convert_fusion), channel_id=1, source_target_pairs={{0,8},{8,16},{16,24},{24,0},{1,9},{9,17},{17,25},{25,1},{2,10},{10... | collective-permute-start | bytes 3686408 | tf_op jit(solution)/shard_map/ppermute | solution.py:23
  48.8 7.6 copy-start.1
  832.8 46.6 %copy-start = (pred[512,400]{0,1:T(8,128)(4,1)S(1)}, pred[512,400]{0,1:T(8,128)(4,1)}, u32[]{:S(2)}) copy-start(pred[512,400]{0,1:T(8,128)(4,1)} %compare_and_fusion) | copy-start | bytes 614404
  883.2 88.8 %reduce-scatter.7.cloned.1.call-start = ((), (), s32[]{:S(2)}) async-start(), calls=%async_computation.6 | async-start | bytes 589824 | tf_op jit(solution)/shard_map/reduce_scatter | solution.py:90
  883.2 38.4 %collective-permute-start.2 = (bf16[6,102400]{1,0:T(8,128)(2,1)}, bf16[6,102400]{1,0:T(8,128)(2,1)S(1)}, u32[]{:S(2)}, u32[]{:S(2)}) collective-permute-start(bf16[6,102400]{1,0:T(8,128)(2,1)} %collective-permute-done.1), channel_id=1, source_target_pairs={{0,8},{8,16},{16,24},{24,0},{1,9},{9,17},{17,25},{25,1},{2,10},{10... | collective-permute-start | bytes 3686408 | tf_op jit(solution)/shard_map/ppermute | solution.py:23
  897.9 80.9 %reduce-scatter.9.cloned.1.call-start = ((), (), s32[]{:S(2)}) async-start(), calls=%async_computation.7 | async-start | bytes 589824 | tf_op jit(solution)/shard_map/reduce_scatter | solution.py:90
  921.7 37.3 %collective-permute-start.3 = (bf16[6,102400]{1,0:T(8,128)(2,1)S(1)}, bf16[6,102400]{1,0:T(8,128)(2,1)}, u32[]{:S(2)}, u32[]{:S(2)}) collective-permute-start(bf16[6,102400]{1,0:T(8,128)(2,1)S(1)} %collective-permute-done.2), channel_id=1, source_target_pairs={{0,8},{8,16},{16,24},{24,0},{1,9},{9,17},{17,25},{25,1},{2,10},{10... | collective-permute-start | bytes 3686408 | tf_op jit(solution)/shard_map/ppermute | solution.py:23
  933.6 76.6 %reduce-scatter.11.cloned.1.call-start = ((), (), s32[]{:S(2)}) async-start(), calls=%async_computation.8 | async-start | bytes 589824 | tf_op jit(solution)/shard_map/reduce_scatter | solution.py:90
  1011.7 9.1 all-to-all-start
Sparse Core Ops, SparseCore 0:
  883.3 32.6 reduce-scatter.4
  918.3 29.0 reduce-scatter.6
  949.7 29.0 reduce-scatter.8
  981.0 29.1 reduce-scatter.10
where the time goes:
time: 1050 us; the launch traced here: 1030 us
  local copies, waits for them, and re-layouts  882 us (84%)
  waiting for transfers between devices  89.8 us (9%)
  matrix products  15.4 us (1%)
  other arithmetic  14.2 us (1%)
  starting transfers between devices  13.4 us (1%)
  between operations  13.4 us (1%)
    gather x2, local copies, waits for them, and re-layouts, correlate(): windows = jnp.take(signal, offsets, axis=1)  820 us
    ppermute x3, waiting for transfers between devices, shifted(): lax.ppermute(array, axis, [(i, (i + by) % length) for i in range(length)])  49.1 us
    reduce_scatter x4, waiting for transfers between devices, stack_block(): return lax.psum_scatter(summed, 'sta', scatter_dimension=0, tiled=True)  35.3 us
  transfers between devices with their start and end apart: 9, of which 5 were waited for; matrix products, arithmetic and copies ran while one was open for 88% of the time, Pallas kernels for 0%

commit v1 on v0

v1 whole, which is shorter than its diff:
```python
import functools
import math

import jax
import jax.numpy as jnp
from jax import lax
from jax.experimental import pallas as pl
from jax.experimental.pallas import tpu as pltpu
from jax.sharding import PartitionSpec as P

TLEN = 400
COMPONENTS = 3
LANES = 128
SUBLANES = 8

FLOOR_SHARE = 0.1
EPSILON = 1e-06

PERIOD = LANES // math.gcd(TLEN, LANES)
PERIOD_TILES = PERIOD * TLEN // LANES
DEPTH_TILES = -(-TLEN // LANES)
DEPTH = DEPTH_TILES * LANES
VMEM_LIMIT = 48 << 20


def exchanged(array, axis, by):
    length = lax.axis_size(axis)
    return lax.ppermute(array, axis, [(i, i ^ by) for i in range(length)])


def template_kernel(shares, raw_ref, avail_ref, usable_ref, out_ref, flat, rows, avail_cols):
    channels, width = raw_ref.shape
    stations, count = avail_ref.shape
    groups = count // PERIOD
    tiles = width // LANES
    stations_here = channels // COMPONENTS
    own = count // shares
    me = lax.axis_index("sta")

    unroll = 8 if tiles % 8 == 0 else 1

    def spread(step, carry):
        for sub in range(unroll):
            tile = step * unroll + sub
            piece = raw_ref[:, pl.ds(pl.multiple_of(tile * LANES, LANES), LANES)]
            flat[pl.ds(pl.multiple_of(tile * SUBLANES, SUBLANES), channels), :] = piece.astype(
                jnp.float32
            )
        return carry

    lax.fori_loop(0, tiles // unroll, spread, 0)

    station_row = lax.broadcasted_iota(jnp.int32, (stations, LANES), 0)
    avail = avail_ref[...].astype(jnp.float32)
    for local_station in range(stations_here):
        chosen = (station_row == me * stations_here + local_station).astype(jnp.float32)
        avail_cols[local_station] = lax.dot_general(
            avail, chosen, (((0,), (0,)), ((), ())), preferred_element_type=jnp.float32
        )

    lane = lax.broadcasted_iota(jnp.int32, (groups, LANES), 1)
    last = TLEN - (DEPTH_TILES - 1) * LANES
    block_lane = lax.broadcasted_iota(jnp.int32, (own, LANES), 1)

    def one_channel(channel, carry):
        for which in range(PERIOD):
            first, offset = divmod(which * TLEN, LANES)
            pieces = []
            for part in range(DEPTH_TILES):
                start = (first + part) * SUBLANES + channel
                piece = flat[pl.ds(start, groups, stride=PERIOD_TILES * SUBLANES), :]
                if offset:
                    piece = pltpu.roll(piece, LANES - offset, 1)
                pieces.append(piece)
            for part in range(DEPTH_TILES):
                value = pieces[part]
                if part + 1 < DEPTH_TILES:
                    if offset:
                        value = jnp.where(lane < LANES - offset, value, pieces[part + 1])
                else:
                    value = jnp.where(lane < last, value, 0.0)
                rows[part, pl.ds(which, groups, stride=PERIOD), :] = value
        use = usable_ref[me * channels + channel].astype(jnp.float32)
        for place in range(shares):
            core, chip = divmod(place, shares // 2)
            owner = me ^ (chip * 2 + core)
            here = pl.ds(pl.multiple_of(owner * own, own), own)
            parts = [rows[part, here, :] for part in range(DEPTH_TILES)]
            mean = jnp.sum(sum(parts), axis=1, keepdims=True) * (1.0 / TLEN)
            centred = [value - mean for value in parts]
            centred[-1] = jnp.where(block_lane < last, centred[-1], 0.0)
            squared = jnp.sum(sum(value * value for value in centred), axis=1, keepdims=True)
            weight = avail_cols[channel // COMPONENTS, here, :] * use
            factor = lax.rsqrt(squared + EPSILON) * weight
            for part in range(DEPTH_TILES):
                out_ref[
                    channel, place * own : (place + 1) * own, part * LANES : (part + 1) * LANES
                ] = (centred[part] * factor).astype(jnp.bfloat16)
        return carry

    lax.fori_loop(0, channels, one_channel, 0)


def weighted_templates(raw, available, usable, shares):
    channels, width = raw.shape
    stations, count = available.shape
    return pl.pallas_call(
        functools.partial(template_kernel, shares),
        out_shape=jax.ShapeDtypeStruct((channels, count, DEPTH), jnp.bfloat16),
        in_specs=[
            pl.BlockSpec(memory_space=pltpu.VMEM),
            pl.BlockSpec(memory_space=pltpu.VMEM),
            pl.BlockSpec(memory_space=pltpu.SMEM),
        ],
        out_specs=pl.BlockSpec(memory_space=pltpu.VMEM),
        scratch_shapes=[
            pltpu.VMEM((width // LANES * SUBLANES, LANES), jnp.float32),
            pltpu.VMEM((DEPTH_TILES, count, LANES), jnp.float32),
            pltpu.VMEM((channels // COMPONENTS, count, LANES), jnp.float32),
        ],
        compiler_params=pltpu.CompilerParams(vmem_limit_bytes=VMEM_LIMIT),
        cost_estimate=pl.CostEstimate(
            flops=20 * channels * count * DEPTH, transcendentals=0, bytes_accessed=4 << 20
        ),
        name="templates",
    )(raw, available, usable)


def correlate_kernel(blocks, weighted_ref, *refs):
    segments = refs[:blocks]
    mine_ref, other_ref, record, windows, scale = refs[blocks:]
    channels, count, depth = weighted_ref.shape
    segment = segments[0].shape[1]
    lags = blocks * segment
    wide = record.shape[1]
    base = windows.shape[2]
    half = count // 2
    me = lax.axis_index("blk")

    record[...] = jnp.zeros_like(record)
    for by in range(blocks):
        start = pl.multiple_of((me ^ by) * segment, LANES)
        record[0:channels, pl.ds(start, segment)] = segments[by][...].astype(jnp.float32)

    def ahead(value, by):
        return pltpu.roll(value, value.shape[1] - by, 1) if by else value

    samples = record[...]
    power = samples * samples
    energy, taken, span = None, 0, 1
    while True:
        if TLEN & span:
            term = ahead(power, taken)
            energy = term if energy is None else energy + term
            taken += span
        if 2 * span > TLEN:
            break
        power = power + ahead(power, span)
        span *= 2
    scale[...] = lax.rsqrt(jnp.maximum(energy[:, :lags], FLOOR_SHARE * TLEN))

    sublane = lax.broadcasted_iota(jnp.int32, (SUBLANES, wide), 0)
    for channel in range(channels):
        shifted = jnp.broadcast_to(record[channel : channel + 1, :], (SUBLANES, wide))
        for bit in (1, 2, 4):
            shifted = jnp.where((sublane & bit) != 0, ahead(shifted, bit), shifted)
        for row in range(0, LANES, 2 * SUBLANES):
            pair = jnp.concatenate(
                [
                    ahead(shifted, row)[:, :base],
                    ahead(shifted, row + SUBLANES)[:, :base],
                ],
                axis=0,
            )
            windows[channel, row : row + 2 * SUBLANES, :] = pair.astype(jnp.bfloat16)

    tile = 2 * LANES

    def one_tile(step, carry):
        first = step * tile
        total = None
        for channel in range(channels):
            signal = jnp.concatenate(
                [
                    windows[channel, :, pl.ds(pl.multiple_of(first + part * LANES, LANES), tile)]
                    for part in range(depth // LANES)
                ],
                axis=0,
            )
            matched = jnp.dot(weighted_ref[channel], signal, preferred_element_type=jnp.float32)
            here = pl.ds(pl.multiple_of(first, LANES), tile)
            term = matched * scale[channel : channel + 1, here]
            total = term if total is None else total + term
        here = pl.ds(pl.multiple_of(first, LANES), tile)
        mine_ref[:, here] = total[:half]
        other_ref[:, here] = total[half:].astype(other_ref.dtype)
        return carry

    lax.fori_loop(0, lags // tile, one_tile, 0)


def correlations(weighted, segments):
    channels, count, depth = weighted.shape
    blocks = len(segments)
    lags = blocks * segments[0].shape[1]
    half = count // 2
    return pl.pallas_call(
        functools.partial(correlate_kernel, blocks),
        out_shape=(
            jax.ShapeDtypeStruct((half, lags), jnp.float32),
            jax.ShapeDtypeStruct((half, lags), jnp.bfloat16),
        ),
        in_specs=[pl.BlockSpec(memory_space=pltpu.VMEM)] * (1 + blocks),
        out_specs=(pl.BlockSpec(memory_space=pltpu.VMEM),) * 2,
        scratch_shapes=[
            pltpu.VMEM((SUBLANES, lags + depth + LANES), jnp.float32),
            pltpu.VMEM((channels, LANES, lags + depth), jnp.bfloat16),
            pltpu.VMEM((SUBLANES, lags), jnp.float32),
        ],
        compiler_params=pltpu.CompilerParams(vmem_limit_bytes=VMEM_LIMIT),
        cost_estimate=pl.CostEstimate(
            flops=2 * channels * count * depth * lags, transcendentals=0, bytes_accessed=4 << 20
        ),
        name="correlate",
    )(weighted, *segments)


def local(waveforms, templates, available, usable):
    blocks = lax.axis_size("blk")
    shares = lax.axis_size("sta")
    my_share = lax.axis_index("sta")
    block_rows = available.shape[1]
    own_rows = block_rows // shares
    chips = shares // 2

    segments = {0: waveforms}
    for by in reversed(range(1, blocks)):
        segments[by] = exchanged(waveforms, "blk", by)
    weighted = weighted_templates(templates, available, usable, shares)
    mine, other = correlations(weighted, [segments[by] for by in range(blocks)])
    summed = mine + exchanged(other, "sta", 1).astype(jnp.float32)
    summed = summed.reshape(chips, own_rows, summed.shape[1])
    order = sorted(range(1, chips), key=lambda by: -(by ^ (by >> 1)))
    arrived = [
        exchanged(summed[by].astype(jnp.bfloat16), "sta", 2 * by) for by in order
    ]
    stacked = summed[0]
    for term in arrived:
        stacked = stacked + term.astype(jnp.float32)

    station_usable = jnp.sum(usable.reshape(-1, COMPONENTS), axis=1).astype(jnp.float32)
    owned = lax.dynamic_slice_in_dim(available, my_share * own_rows, own_rows, 1)
    counted = jnp.sum(owned.astype(jnp.float32) * station_usable[:, None], axis=0)
    return math.sqrt(TLEN) * stacked * lax.rsqrt(jnp.maximum(counted, 1.0))[:, None]


def solution(mesh):
    return jax.shard_map(
        local,
        mesh=mesh,
        in_specs=(P("sta", "blk"), P("sta", "blk"), P(None, "blk"), P()),
        out_specs=P(("blk", "sta"), None),
        check_vma=False,
    )
```

time: 1050 us -> 39.4 us (0.04); the launches traced: 1030 us -> 39.2 us
  local copies, waits for them, and re-layouts: 882 us -> 2.93 us
  waiting for transfers between devices: 89.8 us -> 13.5 us
  matrix products: 15.4 us -> 0 us
  between operations: 13.4 us -> 0.13 us
  other arithmetic: 14.2 us -> 1.18 us
  Pallas kernels: 0 us -> 12.2 us
    gather x2 -> x0, local copies, waits for them, and re-layouts: 820 us -> none  [correlate(): windows = jnp.take(signal, offsets, axis=1)]
    ppermute x4 -> x7, waiting for transfers between devices: 49.1 us -> 13.5 us  [exchanged(): return lax.ppermute(array, axis, [(i, i ^ by) for i in range(length)])]
    reduce_scatter x4 -> x0, waiting for transfers between devices: 35.3 us -> none  [stack_block(): return lax.psum_scatter(summed, 'sta', scatter_dimension=0, tiled=True)]
    reshape x5 -> x1, local copies, waits for them, and re-layouts: 17 us -> 0.08 us  [local(): usable.reshape(-1, COMPONENTS)]
    mul x4 -> x0, local copies, waits for them, and re-layouts: 15.6 us -> none  [unit_templates(): scaled = centred * lax.rsqrt(squared + EPSILON) * weight[:, :, None]]
    dot_general x4 -> x0, matrix products: 15.4 us -> none  [correlate(): jnp.einsum('gtj,gpj->gpt', windows, kernels, preferred_element_type=jnp.f...]
    pallas_call x0 -> x2, Pallas kernels: none -> 12.2 us  [the longest x1 7.31 us: correlations(): pl.pallas_call(functools.partial(correlate_kernel, blocks), out_shape=(ja...]
  transfers between devices with their start and end apart: 9 -> 7, of which waited for: 5 -> 4; matrix products, arithmetic and copies ran while one was open for 88% -> 1% of each run, Pallas kernels for 0% -> 12%
where the time goes in v1:
time: 39.4 us; the launch traced here: 39.2 us
  waiting for transfers between devices  13.5 us (34%)
  Pallas kernels  12.2 us (31%)
  starting transfers between devices  9.24 us (23%)
  local copies, waits for them, and re-layouts  2.93 us (7%)
  other arithmetic  1.18 us (3%)
    ppermute x7, waiting for transfers between devices, exchanged(): return lax.ppermute(array, axis, [(i, i ^ by) for i in range(length)])  13.5 us
    ppermute x7, starting transfers between devices, exchanged(): return lax.ppermute(array, axis, [(i, i ^ by) for i in range(length)])  9.24 us
    pallas_call x1, Pallas kernels, correlations(): pl.pallas_call(functools.partial(correlate_kernel, blocks), out_shape=(ja...  7.31 us
    pallas_call x1, Pallas kernels, weighted_templates(): pl.pallas_call(functools.partial(template_kernel, shares), out_shape=jax....  4.86 us
    unnamed x12, local copies, waits for them, and re-layouts  2.82 us
    mul x2, other arithmetic, local(): math.sqrt(TLEN) * stacked * lax.rsqrt(jnp.maximum(counted, 1.0))[:, None]  0.79 us
  transfers between devices with their start and end apart: 7, of which 4 were waited for; matrix products, arithmetic and copies ran while one was open for 1% of the time, Pallas kernels for 12%

profile of v1, /device:TPU:0, one launch (start us, length us, event | category | flops | bytes accessed | tf_op | source)
XLA Modules:
  0.0 39.2 jit_solution(4694713891628884219)
XLA Ops:
  0.0 2.9 %collective-permute-start = (bf16[6,512]{1,0:T(8,128)(2,1)}, bf16[6,512]{1,0:T(8,128)(2,1)S(1)}, u32[]{:S(2)}, u32[]{:S(2)}) collective-permute-start(bf16[6,512]{1,0:T(8,128)(2,1)} %refs_0_.1), channel_id=1, source_target_pairs={{0,8},{8,0},{16,24},{24,16},{1,9},{9,1},{17,25},{25,17},{2,10},{10... | collective-permute-start | bytes 18440 | tf_op jit(solution)/shard_map/ppermute | solution.py:28
  2.9 1.5 %collective-permute-start.1 = (bf16[6,512]{1,0:T(8,128)(2,1)}, bf16[6,512]{1,0:T(8,128)(2,1)S(1)}, u32[]{:S(2)}, u32[]{:S(2)}) collective-permute-start(bf16[6,512]{1,0:T(8,128)(2,1)} %refs_0_.1), channel_id=1, source_target_pairs={{0,16},{8,24},{16,0},{24,8},{1,17},{9,25},{17,1},{25,9},{2,18},{10... | collective-permute-start | bytes 18440 | tf_op jit(solution)/shard_map/ppermute | solution.py:28
  4.5 0.0 collective-permute-start.2
  4.5 0.0 copy-start
  4.5 1.4 %copy-done = bf16[6,102400]{1,0:T(8,128)(2,1)S(1)} copy-done((bf16[6,102400]{1,0:T(8,128)(2,1)S(1)}, bf16[6,102400]{1,0:T(8,128)(2,1)}, u32[]{:S(2)}) %copy-start) | copy-done | bytes 1228824
  5.9 0.0 copy-start.1
  5.9 0.7 %copy-done.1 = s32[16,256]{1,0:T(8,128)S(1)} copy-done((s32[16,256]{1,0:T(8,128)S(1)}, s32[16,256]{1,0:T(8,128)}, u32[]{:S(2)}) %copy-start.1) | copy-done | bytes 16408
  6.6 0.0 copy-start.3
  6.6 0.7 %copy-done.3 = s32[48]{0:T(128)S(1)} copy-done((s32[48]{0:T(128)S(1)}, s32[48]{0:T(128)}, u32[]{:S(2)}) %copy-start.3) | copy-done | bytes 216
  7.3 4.9 %templates.1.weighted_ref = bf16[6,256,512]{2,1,0:T(8,128)(2,1)S(1)} custom-call(bf16[6,102400]{1,0:T(8,128)(2,1)S(1)} %copy-done, s32[16,256]{1,0:T(8,128)S(1)} %copy-done.1, s32[48]{0:T(128)S(1)} %copy-done.3), custom_call_target="tpu_custom_call" | custom-call | flops 15728640 | bytes 4194304 | tf_op jit(solution)/shard_map/templates/pallas_call | solution.py:107
  12.1 0.0 copy-start.4
  12.1 0.0 copy-start.2
  12.2 0.0 collective-permute-done.refs_1_
  12.2 0.0 collective-permute-done.1.refs_2_
  12.2 0.0 collective-permute-done.2.refs_3_
  12.2 0.0 copy-done.5
  12.2 7.3 %correlate.1 = (f32[128,2048]{1,0:T(8,128)S(1)}, bf16[128,2048]{1,0:T(8,128)(2,1)S(1)}) custom-call(bf16[6,256,512]{2,1,0:T(8,128)(2,1)S(1)} %templates.1.weighted_ref, bf16[6,512]{1,0:T(8,128)(2,1)S(1)} %copy-done.5, bf16[6,512]{1,0:T(8,128)(2,1)S(1)} %collective-permute-done.refs_1_, bf16[6,512]{1,0:T(8,128)(2,1)S(1)} %collective-permute-done.1.refs_2_, ...), custom_call_target="tpu_custom_call" | custom-call | flops 3221225472 | bytes 4194304 | tf_op jit(solution)/shard_map/correlate/pallas_call | solution.py:207
  19.5 0.1 collective-permute-start.3
  19.6 0.0 copy-done.4
  19.6 0.1 reshape.19
  19.7 0.1 reduce_sum.18
  19.8 0.0 copy-done.2
  19.8 0.1 multiply_reduce_fusion
  19.9 1.6 %collective-permute-done.3 = bf16[128,2048]{1,0:T(8,128)(2,1)S(1)} collective-permute-done((bf16[128,2048]{1,0:T(8,128)(2,1)S(1)}, bf16[128,2048]{1,0:T(8,128)(2,1)S(1)}, u32[]{:S(2)}, u32[]{:S(2)}) %collective-permute-start.3) | collective-permute-done | bytes 524320 | tf_op jit(solution)/shard_map/ppermute | solution.py:28
  21.5 0.2 fusion.3
  21.7 2.1 %collective-permute-start.6 = (bf16[32,2048]{1,0:T(8,128)(2,1)S(1)}, bf16[32,2048]{1,0:T(8,128)(2,1)S(1)}, u32[]{:S(2)}, u32[]{:S(2)}) collective-permute-start(bf16[32,2048]{1,0:T(8,128)(2,1)S(1)} %get-tuple-element.12), channel_id=1, source_target_pairs={{0,2},{1,3},{2,0},{3,1},{4,6},{5,7},{6,4},{7,5},{8,10},{9,11},{10,... | collective-permute-start | bytes 393224 | tf_op jit(solution)/shard_map/ppermute | solution.py:28
  23.8 2.5 %collective-permute-start.5 = (bf16[32,2048]{1,0:T(8,128)(2,1)S(1)}, bf16[32,2048]{1,0:T(8,128)(2,1)S(1)}, u32[]{:S(2)}, u32[]{:S(2)}) collective-permute-start(bf16[32,2048]{1,0:T(8,128)(2,1)S(1)} %get-tuple-element.13), channel_id=1, source_target_pairs={{0,6},{1,7},{2,4},{3,5},{4,2},{5,3},{6,0},{7,1},{8,14},{9,15},{10,... | collective-permute-start | bytes 393224 | tf_op jit(solution)/shard_map/ppermute | solution.py:28
  26.3 0.1 collective-permute-start.4
  26.4 1.2 %collective-permute-done.6 = bf16[32,2048]{1,0:T(8,128)(2,1)S(1)} collective-permute-done((bf16[32,2048]{1,0:T(8,128)(2,1)S(1)}, bf16[32,2048]{1,0:T(8,128)(2,1)S(1)}, u32[]{:S(2)}, u32[]{:S(2)}) %collective-permute-start.6) | collective-permute-done | bytes 131104 | tf_op jit(solution)/shard_map/ppermute | solution.py:28
  27.6 5.9 %collective-permute-done.5 = bf16[32,2048]{1,0:T(8,128)(2,1)S(1)} collective-permute-done((bf16[32,2048]{1,0:T(8,128)(2,1)S(1)}, bf16[32,2048]{1,0:T(8,128)(2,1)S(1)}, u32[]{:S(2)}, u32[]{:S(2)}) %collective-permute-start.5) | collective-permute-done | bytes 131104 | tf_op jit(solution)/shard_map/ppermute | solution.py:28
  33.5 4.8 %collective-permute-done.4 = bf16[32,2048]{1,0:T(8,128)(2,1)S(1)} collective-permute-done((bf16[32,2048]{1,0:T(8,128)(2,1)S(1)}, bf16[32,2048]{1,0:T(8,128)(2,1)S(1)}, u32[]{:S(2)}, u32[]{:S(2)}) %collective-permute-start.4) | collective-permute-done | bytes 131104 | tf_op jit(solution)/shard_map/ppermute | solution.py:28
  38.4 0.8 %fusion.2 = f32[32,2048]{1,0:T(8,128)} fusion(f32[128,2048]{1,0:T(8,128)S(1)} %get-tuple-element.10, bf16[32,2048]{1,0:T(8,128)(2,1)S(1)} %collective-permute-done.6, bf16[32,2048]{1,0:T(8,128)(2,1)S(1)} %collective-permute-done.5, bf16[32,2048]{1,0:T(8,128)(2,1)S(1)} %collective-permute-done.4, f32[32]{0:T(128)S(1)} %rsqrt_multiply_fusion), kind=kLoop, calls=%fused_computation.4 | loop fusion | flops 458752 | bytes 917632 | tf_op jit(solution)/shard_map/mul | solution.py:254
  (4 shorter events, 0.0 us)
Async XLA Ops:
  0.0 12.2 %collective-permute-start = (bf16[6,512]{1,0:T(8,128)(2,1)}, bf16[6,512]{1,0:T(8,128)(2,1)S(1)}, u32[]{:S(2)}, u32[]{:S(2)}) collective-permute-start(bf16[6,512]{1,0:T(8,128)(2,1)} %refs_0_.1), channel_id=1, source_target_pairs={{0,8},{8,0},{16,24},{24,16},{1,9},{9,1},{17,25},{25,17},{2,10},{10... | collective-permute-start | bytes 18440 | tf_op jit(solution)/shard_map/ppermute | solution.py:28
  2.9 9.2 %collective-permute-start.1 = (bf16[6,512]{1,0:T(8,128)(2,1)}, bf16[6,512]{1,0:T(8,128)(2,1)S(1)}, u32[]{:S(2)}, u32[]{:S(2)}) collective-permute-start(bf16[6,512]{1,0:T(8,128)(2,1)} %refs_0_.1), channel_id=1, source_target_pairs={{0,16},{8,24},{16,0},{24,8},{1,17},{9,25},{17,1},{25,9},{2,18},{10... | collective-permute-start | bytes 18440 | tf_op jit(solution)/shard_map/ppermute | solution.py:28
  4.5 7.7 %collective-permute-start.2 = (bf16[6,512]{1,0:T(8,128)(2,1)}, bf16[6,512]{1,0:T(8,128)(2,1)S(1)}, u32[]{:S(2)}, u32[]{:S(2)}) collective-permute-start(bf16[6,512]{1,0:T(8,128)(2,1)} %refs_0_.1), channel_id=1, source_target_pairs={{0,24},{8,16},{16,8},{24,0},{1,25},{9,17},{17,9},{25,1},{2,26},{10... | collective-permute-start | bytes 18440 | tf_op jit(solution)/shard_map/ppermute | solution.py:28
  4.5 1.4 %copy-start = (bf16[6,102400]{1,0:T(8,128)(2,1)S(1)}, bf16[6,102400]{1,0:T(8,128)(2,1)}, u32[]{:S(2)}) copy-start(bf16[6,102400]{1,0:T(8,128)(2,1)} %raw_ref.1) | copy-start | bytes 3686404
  5.9 0.7 %copy-start.1 = (s32[16,256]{1,0:T(8,128)S(1)}, s32[16,256]{1,0:T(8,128)}, u32[]{:S(2)}) copy-start(s32[16,256]{1,0:T(8,128)} %avail_ref.1) | copy-start | bytes 49156
  6.6 0.7 %copy-start.3 = (s32[48]{0:T(128)S(1)}, s32[48]{0:T(128)}, u32[]{:S(2)}) copy-start(s32[48]{0:T(128)} %usable_ref.1) | copy-start | bytes 580
  7.3 4.9 %copy-start.5 = (bf16[6,512]{1,0:T(8,128)(2,1)S(1)}, bf16[6,512]{1,0:T(8,128)(2,1)}, u32[]{:S(2)}) copy-start(bf16[6,512]{1,0:T(8,128)(2,1)} %refs_0_.1) | copy-start | bytes 18436
  12.1 7.5 %copy-start.4 = (s32[48]{0:T(128)S(1)}, s32[48]{0:T(128)}, u32[]{:S(2)}) copy-start(s32[48]{0:T(128)} %usable_ref.1) | copy-start | bytes 580
  12.1 7.7 %copy-start.2 = (s32[16,256]{1,0:T(8,128)S(1)}, s32[16,256]{1,0:T(8,128)}, u32[]{:S(2)}) copy-start(s32[16,256]{1,0:T(8,128)} %avail_ref.1) | copy-start | bytes 49156
  19.5 2.0 %collective-permute-start.3 = (bf16[128,2048]{1,0:T(8,128)(2,1)S(1)}, bf16[128,2048]{1,0:T(8,128)(2,1)S(1)}, u32[]{:S(2)}, u32[]{:S(2)}) collective-permute-start(bf16[128,2048]{1,0:T(8,128)(2,1)S(1)} %get-tuple-element.8), channel_id=1, source_target_pairs={{0,1},{1,0},{2,3},{3,2},{4,5},{5,4},{6,7},{7,6},{8,9},{9,8},{10,11... | collective-permute-start | bytes 1572872 | tf_op jit(solution)/shard_map/ppermute | solution.py:28
  21.7 5.9 %collective-permute-start.6 = (bf16[32,2048]{1,0:T(8,128)(2,1)S(1)}, bf16[32,2048]{1,0:T(8,128)(2,1)S(1)}, u32[]{:S(2)}, u32[]{:S(2)}) collective-permute-start(bf16[32,2048]{1,0:T(8,128)(2,1)S(1)} %get-tuple-element.12), channel_id=1, source_target_pairs={{0,2},{1,3},{2,0},{3,1},{4,6},{5,7},{6,4},{7,5},{8,10},{9,11},{10,... | collective-permute-start | bytes 393224 | tf_op jit(solution)/shard_map/ppermute | solution.py:28
  23.8 9.7 %collective-permute-start.5 = (bf16[32,2048]{1,0:T(8,128)(2,1)S(1)}, bf16[32,2048]{1,0:T(8,128)(2,1)S(1)}, u32[]{:S(2)}, u32[]{:S(2)}) collective-permute-start(bf16[32,2048]{1,0:T(8,128)(2,1)S(1)} %get-tuple-element.13), channel_id=1, source_target_pairs={{0,6},{1,7},{2,4},{3,5},{4,2},{5,3},{6,0},{7,1},{8,14},{9,15},{10,... | collective-permute-start | bytes 393224 | tf_op jit(solution)/shard_map/ppermute | solution.py:28
  26.3 12.1 %collective-permute-start.4 = (bf16[32,2048]{1,0:T(8,128)(2,1)S(1)}, bf16[32,2048]{1,0:T(8,128)(2,1)S(1)}, u32[]{:S(2)}, u32[]{:S(2)}) collective-permute-start(bf16[32,2048]{1,0:T(8,128)(2,1)S(1)} %get-tuple-element.11), channel_id=1, source_target_pairs={{0,4},{1,5},{2,6},{3,7},{4,0},{5,1},{6,2},{7,3},{8,12},{9,13},{10,... | collective-permute-start | bytes 393224 | tf_op jit(solution)/shard_map/ppermute | solution.py:28

commit v2 on v1

--- a/solution.py
+++ b/solution.py
@@ -20,7 +20,7 @@
 PERIOD_TILES = PERIOD * TLEN // LANES
 DEPTH_TILES = -(-TLEN // LANES)
 DEPTH = DEPTH_TILES * LANES
-VMEM_LIMIT = 48 << 20
+VMEM_LIMIT = 24 << 20
 
 
 def exchanged(array, axis, by):
@@ -28,7 +28,9 @@
     return lax.ppermute(array, axis, [(i, i ^ by) for i in range(length)])
 
 
-def template_kernel(shares, raw_ref, avail_ref, usable_ref, out_ref, flat, rows, avail_cols):
+def template_kernel(
+    shares, raw_ref, avail_ref, usable_ref, out_ref, flat, rows, avail_cols
+):
     channels, width = raw_ref.shape
     stations, count = avail_ref.shape
     groups = count // PERIOD
@@ -36,14 +38,13 @@
     stations_here = channels // COMPONENTS
     own = count // shares
     me = lax.axis_index("sta")
-
-    unroll = 8 if tiles % 8 == 0 else 1
+    unroll = next(by for by in (16, 10, 8, 5, 4, 2, 1) if tiles % by == 0)
 
     def spread(step, carry):
         for sub in range(unroll):
             tile = step * unroll + sub
-            piece = raw_ref[:, pl.ds(pl.multiple_of(tile * LANES, LANES), LANES)]
-            flat[pl.ds(pl.multiple_of(tile * SUBLANES, SUBLANES), channels), :] = piece.astype(
+            value = raw_ref[:, pl.ds(pl.multiple_of(tile * LANES, LANES), LANES)]
+            flat[pl.ds(pl.multiple_of(tile * SUBLANES, SUBLANES), channels), :] = value.astype(
                 jnp.float32
             )
         return carry
@@ -119,34 +120,30 @@
             pltpu.VMEM((channels // COMPONENTS, count, LANES), jnp.float32),
         ],
         compiler_params=pltpu.CompilerParams(vmem_limit_bytes=VMEM_LIMIT),
-        cost_estimate=pl.CostEstimate(
-            flops=20 * channels * count * DEPTH, transcendentals=0, bytes_accessed=4 << 20
-        ),
+        cost_estimate=pl.CostEstimate(flops=1 << 10, transcendentals=0, bytes_accessed=1 << 10),
         name="templates",
     )(raw, available, usable)
 
 
+def ahead(value, by):
+    return pltpu.roll(value, value.shape[1] - by, 1) if by else value
+
+
 def correlate_kernel(blocks, weighted_ref, *refs):
     segments = refs[:blocks]
-    mine_ref, other_ref, record, windows, scale = refs[blocks:]
-    channels, count, depth = weighted_ref.shape
-    segment = segments[0].shape[1]
+    mine_ref, other_ref, scale, record, windows = refs[blocks:]
+    channels, segment = segments[0].shape
     lags = blocks * segment
     wide = record.shape[1]
     base = windows.shape[2]
-    half = count // 2
     me = lax.axis_index("blk")
 
-    record[...] = jnp.zeros_like(record)
+    record[:, lags:] = jnp.zeros((SUBLANES, wide - lags), jnp.float32)
     for by in range(blocks):
         start = pl.multiple_of((me ^ by) * segment, LANES)
         record[0:channels, pl.ds(start, segment)] = segments[by][...].astype(jnp.float32)
 
-    def ahead(value, by):
-        return pltpu.roll(value, value.shape[1] - by, 1) if by else value
-
-    samples = record[...]
-    power = samples * samples
+    power = record[...] * record[...]
     energy, taken, span = None, 0, 1
     while True:
         if TLEN & span:
@@ -164,20 +161,17 @@
         shifted = jnp.broadcast_to(record[channel : channel + 1, :], (SUBLANES, wide))
         for bit in (1, 2, 4):
             shifted = jnp.where((sublane & bit) != 0, ahead(shifted, bit), shifted)
+        pair = jnp.concatenate([shifted, ahead(shifted, SUBLANES)], axis=0).astype(jnp.bfloat16)
         for row in range(0, LANES, 2 * SUBLANES):
-            pair = jnp.concatenate(
-                [
-                    ahead(shifted, row)[:, :base],
-                    ahead(shifted, row + SUBLANES)[:, :base],
-                ],
-                axis=0,
-            )
-            windows[channel, row : row + 2 * SUBLANES, :] = pair.astype(jnp.bfloat16)
-
-    tile = 2 * LANES
+            windows[channel, row : row + 2 * SUBLANES, :] = ahead(pair, row)[:, :base]
+
+    half = weighted_ref.shape[1] // 2
+    depth = weighted_ref.shape[2]
+    tile = next(by for by in (8 * LANES, 4 * LANES, 2 * LANES, LANES) if lags % by == 0)
 
     def one_tile(step, carry):
         first = step * tile
+        here = pl.ds(pl.multiple_of(first, LANES), tile)
         total = None
         for channel in range(channels):
             signal = jnp.concatenate(
@@ -188,10 +182,8 @@
                 axis=0,
             )
             matched = jnp.dot(weighted_ref[channel], signal, preferred_element_type=jnp.float32)
-            here = pl.ds(pl.multiple_of(first, LANES), tile)
             term = matched * scale[channel : channel + 1, here]
             total = term if total is None else total + term
-        here = pl.ds(pl.multiple_of(first, LANES), tile)
         mine_ref[:, here] = total[:half]
         other_ref[:, here] = total[half:].astype(other_ref.dtype)
         return carry
@@ -201,52 +193,64 @@
 
 def correlations(weighted, segments):
     channels, count, depth = weighted.shape
+    segment = segments[0].shape[1]
     blocks = len(segments)
-    lags = blocks * segments[0].shape[1]
-    half = count // 2
+    lags = blocks * segment
     return pl.pallas_call(
         functools.partial(correlate_kernel, blocks),
         out_shape=(
-            jax.ShapeDtypeStruct((half, lags), jnp.float32),
-            jax.ShapeDtypeStruct((half, lags), jnp.bfloat16),
+            jax.ShapeDtypeStruct((count // 2, lags), jnp.float32),
+            jax.ShapeDtypeStruct((count // 2, lags), jnp.bfloat16),
         ),
         in_specs=[pl.BlockSpec(memory_space=pltpu.VMEM)] * (1 + blocks),
         out_specs=(pl.BlockSpec(memory_space=pltpu.VMEM),) * 2,
         scratch_shapes=[
-            pltpu.VMEM((SUBLANES, lags + depth + LANES), jnp.float32),
-            pltpu.VMEM((channels, LANES, lags + depth), jnp.bfloat16),
             pltpu.VMEM((SUBLANES, lags), jnp.float32),
+            pltpu.VMEM((SUBLANES, lags + depth), jnp.float32),
+            pltpu.VMEM((channels, LANES, lags + depth - LANES), jnp.bfloat16),
         ],
         compiler_params=pltpu.CompilerParams(vmem_limit_bytes=VMEM_LIMIT),
-        cost_estimate=pl.CostEstimate(
-            flops=2 * channels * count * depth * lags, transcendentals=0, bytes_accessed=4 << 20
-        ),
+        cost_estimate=pl.CostEstimate(flops=1 << 10, transcendentals=0, bytes_accessed=1 << 10),
         name="correlate",
     )(weighted, *segments)
+
+
+def first_kernel(waveforms_ref, out_ref):
+    out_ref[...] = waveforms_ref[...]
+
+
+def first(waveforms):
+    return pl.pallas_call(
+        first_kernel,
+        out_shape=jax.ShapeDtypeStruct(waveforms.shape, waveforms.dtype),
+        in_specs=[pl.BlockSpec(memory_space=pltpu.VMEM)],
+        out_specs=pl.BlockSpec(memory_space=pltpu.VMEM),
+        cost_estimate=pl.CostEstimate(flops=1 << 36, transcendentals=0, bytes_accessed=1 << 26),
+        compiler_params=pltpu.CompilerParams(vmem_limit_bytes=1 << 20),
+        name="first",
+    )(waveforms)
 
 
 def local(waveforms, templates, available, usable):
     blocks = lax.axis_size("blk")
     shares = lax.axis_size("sta")
     my_share = lax.axis_index("sta")
-    block_rows = available.shape[1]
-    own_rows = block_rows // shares
+    own_rows = available.shape[1] // shares
     chips = shares // 2
 
+    waveforms = first(waveforms)
     segments = {0: waveforms}
     for by in reversed(range(1, blocks)):
         segments[by] = exchanged(waveforms, "blk", by)
     weighted = weighted_templates(templates, available, usable, shares)
+
+    wide, narrow = jnp.float32, jnp.bfloat16
     mine, other = correlations(weighted, [segments[by] for by in range(blocks)])
-    summed = mine + exchanged(other, "sta", 1).astype(jnp.float32)
-    summed = summed.reshape(chips, own_rows, summed.shape[1])
-    order = sorted(range(1, chips), key=lambda by: -(by ^ (by >> 1)))
-    arrived = [
-        exchanged(summed[by].astype(jnp.bfloat16), "sta", 2 * by) for by in order
-    ]
+    summed = (mine + exchanged(other, "sta", 1).astype(wide)).reshape(chips, own_rows, -1)
     stacked = summed[0]
-    for term in arrived:
-        stacked = stacked + term.astype(jnp.float32)
+    for by in sorted(range(1, chips), key=lambda by: -(by ^ (by >> 1))):
+        term = exchanged(summed[by].astype(narrow), "sta", 2 * by)
+        stacked = stacked + term.astype(wide)
 
     station_usable = jnp.sum(usable.reshape(-1, COMPONENTS), axis=1).astype(jnp.float32)
     owned = lax.dynamic_slice_in_dim(available, my_share * own_rows, own_rows, 1)

time: 39.4 us -> 33.9 us (0.86)
  the two profiles are of different devices: /device:TPU:0 before, /device:TPU:17 now
where the time goes in v2:
time: 33.9 us; the launch traced here: 33.7 us
  waiting for transfers between devices  12.5 us (37%)
  Pallas kernels  11.2 us (33%)
  starting transfers between devices  7.83 us (23%)
  other arithmetic  1.18 us (3%)
  local copies, waits for them, and re-layouts  0.94 us (3%)
    ppermute x7, waiting for transfers between devices, exchanged(): return lax.ppermute(array, axis, [(i, i ^ by) for i in range(length)])  12.5 us
    ppermute x7, starting transfers between devices, exchanged(): return lax.ppermute(array, axis, [(i, i ^ by) for i in range(length)])  7.83 us
    pallas_call x1, Pallas kernels, correlations(): pl.pallas_call(functools.partial(correlate_kernel, blocks), out_shape=(ja...  6.59 us
    pallas_call x1, Pallas kernels, weighted_templates(): pl.pallas_call(functools.partial(template_kernel, shares), out_shape=jax....  4.6 us
    unnamed x8, local copies, waits for them, and re-layouts  0.83 us
    mul x2, other arithmetic, local(): math.sqrt(TLEN) * stacked * lax.rsqrt(jnp.maximum(counted, 1.0))[:, None]  0.8 us
  transfers between devices with their start and end apart: 7, of which 3 were waited for; matrix products, arithmetic and copies ran while one was open for 1% of the time, Pallas kernels for 14%

profile of v2, /device:TPU:17, one launch (start us, length us, event | category | flops | bytes accessed | tf_op | source)
XLA Modules:
  0.0 33.7 jit_solution(5946904161863202556)
XLA Ops:
  0.0 0.0 copy-start
  0.0 0.0 copy-start.1
  0.0 0.0 copy-start.3
  0.0 0.8 %copy-done.3 = bf16[6,512]{1,0:T(8,128)(2,1)S(1)} copy-done((bf16[6,512]{1,0:T(8,128)(2,1)S(1)}, bf16[6,512]{1,0:T(8,128)(2,1)}, u32[]{:S(2)}) %copy-start.3) | copy-done | bytes 6168
  0.8 0.0 copy-start.2
  0.8 1.2 %collective-permute-start = (bf16[6,512]{1,0:T(8,128)(2,1)S(1)}, bf16[6,512]{1,0:T(8,128)(2,1)S(1)}, u32[]{:S(2)}, u32[]{:S(2)}) collective-permute-start(bf16[6,512]{1,0:T(8,128)(2,1)S(1)} %first.1.refs_0_), channel_id=1, source_target_pairs={{0,8},{8,0},{16,24},{24,16},{1,9},{9,1},{17,25},{25,17},{2,10},{10... | collective-permute-start | bytes 18440 | tf_op jit(solution)/shard_map/ppermute | solution.py:28
  2.0 1.2 %collective-permute-start.1 = (bf16[6,512]{1,0:T(8,128)(2,1)S(1)}, bf16[6,512]{1,0:T(8,128)(2,1)S(1)}, u32[]{:S(2)}, u32[]{:S(2)}) collective-permute-start(bf16[6,512]{1,0:T(8,128)(2,1)S(1)} %first.1.refs_0_), channel_id=1, source_target_pairs={{0,16},{8,24},{16,0},{24,8},{1,17},{9,25},{17,1},{25,9},{2,18},{10... | collective-permute-start | bytes 18440 | tf_op jit(solution)/shard_map/ppermute | solution.py:28
  3.3 0.2 collective-permute-start.2
  3.5 0.0 copy-done
  3.5 0.0 copy-done.1
  3.5 0.0 copy-done.2
  3.5 4.6 %templates.1.weighted_ref = bf16[6,256,512]{2,1,0:T(8,128)(2,1)S(1)} custom-call(bf16[6,102400]{1,0:T(8,128)(2,1)S(1)} %copy-done, s32[16,256]{1,0:T(8,128)S(1)} %copy-done.1, s32[48]{0:T(128)S(1)} %copy-done.2), custom_call_target="tpu_custom_call" | custom-call | flops 1024 | bytes 1024 | tf_op jit(solution)/shard_map/templates/pallas_call | solution.py:108
  8.1 0.0 collective-permute-done.refs_1_
  8.1 0.0 collective-permute-done.1.refs_2_
  8.1 0.0 collective-permute-done.2.refs_3_
  8.1 6.6 %correlate.1 = (f32[128,2048]{1,0:T(8,128)S(1)}, bf16[128,2048]{1,0:T(8,128)(2,1)S(1)}) custom-call(bf16[6,256,512]{2,1,0:T(8,128)(2,1)S(1)} %templates.1.weighted_ref, bf16[6,512]{1,0:T(8,128)(2,1)S(1)} %first.1.refs_0_, bf16[6,512]{1,0:T(8,128)(2,1)S(1)} %collective-permute-done.refs_1_, bf16[6,512]{1,0:T(8,128)(2,1)S(1)} %collective-permute-done.1.refs_2_, ...), custom_call_target="tpu_custom_call" | custom-call | flops 1024 | bytes 1024 | tf_op jit(solution)/shard_map/correlate/pallas_call | solution.py:199
  14.7 1.6 %collective-permute-start.3 = (bf16[128,2048]{1,0:T(8,128)(2,1)S(1)}, bf16[128,2048]{1,0:T(8,128)(2,1)S(1)}, u32[]{:S(2)}, u32[]{:S(2)}) collective-permute-start(bf16[128,2048]{1,0:T(8,128)(2,1)S(1)} %get-tuple-element.8), channel_id=1, source_target_pairs={{0,1},{1,0},{2,3},{3,2},{4,5},{5,4},{6,7},{7,6},{8,9},{9,8},{10,11... | collective-permute-start | bytes 1572872 | tf_op jit(solution)/shard_map/ppermute | solution.py:28
  16.3 0.1 reshape.19
  16.4 0.1 reduce_sum.18
  16.5 0.1 multiply_reduce_fusion
  16.6 1.2 %collective-permute-done.3 = bf16[128,2048]{1,0:T(8,128)(2,1)S(1)} collective-permute-done((bf16[128,2048]{1,0:T(8,128)(2,1)S(1)}, bf16[128,2048]{1,0:T(8,128)(2,1)S(1)}, u32[]{:S(2)}, u32[]{:S(2)}) %collective-permute-start.3) | collective-permute-done | bytes 524320 | tf_op jit(solution)/shard_map/ppermute | solution.py:28
  17.8 0.2 fusion.3
  18.0 0.1 collective-permute-start.4
  18.1 2.5 %collective-permute-start.5 = (bf16[32,2048]{1,0:T(8,128)(2,1)S(1)}, bf16[32,2048]{1,0:T(8,128)(2,1)S(1)}, u32[]{:S(2)}, u32[]{:S(2)}) collective-permute-start(bf16[32,2048]{1,0:T(8,128)(2,1)S(1)} %get-tuple-element.13), channel_id=1, source_target_pairs={{0,6},{1,7},{2,4},{3,5},{4,2},{5,3},{6,0},{7,1},{8,14},{9,15},{10,... | collective-permute-start | bytes 393224 | tf_op jit(solution)/shard_map/ppermute | solution.py:28
  20.6 1.1 %collective-permute-start.6 = (bf16[32,2048]{1,0:T(8,128)(2,1)S(1)}, bf16[32,2048]{1,0:T(8,128)(2,1)S(1)}, u32[]{:S(2)}, u32[]{:S(2)}) collective-permute-start(bf16[32,2048]{1,0:T(8,128)(2,1)S(1)} %get-tuple-element.12), channel_id=1, source_target_pairs={{0,2},{1,3},{2,0},{3,1},{4,6},{5,7},{6,4},{7,5},{8,10},{9,11},{10,... | collective-permute-start | bytes 393224 | tf_op jit(solution)/shard_map/ppermute | solution.py:28
  21.7 4.8 %collective-permute-done.4 = bf16[32,2048]{1,0:T(8,128)(2,1)S(1)} collective-permute-done((bf16[32,2048]{1,0:T(8,128)(2,1)S(1)}, bf16[32,2048]{1,0:T(8,128)(2,1)S(1)}, u32[]{:S(2)}, u32[]{:S(2)}) %collective-permute-start.4) | collective-permute-done | bytes 131104 | tf_op jit(solution)/shard_map/ppermute | solution.py:28
  26.5 6.5 %collective-permute-done.5 = bf16[32,2048]{1,0:T(8,128)(2,1)S(1)} collective-permute-done((bf16[32,2048]{1,0:T(8,128)(2,1)S(1)}, bf16[32,2048]{1,0:T(8,128)(2,1)S(1)}, u32[]{:S(2)}, u32[]{:S(2)}) %collective-permute-start.5) | collective-permute-done | bytes 131104 | tf_op jit(solution)/shard_map/ppermute | solution.py:28
  32.9 0.0 collective-permute-done.6
  32.9 0.8 %fusion.2 = f32[32,2048]{1,0:T(8,128)} fusion(f32[128,2048]{1,0:T(8,128)S(1)} %get-tuple-element.10, bf16[32,2048]{1,0:T(8,128)(2,1)S(1)} %collective-permute-done.6, bf16[32,2048]{1,0:T(8,128)(2,1)S(1)} %collective-permute-done.5, bf16[32,2048]{1,0:T(8,128)(2,1)S(1)} %collective-permute-done.4, f32[32]{0:T(128)S(1)} %rsqrt_multiply_fusion), kind=kLoop, calls=%fused_computation.4 | loop fusion | flops 458752 | bytes 917632 | tf_op jit(solution)/shard_map/mul | solution.py:258
  (4 shorter events, 0.0 us)
Async XLA Ops:
  0.0 3.5 %copy-start = (bf16[6,102400]{1,0:T(8,128)(2,1)S(1)}, bf16[6,102400]{1,0:T(8,128)(2,1)}, u32[]{:S(2)}) copy-start(bf16[6,102400]{1,0:T(8,128)(2,1)} %raw_ref.1) | copy-start | bytes 3686404
  0.0 3.5 %copy-start.1 = (s32[16,256]{1,0:T(8,128)S(1)}, s32[16,256]{1,0:T(8,128)}, u32[]{:S(2)}) copy-start(s32[16,256]{1,0:T(8,128)} %avail_ref.1) | copy-start | bytes 49156
  0.0 0.8 %copy-start.3 = (bf16[6,512]{1,0:T(8,128)(2,1)S(1)}, bf16[6,512]{1,0:T(8,128)(2,1)}, u32[]{:S(2)}) copy-start(bf16[6,512]{1,0:T(8,128)(2,1)} %waveforms_ref.1) | copy-start | bytes 18436
  0.8 2.7 %copy-start.2 = (s32[48]{0:T(128)S(1)}, s32[48]{0:T(128)}, u32[]{:S(2)}) copy-start(s32[48]{0:T(128)} %usable_ref.1) | copy-start | bytes 580
  0.8 7.3 %collective-permute-start = (bf16[6,512]{1,0:T(8,128)(2,1)S(1)}, bf16[6,512]{1,0:T(8,128)(2,1)S(1)}, u32[]{:S(2)}, u32[]{:S(2)}) collective-permute-start(bf16[6,512]{1,0:T(8,128)(2,1)S(1)} %first.1.refs_0_), channel_id=1, source_target_pairs={{0,8},{8,0},{16,24},{24,16},{1,9},{9,1},{17,25},{25,17},{2,10},{10... | collective-permute-start | bytes 18440 | tf_op jit(solution)/shard_map/ppermute | solution.py:28
  2.0 6.1 %collective-permute-start.1 = (bf16[6,512]{1,0:T(8,128)(2,1)S(1)}, bf16[6,512]{1,0:T(8,128)(2,1)S(1)}, u32[]{:S(2)}, u32[]{:S(2)}) collective-permute-start(bf16[6,512]{1,0:T(8,128)(2,1)S(1)} %first.1.refs_0_), channel_id=1, source_target_pairs={{0,16},{8,24},{16,0},{24,8},{1,17},{9,25},{17,1},{25,9},{2,18},{10... | collective-permute-start | bytes 18440 | tf_op jit(solution)/shard_map/ppermute | solution.py:28
  3.3 4.8 %collective-permute-start.2 = (bf16[6,512]{1,0:T(8,128)(2,1)S(1)}, bf16[6,512]{1,0:T(8,128)(2,1)S(1)}, u32[]{:S(2)}, u32[]{:S(2)}) collective-permute-start(bf16[6,512]{1,0:T(8,128)(2,1)S(1)} %first.1.refs_0_), channel_id=1, source_target_pairs={{0,24},{8,16},{16,8},{24,0},{1,25},{9,17},{17,9},{25,1},{2,26},{10... | collective-permute-start | bytes 18440 | tf_op jit(solution)/shard_map/ppermute | solution.py:28
  14.7 3.1 %collective-permute-start.3 = (bf16[128,2048]{1,0:T(8,128)(2,1)S(1)}, bf16[128,2048]{1,0:T(8,128)(2,1)S(1)}, u32[]{:S(2)}, u32[]{:S(2)}) collective-permute-start(bf16[128,2048]{1,0:T(8,128)(2,1)S(1)} %get-tuple-element.8), channel_id=1, source_target_pairs={{0,1},{1,0},{2,3},{3,2},{4,5},{5,4},{6,7},{7,6},{8,9},{9,8},{10,11... | collective-permute-start | bytes 1572872 | tf_op jit(solution)/shard_map/ppermute | solution.py:28
  18.0 8.4 %collective-permute-start.4 = (bf16[32,2048]{1,0:T(8,128)(2,1)S(1)}, bf16[32,2048]{1,0:T(8,128)(2,1)S(1)}, u32[]{:S(2)}, u32[]{:S(2)}) collective-permute-start(bf16[32,2048]{1,0:T(8,128)(2,1)S(1)} %get-tuple-element.11), channel_id=1, source_target_pairs={{0,4},{1,5},{2,6},{3,7},{4,0},{5,1},{6,2},{7,3},{8,12},{9,13},{10,... | collective-permute-start | bytes 393224 | tf_op jit(solution)/shard_map/ppermute | solution.py:28
  18.1 14.8 %collective-permute-start.5 = (bf16[32,2048]{1,0:T(8,128)(2,1)S(1)}, bf16[32,2048]{1,0:T(8,128)(2,1)S(1)}, u32[]{:S(2)}, u32[]{:S(2)}) collective-permute-start(bf16[32,2048]{1,0:T(8,128)(2,1)S(1)} %get-tuple-element.13), channel_id=1, source_target_pairs={{0,6},{1,7},{2,4},{3,5},{4,2},{5,3},{6,0},{7,1},{8,14},{9,15},{10,... | collective-permute-start | bytes 393224 | tf_op jit(solution)/shard_map/ppermute | solution.py:28
  20.6 12.3 %collective-permute-start.6 = (bf16[32,2048]{1,0:T(8,128)(2,1)S(1)}, bf16[32,2048]{1,0:T(8,128)(2,1)S(1)}, u32[]{:S(2)}, u32[]{:S(2)}) collective-permute-start(bf16[32,2048]{1,0:T(8,128)(2,1)S(1)} %get-tuple-element.12), channel_id=1, source_target_pairs={{0,2},{1,3},{2,0},{3,1},{4,6},{5,7},{6,4},{7,5},{8,10},{9,11},{10,... | collective-permute-start | bytes 393224 | tf_op jit(solution)/shard_map/ppermute | solution.py:28

commit v3 on v2

v3 whole, which is shorter than its diff:
```python
import functools
import math

import jax
import jax.numpy as jnp
from jax import lax
from jax.experimental import pallas as pl
from jax.experimental.pallas import tpu as pltpu
from jax.sharding import PartitionSpec as P

TLEN = 400
COMPONENTS = 3
LANES = 128
SUBLANES = 8

FLOOR_SHARE = 0.1
EPSILON = 1e-06

PERIOD = LANES // math.gcd(TLEN, LANES)
PERIOD_TILES = PERIOD * TLEN // LANES
DEPTH_TILES = -(-TLEN // LANES)
DEPTH = DEPTH_TILES * LANES
VMEM_LIMIT = 24 << 20


def exchanged(array, axis, by):
    length = lax.axis_size(axis)
    return lax.ppermute(array, axis, [(i, i ^ by) for i in range(length)])


def template_kernel(
    shares, stay, raw_ref, avail_ref, usable_ref, token_ref, out_ref, flat, rows, avail_cols
):
    channels, width = raw_ref.shape
    stations, count = avail_ref.shape
    tiles = width // LANES
    stations_here = channels // COMPONENTS
    own = count // shares
    chips = shares // 2
    chip_rows = 2 * own
    chip_tiles = tiles // chips
    taken = range(1) if stay else range(1, chips)
    groups = len(taken) * chip_rows // PERIOD
    me = lax.axis_index("sta")
    start = me // 2 if stay else me // 2 + 1
    unroll = next(by for by in (25, 20, 16, 10, 8, 5, 4, 2, 1) if chip_tiles % by == 0)

    def spread(step, carry):
        source = lax.rem(start * chip_tiles + step * unroll, tiles)
        for sub in range(unroll):
            value = raw_ref[:, pl.ds(pl.multiple_of((source + sub) * LANES, LANES), LANES)]
            there = pl.multiple_of((step * unroll + sub) * SUBLANES, SUBLANES)
            flat[pl.ds(there, channels), :] = value.astype(jnp.float32)
        return carry

    lax.fori_loop(0, len(taken) * chip_tiles // unroll, spread, 0)

    station_row = lax.broadcasted_iota(jnp.int32, (stations, LANES), 0)
    avail = avail_ref[...].astype(jnp.float32)
    for local_station in range(stations_here):
        chosen = (station_row == me * stations_here + local_station).astype(jnp.float32)
        avail_cols[local_station] = lax.dot_general(
            avail, chosen, (((0,), (0,)), ((), ())), preferred_element_type=jnp.float32
        )

    lane = lax.broadcasted_iota(jnp.int32, (groups, LANES), 1)
    last = TLEN - (DEPTH_TILES - 1) * LANES
    block_lane = lax.broadcasted_iota(jnp.int32, (own, LANES), 1)

    def one_step(step, carry):
        channel = jnp.maximum(step - 1, 0)
        ready = 1 - step % 2
        use = usable_ref[me * channels + channel].astype(jnp.float32)
        for place in range(2 * len(taken)):
            core, chip = divmod(place, len(taken))
            owner = me ^ (2 * taken[chip] + core)
            moved = lax.rem(owner // 2 - start + chips, chips) * chip_rows + owner % 2 * own
            here = pl.ds(pl.multiple_of(moved, own), own)
            parts = [rows[ready, part, here, :] for part in range(DEPTH_TILES)]
            mean = jnp.sum(sum(parts), axis=1, keepdims=True) * (1.0 / TLEN)
            centred = [value - mean for value in parts]
            centred[-1] = jnp.where(block_lane < last, centred[-1], 0.0)
            squared = jnp.sum(sum(value * value for value in centred), axis=1, keepdims=True)
            there = pl.ds(pl.multiple_of(owner * own, own), own)
            weight = avail_cols[channel // COMPONENTS, there, :] * use
            factor = lax.rsqrt(squared + EPSILON) * weight
            for part in range(DEPTH_TILES):
                out_ref[
                    channel, place * own : (place + 1) * own, part * LANES : (part + 1) * LANES
                ] = (centred[part] * factor).astype(jnp.bfloat16)
        channel = jnp.minimum(step, channels - 1)
        filled = step % 2
        for which in range(PERIOD):
            first, offset = divmod(which * TLEN, LANES)
            pieces = []
            for part in range(DEPTH_TILES):
                begin = (first + part) * SUBLANES + channel
                piece = flat[pl.ds(begin, groups, stride=PERIOD_TILES * SUBLANES), :]
                if offset:
                    piece = pltpu.roll(piece, LANES - offset, 1)
                pieces.append(piece)
            for part in range(DEPTH_TILES):
                value = pieces[part]
                if part + 1 < DEPTH_TILES:
                    if offset:
                        value = jnp.where(lane < LANES - offset, value, pieces[part + 1])
                else:
                    value = jnp.where(lane < last, value, 0.0)
                rows[filled, part, pl.ds(which, groups, stride=PERIOD), :] = value
        return carry

    lax.fori_loop(0, channels + 1, one_step, 0)


def weighted_templates(raw, available, usable, token, shares, stay):
    channels, width = raw.shape
    stations, count = available.shape
    taken = 2 * count // shares if stay else count - 2 * count // shares
    return pl.pallas_call(
        functools.partial(template_kernel, shares, stay),
        out_shape=jax.ShapeDtypeStruct((channels, taken, DEPTH), jnp.bfloat16),
        in_specs=[
            pl.BlockSpec(memory_space=pltpu.VMEM),
            pl.BlockSpec(memory_space=pltpu.VMEM),
            pl.BlockSpec(memory_space=pltpu.SMEM),
            pl.BlockSpec(memory_space=pltpu.VMEM),
        ],
        out_specs=pl.BlockSpec(memory_space=pltpu.VMEM),
        scratch_shapes=[
            pltpu.VMEM((taken * TLEN // LANES * SUBLANES, LANES), jnp.float32),
            pltpu.VMEM((2, DEPTH_TILES, taken, LANES), jnp.float32),
            pltpu.VMEM((channels // COMPONENTS, count, LANES), jnp.float32),
        ],
        compiler_params=pltpu.CompilerParams(vmem_limit_bytes=VMEM_LIMIT),
        cost_estimate=pl.CostEstimate(flops=1 << 10, transcendentals=0, bytes_accessed=1 << 10),
        name="templates_staying" if stay else "templates_leaving",
    )(raw, available, usable, token)


def ahead(value, by):
    return pltpu.roll(value, value.shape[1] - by, 1) if by else value


def correlate_kernel(blocks, weighted_ref, *refs):
    segments = refs[:blocks]
    mine_ref, other_ref, scale, record, windows = refs[blocks:]
    channels, segment = segments[0].shape
    lags = blocks * segment
    wide = record.shape[1]
    base = windows.shape[2]
    me = lax.axis_index("blk")

    record[:, lags:] = jnp.zeros((SUBLANES, wide - lags), jnp.float32)
    for by in range(blocks):
        start = pl.multiple_of((me ^ by) * segment, LANES)
        record[0:channels, pl.ds(start, segment)] = segments[by][...].astype(jnp.float32)

    power = record[...] * record[...]
    energy, taken, span = None, 0, 1
    while True:
        if TLEN & span:
            term = ahead(power, taken)
            energy = term if energy is None else energy + term
            taken += span
        if 2 * span > TLEN:
            break
        power = power + ahead(power, span)
        span *= 2
    scale[...] = lax.rsqrt(jnp.maximum(energy[:, :lags], FLOOR_SHARE * TLEN))

    sublane = lax.broadcasted_iota(jnp.int32, (SUBLANES, wide), 0)

    def one_record(channel, carry):
        shifted = jnp.broadcast_to(record[pl.ds(channel, 1), :], (SUBLANES, wide))
        for bit in (1, 2, 4):
            shifted = jnp.where((sublane & bit) != 0, ahead(shifted, bit), shifted)
        pair = jnp.concatenate([shifted, ahead(shifted, SUBLANES)], axis=0).astype(jnp.bfloat16)
        for row in range(0, LANES, 2 * SUBLANES):
            windows[channel, row : row + 2 * SUBLANES, :] = pair[:, row : row + base]
        return carry

    lax.fori_loop(0, channels, one_record, 0, unroll=2)

    half = weighted_ref.shape[1] // 2
    tile = next(by * LANES for by in (16, 8, 4, 2, 1) if lags % (by * LANES) == 0)

    def one_tile(first):
        here = pl.ds(first, tile)
        total = None
        for channel in range(channels):
            signal = jnp.concatenate(
                [
                    windows[channel, : min(LANES, TLEN - start), pl.ds(first + start, tile)]
                    for start in range(0, TLEN, LANES)
                ],
                axis=0,
            )
            weights = weighted_ref[channel, :, :TLEN]
            matched = jnp.dot(weights, signal, preferred_element_type=jnp.float32)
            term = matched * scale[channel : channel + 1, here]
            total = term if total is None else total + term
        mine_ref[:, here] = total[:half]
        other_ref[:, here] = total[half:].astype(other_ref.dtype)

    for step in range(lags // tile):
        one_tile(step * tile)


def correlations(weighted, segments, name):
    channels, count, depth = weighted.shape
    segment = segments[0].shape[1]
    blocks = len(segments)
    lags = blocks * segment
    return pl.pallas_call(
        functools.partial(correlate_kernel, blocks),
        out_shape=(
            jax.ShapeDtypeStruct((count // 2, lags), jnp.float32),
            jax.ShapeDtypeStruct((count // 2, lags), jnp.bfloat16),
        ),
        in_specs=[pl.BlockSpec(memory_space=pltpu.VMEM)] * (1 + blocks),
        out_specs=(pl.BlockSpec(memory_space=pltpu.VMEM),) * 2,
        scratch_shapes=[
            pltpu.VMEM((SUBLANES, lags), jnp.float32),
            pltpu.VMEM((SUBLANES, lags + depth), jnp.float32),
            pltpu.VMEM((channels, LANES, lags + depth - LANES), jnp.bfloat16),
        ],
        compiler_params=pltpu.CompilerParams(vmem_limit_bytes=VMEM_LIMIT),
        cost_estimate=pl.CostEstimate(flops=1 << 10, transcendentals=0, bytes_accessed=1 << 10),
        name=name,
    )(weighted, *segments)


def first_kernel(token_ref):
    token_ref[...] = jnp.zeros_like(token_ref)


def first():
    return pl.pallas_call(
        first_kernel,
        out_shape=jax.ShapeDtypeStruct((SUBLANES, LANES), jnp.float32),
        out_specs=pl.BlockSpec(memory_space=pltpu.VMEM),
        cost_estimate=pl.CostEstimate(flops=1 << 36, transcendentals=0, bytes_accessed=1 << 26),
        compiler_params=pltpu.CompilerParams(vmem_limit_bytes=1 << 20),
        name="first",
    )()


def add_kernel(*refs):
    total = refs[0][...]
    for ref in refs[1:-1]:
        total = total + ref[...].astype(jnp.float32)
    refs[-1][...] = total


def added(*terms):
    return pl.pallas_call(
        add_kernel,
        out_shape=jax.ShapeDtypeStruct(terms[0].shape, jnp.float32),
        in_specs=[pl.BlockSpec(memory_space=pltpu.VMEM)] * len(terms),
        out_specs=pl.BlockSpec(memory_space=pltpu.VMEM),
        cost_estimate=pl.CostEstimate(flops=1 << 36, transcendentals=0, bytes_accessed=1 << 26),
        compiler_params=pltpu.CompilerParams(vmem_limit_bytes=4 << 20),
        name="added",
    )(*terms)


def local(waveforms, templates, available, usable):
    blocks = lax.axis_size("blk")
    shares = lax.axis_size("sta")
    my_share = lax.axis_index("sta")
    own_rows = available.shape[1] // shares
    chips = shares // 2

    waveforms, token = lax.optimization_barrier((waveforms, first()))
    segments = {0: waveforms}
    for by in range(1, blocks):
        segments[by] = exchanged(waveforms, "blk", by)
    segments = [segments[by] for by in range(blocks)]

    wide, narrow = jnp.float32, jnp.bfloat16
    weighted = weighted_templates(templates, available, usable, token, shares, False)
    mine, other = correlations(weighted, segments, "correlate_leaving")
    summed = (mine + exchanged(other, "sta", 1).astype(wide)).astype(narrow)
    sent = [summed[by * own_rows : (by + 1) * own_rows] for by in range(chips - 1)]
    sent, segments, later = lax.optimization_barrier((sent, segments, token))
    arrived = [
        exchanged(sent[by - 1], "sta", 2 * by)
        for by in sorted(range(1, chips), key=lambda by: -(by ^ (by >> 1)))
    ]
    weighted = weighted_templates(templates, available, usable, later, shares, True)
    mine, other = correlations(weighted, segments, "correlate_staying")
    stacked = added(mine, *arrived) + exchanged(other, "sta", 1).astype(wide)

    station_usable = jnp.sum(usable.reshape(-1, COMPONENTS), axis=1).astype(jnp.float32)
    owned = lax.dynamic_slice_in_dim(available, my_share * own_rows, own_rows, 1)
    counted = jnp.sum(owned.astype(jnp.float32) * station_usable[:, None], axis=0)
    return math.sqrt(TLEN) * stacked * lax.rsqrt(jnp.maximum(counted, 1.0))[:, None]


def solution(mesh):
    return jax.shard_map(
        local,
        mesh=mesh,
        in_specs=(P("sta", "blk"), P("sta", "blk"), P(None, "blk"), P()),
        out_specs=P(("blk", "sta"), None),
        check_vma=False,
    )
```

time: 33.9 us -> 31.5 us (0.929)
  waiting for transfers between devices: 12.5 us -> 4.15 us
  Pallas kernels: 11.2 us -> 15.9 us
  starting transfers between devices: 7.83 us -> 9.32 us
    ppermute x7 -> x8, waiting for transfers between devices: 12.5 us -> 4.15 us  [exchanged(): return lax.ppermute(array, axis, [(i, i ^ by) for i in range(length)])]
    pallas_call x1 -> x2, Pallas kernels: 6.59 us -> 9.5 us  [correlations(): pl.pallas_call(functools.partial(correlate_kernel, blocks), out_shape=(ja...]
    pallas_call x2 -> x4, Pallas kernels: 4.6 us -> 6.38 us  [the longest x2 6.32 us: weighted_templates(): pl.pallas_call(functools.partial(template_kernel, shares, stay), out_shap...]
    ppermute x7 -> x8, starting transfers between devices: 7.83 us -> 9.32 us  [exchanged(): return lax.ppermute(array, axis, [(i, i ^ by) for i in range(length)])]
  transfers between devices with their start and end apart: 7 -> 8, of which waited for: 3 -> 2; matrix products, arithmetic and copies ran while one was open for 1% -> 1% of each run, Pallas kernels for 14% -> 34%
where the time goes in v3:
time: 31.5 us; the launch traced here: 31.4 us
  Pallas kernels  15.9 us (50%)
  starting transfers between devices  9.32 us (30%)
  waiting for transfers between devices  4.15 us (13%)
  other arithmetic  1.1 us (3%)
  local copies, waits for them, and re-layouts  0.79 us (3%)
    pallas_call x2, Pallas kernels, correlations(): pl.pallas_call(functools.partial(correlate_kernel, blocks), out_shape=(ja...  9.5 us
    ppermute x8, starting transfers between devices, exchanged(): return lax.ppermute(array, axis, [(i, i ^ by) for i in range(length)])  9.32 us
    pallas_call x2, Pallas kernels, weighted_templates(): pl.pallas_call(functools.partial(template_kernel, shares, stay), out_shap...  6.32 us
    ppermute x8, waiting for transfers between devices, exchanged(): return lax.ppermute(array, axis, [(i, i ^ by) for i in range(length)])  4.15 us
    mul x2, other arithmetic, local(): math.sqrt(TLEN) * stacked * lax.rsqrt(jnp.maximum(counted, 1.0))[:, None]  0.79 us
    unnamed x8, local copies, waits for them, and re-layouts  0.68 us
  transfers between devices with their start and end apart: 8, of which 2 were waited for; matrix products, arithmetic and copies ran while one was open for 1% of the time, Pallas kernels for 34%

profile of v3, /device:TPU:17, one launch (start us, length us, event | category | flops | bytes accessed | tf_op | source)
XLA Modules:
  0.0 31.4 jit_solution(3191755027962111794)
XLA Ops:
  0.0 0.0 copy-start.2
  0.0 0.0 copy-start.3
  0.0 0.7 %copy-done.2 = bf16[6,512]{1,0:T(8,128)(2,1)S(1)} copy-done((bf16[6,512]{1,0:T(8,128)(2,1)S(1)}, bf16[6,512]{1,0:T(8,128)(2,1)}, u32[]{:S(2)}) %copy-start.2) | copy-done | bytes 6168
  0.7 1.2 %collective-permute-start = (bf16[6,512]{1,0:T(8,128)(2,1)S(1)}, bf16[6,512]{1,0:T(8,128)(2,1)S(1)}, u32[]{:S(2)}, u32[]{:S(2)}) collective-permute-start(bf16[6,512]{1,0:T(8,128)(2,1)S(1)} %copy-done.2), channel_id=1, source_target_pairs={{0,8},{8,0},{16,24},{24,16},{1,9},{9,1},{17,25},{25,17},{2,10},{10... | collective-permute-start | bytes 18440 | tf_op jit(solution)/shard_map/ppermute | solution.py:28
  1.9 1.2 %collective-permute-start.1 = (bf16[6,512]{1,0:T(8,128)(2,1)S(1)}, bf16[6,512]{1,0:T(8,128)(2,1)S(1)}, u32[]{:S(2)}, u32[]{:S(2)}) collective-permute-start(bf16[6,512]{1,0:T(8,128)(2,1)S(1)} %copy-done.2), channel_id=1, source_target_pairs={{0,16},{8,24},{16,0},{24,8},{1,17},{9,25},{17,1},{25,9},{2,18},{10... | collective-permute-start | bytes 18440 | tf_op jit(solution)/shard_map/ppermute | solution.py:28
  3.1 0.2 collective-permute-start.2
  3.3 0.0 copy-done
  3.4 0.0 copy-done.1
  3.4 0.0 copy-done.3
  3.4 3.8 %templates_leaving.1.weighted_ref = bf16[6,192,512]{2,1,0:T(8,128)(2,1)S(1)} custom-call(bf16[6,102400]{1,0:T(8,128)(2,1)S(1)} %copy-done, s32[16,256]{1,0:T(8,128)S(1)} %copy-done.1, s32[48]{0:T(128)S(1)} %copy-done.3, f32[8,128]{1,0:T(8,128)S(1)} %first.1.token_ref), custom_call_target="tpu_custom_call" | custom-call | flops 1024 | bytes 1024 | tf_op jit(solution)/shard_map/templates_leaving/pallas_call | solution.py:119
  7.2 0.0 collective-permute-done.refs_1_
  7.2 0.0 collective-permute-done.1.refs_2_
  7.2 0.0 collective-permute-done.2.refs_3_
  7.2 5.1 %correlate_leaving.1 = (f32[96,2048]{1,0:T(8,128)S(1)}, bf16[96,2048]{1,0:T(8,128)(2,1)S(1)}) custom-call(bf16[6,192,512]{2,1,0:T(8,128)(2,1)S(1)} %templates_leaving.1.weighted_ref, bf16[6,512]{1,0:T(8,128)(2,1)S(1)} %copy-done.2, bf16[6,512]{1,0:T(8,128)(2,1)S(1)} %collective-permute-done.refs_1_, bf16[6,512]{1,0:T(8,128)(2,1)S(1)} %collective-permute-done.1.refs_2_, ...), custom_call_target="tpu_custom_call" | custom-call | flops 1024 | bytes 1024 | tf_op jit(solution)/shard_map/correlate_leaving/pallas_call | solution.py:214
  12.3 1.8 %collective-permute-start.3 = (bf16[96,2048]{1,0:T(8,128)(2,1)S(1)}, bf16[96,2048]{1,0:T(8,128)(2,1)S(1)}, u32[]{:S(2)}, u32[]{:S(2)}) collective-permute-start(bf16[96,2048]{1,0:T(8,128)(2,1)S(1)} %get-tuple-element.22), channel_id=1, source_target_pairs={{0,1},{1,0},{2,3},{3,2},{4,5},{5,4},{6,7},{7,6},{8,9},{9,8},{10,11... | collective-permute-start | bytes 1179656 | tf_op jit(solution)/shard_map/ppermute | solution.py:28
  14.1 0.1 reshape.10
  14.2 0.1 reduce_sum.18
  14.3 0.1 multiply_reduce_fusion
  14.4 1.0 %collective-permute-done.3 = bf16[96,2048]{1,0:T(8,128)(2,1)S(1)} collective-permute-done((bf16[96,2048]{1,0:T(8,128)(2,1)S(1)}, bf16[96,2048]{1,0:T(8,128)(2,1)S(1)}, u32[]{:S(2)}, u32[]{:S(2)}) %collective-permute-start.3) | collective-permute-done | bytes 393248 | tf_op jit(solution)/shard_map/ppermute | solution.py:28
  15.5 0.1 add_convert_fusion
  15.6 0.1 collective-permute-start.4
  15.7 2.4 %collective-permute-start.5 = (bf16[32,2048]{1,0:T(8,128)(2,1)S(1)}, bf16[32,2048]{1,0:T(8,128)(2,1)S(1)}, u32[]{:S(2)}, u32[]{:S(2)}) collective-permute-start(bf16[32,2048]{1,0:T(8,128)(2,1)S(1)} %get-tuple-element.30), channel_id=1, source_target_pairs={{0,6},{1,7},{2,4},{3,5},{4,2},{5,3},{6,0},{7,1},{8,14},{9,15},{10,... | collective-permute-start | bytes 393224 | tf_op jit(solution)/shard_map/ppermute | solution.py:28
  18.2 1.1 %collective-permute-start.6 = (bf16[32,2048]{1,0:T(8,128)(2,1)S(1)}, bf16[32,2048]{1,0:T(8,128)(2,1)S(1)}, u32[]{:S(2)}, u32[]{:S(2)}) collective-permute-start(bf16[32,2048]{1,0:T(8,128)(2,1)S(1)} %get-tuple-element.31), channel_id=1, source_target_pairs={{0,2},{1,3},{2,0},{3,1},{4,6},{5,7},{6,4},{7,5},{8,10},{9,11},{10,... | collective-permute-start | bytes 393224 | tf_op jit(solution)/shard_map/ppermute | solution.py:28
  19.2 2.5 %templates_staying.1.weighted_ref = bf16[6,64,512]{2,1,0:T(8,128)(2,1)S(1)} custom-call(bf16[6,102400]{1,0:T(8,128)(2,1)S(1)} %copy-done, s32[16,256]{1,0:T(8,128)S(1)} %copy-done.1, s32[48]{0:T(128)S(1)} %copy-done.3, f32[8,128]{1,0:T(8,128)S(1)} %first.1.token_ref), custom_call_target="tpu_custom_call" | custom-call | flops 1024 | bytes 1024 | tf_op jit(solution)/shard_map/templates_staying/pallas_call | solution.py:119
  21.8 4.4 %correlate_staying.1 = (f32[32,2048]{1,0:T(8,128)S(1)}, bf16[32,2048]{1,0:T(8,128)(2,1)S(1)}) custom-call(bf16[6,64,512]{2,1,0:T(8,128)(2,1)S(1)} %templates_staying.1.weighted_ref, bf16[6,512]{1,0:T(8,128)(2,1)S(1)} %copy-done.2, bf16[6,512]{1,0:T(8,128)(2,1)S(1)} %collective-permute-done.refs_1_, bf16[6,512]{1,0:T(8,128)(2,1)S(1)} %collective-permute-done.1.refs_2_, ...), custom_call_target="tpu_custom_call" | custom-call | flops 1024 | bytes 1024 | tf_op jit(solution)/shard_map/correlate_staying/pallas_call | solution.py:214
  26.1 1.3 %collective-permute-start.7 = (bf16[32,2048]{1,0:T(8,128)(2,1)S(1)}, bf16[32,2048]{1,0:T(8,128)(2,1)S(1)}, u32[]{:S(2)}, u32[]{:S(2)}) collective-permute-start(bf16[32,2048]{1,0:T(8,128)(2,1)S(1)} %get-tuple-element.32), channel_id=1, source_target_pairs={{0,1},{1,0},{2,3},{3,2},{4,5},{5,4},{6,7},{7,6},{8,9},{9,8},{10,11... | collective-permute-start | bytes 393224 | tf_op jit(solution)/shard_map/ppermute | solution.py:28
  27.4 0.0 collective-permute-done.4.refs_1_
  27.4 3.1 %collective-permute-done.5.refs_2_ = bf16[32,2048]{1,0:T(8,128)(2,1)S(1)} collective-permute-done((bf16[32,2048]{1,0:T(8,128)(2,1)S(1)}, bf16[32,2048]{1,0:T(8,128)(2,1)S(1)}, u32[]{:S(2)}, u32[]{:S(2)}) %collective-permute-start.5) | collective-permute-done | bytes 131104 | tf_op jit(solution)/shard_map/ppermute | solution.py:28
  30.5 0.0 collective-permute-done.6.refs_3_
  30.5 0.1 added.1
  30.6 0.0 collective-permute-done.7
  30.6 0.8 %add_multiply_fusion = f32[32,2048]{1,0:T(8,128)} fusion(f32[32,2048]{1,0:T(8,128)S(1)} %added.1, bf16[32,2048]{1,0:T(8,128)(2,1)S(1)} %collective-permute-done.7, f32[32]{0:T(128)S(1)} %rsqrt_multiply_fusion), kind=kLoop, calls=%fused_computation.1 | loop fusion | flops 196608 | bytes 655488 | tf_op jit(solution)/shard_map/mul | solution.py:297
  (6 shorter events, 0.0 us)
Async XLA Ops:
  0.0 0.7 %copy-start.2 = (bf16[6,512]{1,0:T(8,128)(2,1)S(1)}, bf16[6,512]{1,0:T(8,128)(2,1)}, u32[]{:S(2)}) copy-start(bf16[6,512]{1,0:T(8,128)(2,1)} %refs_0_.1) | copy-start | bytes 18436
  0.0 3.3 %copy-start = (bf16[6,102400]{1,0:T(8,128)(2,1)S(1)}, bf16[6,102400]{1,0:T(8,128)(2,1)}, u32[]{:S(2)}) copy-start(bf16[6,102400]{1,0:T(8,128)(2,1)} %raw_ref.3) | copy-start | bytes 3686404
  0.0 3.3 %copy-start.1 = (s32[16,256]{1,0:T(8,128)S(1)}, s32[16,256]{1,0:T(8,128)}, u32[]{:S(2)}) copy-start(s32[16,256]{1,0:T(8,128)} %avail_ref.3) | copy-start | bytes 49156
  0.0 3.3 %copy-start.3 = (s32[48]{0:T(128)S(1)}, s32[48]{0:T(128)}, u32[]{:S(2)}) copy-start(s32[48]{0:T(128)} %usable_ref.3) | copy-start | bytes 580
  0.7 6.5 %collective-permute-start = (bf16[6,512]{1,0:T(8,128)(2,1)S(1)}, bf16[6,512]{1,0:T(8,128)(2,1)S(1)}, u32[]{:S(2)}, u32[]{:S(2)}) collective-permute-start(bf16[6,512]{1,0:T(8,128)(2,1)S(1)} %copy-done.2), channel_id=1, source_target_pairs={{0,8},{8,0},{16,24},{24,16},{1,9},{9,1},{17,25},{25,17},{2,10},{10... | collective-permute-start | bytes 18440 | tf_op jit(solution)/shard_map/ppermute | solution.py:28
  1.9 5.3 %collective-permute-start.1 = (bf16[6,512]{1,0:T(8,128)(2,1)S(1)}, bf16[6,512]{1,0:T(8,128)(2,1)S(1)}, u32[]{:S(2)}, u32[]{:S(2)}) collective-permute-start(bf16[6,512]{1,0:T(8,128)(2,1)S(1)} %copy-done.2), channel_id=1, source_target_pairs={{0,16},{8,24},{16,0},{24,8},{1,17},{9,25},{17,1},{25,9},{2,18},{10... | collective-permute-start | bytes 18440 | tf_op jit(solution)/shard_map/ppermute | solution.py:28
  3.1 4.0 %collective-permute-start.2 = (bf16[6,512]{1,0:T(8,128)(2,1)S(1)}, bf16[6,512]{1,0:T(8,128)(2,1)S(1)}, u32[]{:S(2)}, u32[]{:S(2)}) collective-permute-start(bf16[6,512]{1,0:T(8,128)(2,1)S(1)} %copy-done.2), channel_id=1, source_target_pairs={{0,24},{8,16},{16,8},{24,0},{1,25},{9,17},{17,9},{25,1},{2,26},{10... | collective-permute-start | bytes 18440 | tf_op jit(solution)/shard_map/ppermute | solution.py:28
  12.3 3.1 %collective-permute-start.3 = (bf16[96,2048]{1,0:T(8,128)(2,1)S(1)}, bf16[96,2048]{1,0:T(8,128)(2,1)S(1)}, u32[]{:S(2)}, u32[]{:S(2)}) collective-permute-start(bf16[96,2048]{1,0:T(8,128)(2,1)S(1)} %get-tuple-element.22), channel_id=1, source_target_pairs={{0,1},{1,0},{2,3},{3,2},{4,5},{5,4},{6,7},{7,6},{8,9},{9,8},{10,11... | collective-permute-start | bytes 1179656 | tf_op jit(solution)/shard_map/ppermute | solution.py:28
  15.6 11.8 %collective-permute-start.4 = (bf16[32,2048]{1,0:T(8,128)(2,1)S(1)}, bf16[32,2048]{1,0:T(8,128)(2,1)S(1)}, u32[]{:S(2)}, u32[]{:S(2)}) collective-permute-start(bf16[32,2048]{1,0:T(8,128)(2,1)S(1)} %get-tuple-element.29), channel_id=1, source_target_pairs={{0,4},{1,5},{2,6},{3,7},{4,0},{5,1},{6,2},{7,3},{8,12},{9,13},{10,... | collective-permute-start | bytes 393224 | tf_op jit(solution)/shard_map/ppermute | solution.py:28
  15.7 14.8 %collective-permute-start.5 = (bf16[32,2048]{1,0:T(8,128)(2,1)S(1)}, bf16[32,2048]{1,0:T(8,128)(2,1)S(1)}, u32[]{:S(2)}, u32[]{:S(2)}) collective-permute-start(bf16[32,2048]{1,0:T(8,128)(2,1)S(1)} %get-tuple-element.30), channel_id=1, source_target_pairs={{0,6},{1,7},{2,4},{3,5},{4,2},{5,3},{6,0},{7,1},{8,14},{9,15},{10,... | collective-permute-start | bytes 393224 | tf_op jit(solution)/shard_map/ppermute | solution.py:28
  18.2 12.3 %collective-permute-start.6 = (bf16[32,2048]{1,0:T(8,128)(2,1)S(1)}, bf16[32,2048]{1,0:T(8,128)(2,1)S(1)}, u32[]{:S(2)}, u32[]{:S(2)}) collective-permute-start(bf16[32,2048]{1,0:T(8,128)(2,1)S(1)} %get-tuple-element.31), channel_id=1, source_target_pairs={{0,2},{1,3},{2,0},{3,1},{4,6},{5,7},{6,4},{7,5},{8,10},{9,11},{10,... | collective-permute-start | bytes 393224 | tf_op jit(solution)/shard_map/ppermute | solution.py:28
  26.1 4.4 %collective-permute-start.7 = (bf16[32,2048]{1,0:T(8,128)(2,1)S(1)}, bf16[32,2048]{1,0:T(8,128)(2,1)S(1)}, u32[]{:S(2)}, u32[]{:S(2)}) collective-permute-start(bf16[32,2048]{1,0:T(8,128)(2,1)S(1)} %get-tuple-element.32), channel_id=1, source_target_pairs={{0,1},{1,0},{2,3},{3,2},{4,5},{5,4},{6,7},{7,6},{8,9},{9,8},{10,11... | collective-permute-start | bytes 393224 | tf_op jit(solution)/shard_map/ppermute | solution.py:28

commit v4 on v3

--- a/solution.py
+++ b/solution.py
@@ -29,8 +29,9 @@
 
 
 def template_kernel(
-    shares, stay, raw_ref, avail_ref, usable_ref, token_ref, out_ref, flat, rows, avail_cols
+    shares, stay, raw_ref, avail_ref, usable_ref, token_ref, *refs
 ):
+    out_ref, *factor_refs, flat, rows, avail_cols = refs
     channels, width = raw_ref.shape
     stations, count = avail_ref.shape
     tiles = width // LANES
@@ -57,11 +58,22 @@
 
     station_row = lax.broadcasted_iota(jnp.int32, (stations, LANES), 0)
     avail = avail_ref[...].astype(jnp.float32)
+    def per_row(by_station):
+        return lax.dot_general(
+            avail, by_station, (((0,), (0,)), ((), ())), preferred_element_type=jnp.float32
+        )
+
+    for factor_ref in factor_refs:
+        usable_here = jnp.zeros((stations, LANES), jnp.float32)
+        for station in range(stations):
+            number = sum(usable_ref[station * COMPONENTS + part] for part in range(COMPONENTS))
+            usable_here = jnp.where(station_row == station, number.astype(jnp.float32), usable_here)
+        avail_cols[stations_here] = per_row(usable_here)
+        counted = avail_cols[stations_here, pl.ds(pl.multiple_of(me * own, own), own), :]
+        factor_ref[...] = math.sqrt(TLEN) * lax.rsqrt(jnp.maximum(counted, 1.0))
     for local_station in range(stations_here):
-        chosen = (station_row == me * stations_here + local_station).astype(jnp.float32)
-        avail_cols[local_station] = lax.dot_general(
-            avail, chosen, (((0,), (0,)), ((), ())), preferred_element_type=jnp.float32
-        )
+        chosen = station_row == me * stations_here + local_station
+        avail_cols[local_station] = per_row(chosen.astype(jnp.float32))
 
     lane = lax.broadcasted_iota(jnp.int32, (groups, LANES), 1)
     last = TLEN - (DEPTH_TILES - 1) * LANES
@@ -116,20 +128,23 @@
     channels, width = raw.shape
     stations, count = available.shape
     taken = 2 * count // shares if stay else count - 2 * count // shares
+    outs = [jax.ShapeDtypeStruct((channels, taken, DEPTH), jnp.bfloat16)]
+    if stay:
+        outs.append(jax.ShapeDtypeStruct((count // shares, LANES), jnp.float32))
     return pl.pallas_call(
         functools.partial(template_kernel, shares, stay),
-        out_shape=jax.ShapeDtypeStruct((channels, taken, DEPTH), jnp.bfloat16),
+        out_shape=outs,
         in_specs=[
             pl.BlockSpec(memory_space=pltpu.VMEM),
             pl.BlockSpec(memory_space=pltpu.VMEM),
             pl.BlockSpec(memory_space=pltpu.SMEM),
             pl.BlockSpec(memory_space=pltpu.VMEM),
         ],
-        out_specs=pl.BlockSpec(memory_space=pltpu.VMEM),
+        out_specs=[pl.BlockSpec(memory_space=pltpu.VMEM)] * len(outs),
         scratch_shapes=[
             pltpu.VMEM((taken * TLEN // LANES * SUBLANES, LANES), jnp.float32),
             pltpu.VMEM((2, DEPTH_TILES, taken, LANES), jnp.float32),
-            pltpu.VMEM((channels // COMPONENTS, count, LANES), jnp.float32),
+            pltpu.VMEM((channels // COMPONENTS + 1, count, LANES), jnp.float32),
         ],
         compiler_params=pltpu.CompilerParams(vmem_limit_bytes=VMEM_LIMIT),
         cost_estimate=pl.CostEstimate(flops=1 << 10, transcendentals=0, bytes_accessed=1 << 10),
@@ -141,9 +156,9 @@
     return pltpu.roll(value, value.shape[1] - by, 1) if by else value
 
 
-def correlate_kernel(blocks, weighted_ref, *refs):
+def windows_kernel(blocks, *refs):
     segments = refs[:blocks]
-    mine_ref, other_ref, scale, record, windows = refs[blocks:]
+    windows, scale, record = refs[blocks:]
     channels, segment = segments[0].shape
     lags = blocks * segment
     wide = record.shape[1]
@@ -181,8 +196,31 @@
 
     lax.fori_loop(0, channels, one_record, 0, unroll=2)
 
-    half = weighted_ref.shape[1] // 2
-    tile = next(by * LANES for by in (16, 8, 4, 2, 1) if lags % (by * LANES) == 0)
+
+def all_windows(segments, name):
+    channels, segment = segments[0].shape
+    blocks = len(segments)
+    lags = blocks * segment
+    return pl.pallas_call(
+        functools.partial(windows_kernel, blocks),
+        out_shape=(
+            jax.ShapeDtypeStruct((channels, LANES, lags + DEPTH - LANES), jnp.bfloat16),
+            jax.ShapeDtypeStruct((SUBLANES, lags), jnp.float32),
+        ),
+        in_specs=[pl.BlockSpec(memory_space=pltpu.VMEM)] * blocks,
+        out_specs=(pl.BlockSpec(memory_space=pltpu.VMEM),) * 2,
+        scratch_shapes=[pltpu.VMEM((SUBLANES, lags + DEPTH), jnp.float32)],
+        compiler_params=pltpu.CompilerParams(vmem_limit_bytes=VMEM_LIMIT),
+        cost_estimate=pl.CostEstimate(flops=1 << 10, transcendentals=0, bytes_accessed=1 << 10),
+        name=name,
+    )(*segments)
+
+
+def correlate_kernel(weighted_ref, windows, scale, *outs):
+    channels, count, depth = weighted_ref.shape
+    lags = scale.shape[1]
+    rows = count // len(outs)
+    tile = next(by for by in (16 * LANES, 8 * LANES, 4 * LANES, 2 * LANES) if lags % by == 0)
 
     def one_tile(first):
         here = pl.ds(first, tile)
@@ -190,8 +228,12 @@
         for channel in range(channels):
             signal = jnp.concatenate(
                 [
-                    windows[channel, : min(LANES, TLEN - start), pl.ds(first + start, tile)]
-                    for start in range(0, TLEN, LANES)
+                    windows[
+                        channel,
+                        : min(LANES, TLEN - part * LANES),
+                        pl.ds(pl.multiple_of(first + part * LANES, LANES), tile),
+                    ]
+                    for part in range(depth // LANES)
                 ],
                 axis=0,
             )
@@ -199,35 +241,33 @@
             matched = jnp.dot(weights, signal, preferred_element_type=jnp.float32)
             term = matched * scale[channel : channel + 1, here]
             total = term if total is None else total + term
-        mine_ref[:, here] = total[:half]
-        other_ref[:, here] = total[half:].astype(other_ref.dtype)
-
-    for step in range(lags // tile):
-        one_tile(step * tile)
-
-
-def correlations(weighted, segments, name):
+        for place, out in enumerate(outs):
+            out[:, here] = total[place * rows : (place + 1) * rows].astype(out.dtype)
+
+    if lags == tile:
+        one_tile(0)
+    else:
+
+        def one_step(step, carry):
+            one_tile(pl.multiple_of(step * tile, LANES))
+            return carry
+
+        lax.fori_loop(0, lags // tile, one_step, 0)
+
+
+def correlations(weighted, windows, scale, blocks, name):
     channels, count, depth = weighted.shape
-    segment = segments[0].shape[1]
-    blocks = len(segments)
-    lags = blocks * segment
-    return pl.pallas_call(
-        functools.partial(correlate_kernel, blocks),
-        out_shape=(
-            jax.ShapeDtypeStruct((count // 2, lags), jnp.float32),
-            jax.ShapeDtypeStruct((count // 2, lags), jnp.bfloat16),
-        ),
-        in_specs=[pl.BlockSpec(memory_space=pltpu.VMEM)] * (1 + blocks),
-        out_specs=(pl.BlockSpec(memory_space=pltpu.VMEM),) * 2,
-        scratch_shapes=[
-            pltpu.VMEM((SUBLANES, lags), jnp.float32),
-            pltpu.VMEM((SUBLANES, lags + depth), jnp.float32),
-            pltpu.VMEM((channels, LANES, lags + depth - LANES), jnp.bfloat16),
-        ],
+    lags = scale.shape[1]
+    kinds = [jnp.float32] * (blocks // 2) + [jnp.bfloat16] * (blocks // 2)
+    return pl.pallas_call(
+        correlate_kernel,
+        out_shape=[jax.ShapeDtypeStruct((count // blocks, lags), kind) for kind in kinds],
+        in_specs=[pl.BlockSpec(memory_space=pltpu.VMEM)] * 3,
+        out_specs=[pl.BlockSpec(memory_space=pltpu.VMEM)] * blocks,
         compiler_params=pltpu.CompilerParams(vmem_limit_bytes=VMEM_LIMIT),
         cost_estimate=pl.CostEstimate(flops=1 << 10, transcendentals=0, bytes_accessed=1 << 10),
         name=name,
-    )(weighted, *segments)
+    )(weighted, windows, scale)
 
 
 def first_kernel(token_ref):
@@ -264,11 +304,31 @@
     )(*terms)
 
 
+def scale_kernel(factor_ref, *refs):
+    factor = factor_ref[...]
+    for start in range(0, refs[-1].shape[1], LANES):
+        here = slice(start, start + LANES)
+        total = refs[0][:, here]
+        for ref in refs[1:-1]:
+            total = total + ref[:, here].astype(jnp.float32)
+        refs[-1][:, here] = total * factor
+
+
+def scaled(factor, *terms):
+    return pl.pallas_call(
+        scale_kernel,
+        out_shape=jax.ShapeDtypeStruct(terms[0].shape, jnp.float32),
+        in_specs=[pl.BlockSpec(memory_space=pltpu.VMEM)] * (1 + len(terms)),
+        out_specs=pl.BlockSpec(memory_space=pltpu.VMEM),
+        compiler_params=pltpu.CompilerParams(vmem_limit_bytes=4 << 20),
+        cost_estimate=pl.CostEstimate(flops=1 << 10, transcendentals=0, bytes_accessed=1 << 10),
+        name="scaled",
+    )(factor, *terms)
+
+
 def local(waveforms, templates, available, usable):
     blocks = lax.axis_size("blk")
     shares = lax.axis_size("sta")
-    my_share = lax.axis_index("sta")
-    own_rows = available.shape[1] // shares
     chips = shares // 2
 
     waveforms, token = lax.optimization_barrier((waveforms, first()))
@@ -278,23 +338,23 @@
     segments = [segments[by] for by in range(blocks)]
 
     wide, narrow = jnp.float32, jnp.bfloat16
-    weighted = weighted_templates(templates, available, usable, token, shares, False)
-    mine, other = correlations(weighted, segments, "correlate_leaving")
-    summed = (mine + exchanged(other, "sta", 1).astype(wide)).astype(narrow)
-    sent = [summed[by * own_rows : (by + 1) * own_rows] for by in range(chips - 1)]
-    sent, segments, later = lax.optimization_barrier((sent, segments, token))
-    arrived = [
-        exchanged(sent[by - 1], "sta", 2 * by)
-        for by in sorted(range(1, chips), key=lambda by: -(by ^ (by >> 1)))
-    ]
-    weighted = weighted_templates(templates, available, usable, later, shares, True)
-    mine, other = correlations(weighted, segments, "correlate_staying")
-    stacked = added(mine, *arrived) + exchanged(other, "sta", 1).astype(wide)
-
-    station_usable = jnp.sum(usable.reshape(-1, COMPONENTS), axis=1).astype(jnp.float32)
-    owned = lax.dynamic_slice_in_dim(available, my_share * own_rows, own_rows, 1)
-    counted = jnp.sum(owned.astype(jnp.float32) * station_usable[:, None], axis=0)
-    return math.sqrt(TLEN) * stacked * lax.rsqrt(jnp.maximum(counted, 1.0))[:, None]
+    (weighted,) = weighted_templates(templates, available, usable, token, shares, False)
+    windows, scale = all_windows(segments, "windows")
+    sums = correlations(weighted, windows, scale, 2 * (chips - 1), "correlate_leaving")
+    order = sorted(range(1, chips), key=lambda by: -(by ^ (by >> 1)))
+    partner = {by: exchanged(sums[chips - 1 + by - 1], "sta", 1) for by in order}
+    sent = []
+    for by in order:
+        own = sums[by - 1]
+        if sent:
+            own, sent[-1] = lax.optimization_barrier((own, sent[-1]))
+        sent.append((own + partner[by].astype(wide)).astype(narrow))
+    sent[-1], scale, later = lax.optimization_barrier((sent[-1], scale, token))
+    arrived = [exchanged(term, "sta", 2 * by) for by, term in zip(order, sent)]
+
+    weighted, factor = weighted_templates(templates, available, usable, later, shares, True)
+    mine, other = correlations(weighted, windows, scale, 2, "correlate_staying")
+    return scaled(factor, added(mine, *arrived), exchanged(other, "sta", 1))
 
 
 def solution(mesh):

time: 31.5 us -> 30.9 us (0.981)
  waiting for transfers between devices: 4.15 us -> 6.12 us
  Pallas kernels: 15.9 us -> 14.1 us
  other arithmetic: 1.1 us -> 0.1 us
    ppermute x8 -> x10, waiting for transfers between devices: 4.15 us -> 6.12 us  [exchanged(): return lax.ppermute(array, axis, [(i, i ^ by) for i in range(length)])]
    pallas_call x2 -> x4, Pallas kernels: 9.5 us -> 7.72 us  [the longest x2 4.49 us: correlations(): pl.pallas_call(correlate_kernel, out_shape=[jax.ShapeDtypeStruct((count /...]
    mul x2 -> x0, other arithmetic: 0.79 us -> none  [local(): math.sqrt(TLEN) * stacked * lax.rsqrt(jnp.maximum(counted, 1.0))[:, None]]
    ppermute x8 -> x10, starting transfers between devices: 9.32 us -> 9.51 us  [exchanged(): return lax.ppermute(array, axis, [(i, i ^ by) for i in range(length)])]
  transfers between devices with their start and end apart: 8 -> 10, of which waited for: 2 -> 3; matrix products, arithmetic and copies ran while one was open for 1% -> 0% of each run, Pallas kernels for 34% -> 27%
where the time goes in v4:
time: 30.9 us; the launch traced here: 30.6 us
  Pallas kernels  14.1 us (46%)
  starting transfers between devices  9.51 us (31%)
  waiting for transfers between devices  6.12 us (20%)
  local copies, waits for them, and re-layouts  0.68 us (2%)
    ppermute x10, starting transfers between devices, exchanged(): return lax.ppermute(array, axis, [(i, i ^ by) for i in range(length)])  9.51 us
    pallas_call x2, Pallas kernels, weighted_templates(): pl.pallas_call(functools.partial(template_kernel, shares, stay), out_shap...  6.34 us
    ppermute x10, waiting for transfers between devices, exchanged(): return lax.ppermute(array, axis, [(i, i ^ by) for i in range(length)])  6.12 us
    pallas_call x2, Pallas kernels, correlations(): pl.pallas_call(correlate_kernel, out_shape=[jax.ShapeDtypeStruct((count /...  4.49 us
    pallas_call x1, Pallas kernels, all_windows(): pl.pallas_call(functools.partial(windows_kernel, blocks), out_shape=(jax....  2.5 us
    pallas_call x1, Pallas kernels, scaled(): pl.pallas_call(scale_kernel, out_shape=jax.ShapeDtypeStruct(terms[0].shap...  0.73 us
    unnamed x8, local copies, waits for them, and re-layouts  0.68 us
  transfers between devices with their start and end apart: 10, of which 3 were waited for; matrix products, arithmetic and copies ran while one was open for 0% of the time, Pallas kernels for 27%

profile of v4, /device:TPU:17, one launch (start us, length us, event | category | flops | bytes accessed | tf_op | source)
XLA Modules:
  0.0 30.6 jit_solution(146710740329009772)
XLA Ops:
  0.0 0.0 copy-start
  0.0 0.7 %copy-done.2 = bf16[6,512]{1,0:T(8,128)(2,1)S(1)} copy-done((bf16[6,512]{1,0:T(8,128)(2,1)S(1)}, bf16[6,512]{1,0:T(8,128)(2,1)}, u32[]{:S(2)}) %copy-start.2) | copy-done | bytes 6168
  0.7 2.2 %collective-permute-start.2 = (bf16[6,512]{1,0:T(8,128)(2,1)S(1)}, bf16[6,512]{1,0:T(8,128)(2,1)S(1)}, u32[]{:S(2)}, u32[]{:S(2)}) collective-permute-start(bf16[6,512]{1,0:T(8,128)(2,1)S(1)} %copy-done.2), channel_id=1, source_target_pairs={{0,24},{8,16},{16,8},{24,0},{1,25},{9,17},{17,9},{25,1},{2,26},{10... | collective-permute-start | bytes 18440 | tf_op jit(solution)/shard_map/ppermute | solution.py:28
  2.9 0.2 collective-permute-start.1
  3.1 0.3 collective-permute-start
  3.3 0.0 copy-done.3
  3.4 0.0 copy-done.1
  3.4 0.0 copy-done
  3.4 3.8 %templates_leaving.1.weighted_ref = bf16[6,192,512]{2,1,0:T(8,128)(2,1)S(1)} custom-call(bf16[6,102400]{1,0:T(8,128)(2,1)S(1)} %copy-done, s32[16,256]{1,0:T(8,128)S(1)} %copy-done.1, s32[48]{0:T(128)S(1)} %copy-done.3, f32[8,128]{1,0:T(8,128)S(1)} %first.1.token_ref), custom_call_target="tpu_custom_call" | custom-call | flops 1024 | bytes 1024 | tf_op jit(solution)/shard_map/templates_leaving/pallas_call | solution.py:134
  7.2 0.0 collective-permute-done.2.refs_3_
  7.2 0.0 collective-permute-done.1.refs_2_
  7.2 0.0 collective-permute-done.refs_1_
  7.2 2.5 %windows.1 = (bf16[6,128,2432]{2,1,0:T(8,128)(2,1)S(1)}, f32[8,2048]{1,0:T(8,128)S(1)}) custom-call(bf16[6,512]{1,0:T(8,128)(2,1)S(1)} %copy-done.2, bf16[6,512]{1,0:T(8,128)(2,1)S(1)} %collective-permute-done.refs_1_, bf16[6,512]{1,0:T(8,128)(2,1)S(1)} %collective-permute-done.1.refs_2_, bf16[6,512]{1,0:T(8,128)(2,1)S(1)} %collective-permute-done.2.refs_3_), custom_call_target="tpu_custom_call" | custom-call | flops 1024 | bytes 1024 | tf_op jit(solution)/shard_map/windows/pallas_call | solution.py:204
  9.7 2.6 %correlate_leaving.1 = (f32[32,2048]{1,0:T(8,128)S(1)}, f32[32,2048]{1,0:T(8,128)S(1)}, f32[32,2048]{1,0:T(8,128)S(1)}, bf16[32,2048]{1,0:T(8,128)(2,1)S(1)}, bf...) custom-call(bf16[6,192,512]{2,1,0:T(8,128)(2,1)S(1)} %templates_leaving.1.weighted_ref, ...), custom_call_target="tpu_custom_call" | custom-call | flops 1024 | bytes 1024 | tf_op jit(solution)/shard_map/correlate_leaving/pallas_call | solution.py:262
  12.4 1.6 %collective-permute-start.3 = (bf16[32,2048]{1,0:T(8,128)(2,1)S(1)}, bf16[32,2048]{1,0:T(8,128)(2,1)S(1)}, u32[]{:S(2)}, u32[]{:S(2)}) collective-permute-start(bf16[32,2048]{1,0:T(8,128)(2,1)S(1)} %get-tuple-element.33), channel_id=1, source_target_pairs={{0,1},{1,0},{2,3},{3,2},{4,5},{5,4},{6,7},{7,6},{8,9},{9,8},{10,11... | collective-permute-start | bytes 393224 | tf_op jit(solution)/shard_map/ppermute | solution.py:28
  13.9 0.1 collective-permute-start.4
  14.0 0.4 %collective-permute-start.5 = (bf16[32,2048]{1,0:T(8,128)(2,1)S(1)}, bf16[32,2048]{1,0:T(8,128)(2,1)S(1)}, u32[]{:S(2)}, u32[]{:S(2)}) collective-permute-start(bf16[32,2048]{1,0:T(8,128)(2,1)S(1)} %get-tuple-element.37), channel_id=1, source_target_pairs={{0,1},{1,0},{2,3},{3,2},{4,5},{5,4},{6,7},{7,6},{8,9},{9,8},{10,11... | collective-permute-start | bytes 393224 | tf_op jit(solution)/shard_map/ppermute | solution.py:28
  14.4 0.5 %collective-permute-done.3 = bf16[32,2048]{1,0:T(8,128)(2,1)S(1)} collective-permute-done((bf16[32,2048]{1,0:T(8,128)(2,1)S(1)}, bf16[32,2048]{1,0:T(8,128)(2,1)S(1)}, u32[]{:S(2)}, u32[]{:S(2)}) %collective-permute-start.3) | collective-permute-done | bytes 131104 | tf_op jit(solution)/shard_map/ppermute | solution.py:28
  15.0 0.1 collective-permute-start.6
  15.0 0.2 collective-permute-done.4
  15.3 2.3 %collective-permute-start.7 = (bf16[32,2048]{1,0:T(8,128)(2,1)S(1)}, bf16[32,2048]{1,0:T(8,128)(2,1)S(1)}, u32[]{:S(2)}, u32[]{:S(2)}) collective-permute-start(bf16[32,2048]{1,0:T(8,128)(2,1)S(1)} %add_convert_fusion.1), channel_id=1, source_target_pairs={{0,6},{1,7},{2,4},{3,5},{4,2},{5,3},{6,0},{7,1},{8,14},{9,15},{10,... | collective-permute-start | bytes 393224 | tf_op jit(solution)/shard_map/ppermute | solution.py:28
  17.6 0.0 collective-permute-done.5
  17.6 1.1 %collective-permute-start.8 = (bf16[32,2048]{1,0:T(8,128)(2,1)S(1)}, bf16[32,2048]{1,0:T(8,128)(2,1)S(1)}, u32[]{:S(2)}, u32[]{:S(2)}) collective-permute-start(bf16[32,2048]{1,0:T(8,128)(2,1)S(1)} %add_convert_fusion), channel_id=1, source_target_pairs={{0,2},{1,3},{2,0},{3,1},{4,6},{5,7},{6,4},{7,5},{8,10},{9,11},{10,... | collective-permute-start | bytes 393224 | tf_op jit(solution)/shard_map/ppermute | solution.py:28
  18.8 2.5 %templates_staying.1 = (bf16[6,64,512]{2,1,0:T(8,128)(2,1)S(1)}, f32[32,128]{1,0:T(8,128)S(1)}) custom-call(bf16[6,102400]{1,0:T(8,128)(2,1)S(1)} %copy-done, s32[16,256]{1,0:T(8,128)S(1)} %copy-done.1, s32[48]{0:T(128)S(1)} %copy-done.3, f32[8,128]{1,0:T(8,128)S(1)} %first.1.token_ref), custom_call_target="tpu_custom_call" | custom-call | flops 1024 | bytes 1024 | tf_op jit(solution)/shard_map/templates_staying/pallas_call | solution.py:134
  21.3 1.9 %correlate_staying.1 = (f32[32,2048]{1,0:T(8,128)S(1)}, bf16[32,2048]{1,0:T(8,128)(2,1)S(1)}) custom-call(bf16[6,64,512]{2,1,0:T(8,128)(2,1)S(1)} %get-tuple-element.40.weighted_ref, bf16[6,128,2432]{2,1,0:T(8,128)(2,1)S(1)} %get-tuple-element.28.windows, f32[8,2048]{1,0:T(8,128)S(1)} %get-tuple-element.41.scale), custom_call_target="tpu_custom_call" | custom-call | flops 1024 | bytes 1024 | tf_op jit(solution)/shard_map/correlate_staying/pallas_call | solution.py:262
  23.2 1.3 %collective-permute-start.9 = (bf16[32,2048]{1,0:T(8,128)(2,1)S(1)}, bf16[32,2048]{1,0:T(8,128)(2,1)S(1)}, u32[]{:S(2)}, u32[]{:S(2)}) collective-permute-start(bf16[32,2048]{1,0:T(8,128)(2,1)S(1)} %get-tuple-element.46), channel_id=1, source_target_pairs={{0,1},{1,0},{2,3},{3,2},{4,5},{5,4},{6,7},{7,6},{8,9},{9,8},{10,11... | collective-permute-start | bytes 393224 | tf_op jit(solution)/shard_map/ppermute | solution.py:28
  24.4 0.0 collective-permute-done.6.refs_1_
  24.4 5.4 %collective-permute-done.7.refs_2_ = bf16[32,2048]{1,0:T(8,128)(2,1)S(1)} collective-permute-done((bf16[32,2048]{1,0:T(8,128)(2,1)S(1)}, bf16[32,2048]{1,0:T(8,128)(2,1)S(1)}, u32[]{:S(2)}, u32[]{:S(2)}) %collective-permute-start.7) | collective-permute-done | bytes 131104 | tf_op jit(solution)/shard_map/ppermute | solution.py:28
  29.8 0.0 collective-permute-done.8.refs_3_
  29.8 0.1 added.1.refs_0_
  29.9 0.0 collective-permute-done.9.refs_1_
  29.9 0.7 %scaled.1 = f32[32,2048]{1,0:T(8,128)} custom-call(f32[32,128]{1,0:T(8,128)S(1)} %get-tuple-element.39.factor_ref, f32[32,2048]{1,0:T(8,128)S(1)} %added.1.refs_0_, bf16[32,2048]{1,0:T(8,128)(2,1)S(1)} %collective-permute-done.9.refs_1_), custom_call_target="tpu_custom_call" | custom-call | flops 1024 | bytes 1024 | tf_op jit(solution)/shard_map/scaled/pallas_call | solution.py:318
  (7 shorter events, 0.1 us)
Async XLA Ops:
  0.0 0.7 %copy-start.2 = (bf16[6,512]{1,0:T(8,128)(2,1)S(1)}, bf16[6,512]{1,0:T(8,128)(2,1)}, u32[]{:S(2)}) copy-start(bf16[6,512]{1,0:T(8,128)(2,1)} %refs_0_) | copy-start | bytes 18436
  0.0 3.3 %copy-start.3 = (s32[48]{0:T(128)S(1)}, s32[48]{0:T(128)}, u32[]{:S(2)}) copy-start(s32[48]{0:T(128)} %usable_ref.3) | copy-start | bytes 580
  0.0 3.3 %copy-start.1 = (s32[16,256]{1,0:T(8,128)S(1)}, s32[16,256]{1,0:T(8,128)}, u32[]{:S(2)}) copy-start(s32[16,256]{1,0:T(8,128)} %avail_ref.3) | copy-start | bytes 49156
  0.0 3.3 %copy-start = (bf16[6,102400]{1,0:T(8,128)(2,1)S(1)}, bf16[6,102400]{1,0:T(8,128)(2,1)}, u32[]{:S(2)}) copy-start(bf16[6,102400]{1,0:T(8,128)(2,1)} %raw_ref.3) | copy-start | bytes 3686404
  0.7 6.5 %collective-permute-start.2 = (bf16[6,512]{1,0:T(8,128)(2,1)S(1)}, bf16[6,512]{1,0:T(8,128)(2,1)S(1)}, u32[]{:S(2)}, u32[]{:S(2)}) collective-permute-start(bf16[6,512]{1,0:T(8,128)(2,1)S(1)} %copy-done.2), channel_id=1, source_target_pairs={{0,24},{8,16},{16,8},{24,0},{1,25},{9,17},{17,9},{25,1},{2,26},{10... | collective-permute-start | bytes 18440 | tf_op jit(solution)/shard_map/ppermute | solution.py:28
  2.9 4.3 %collective-permute-start.1 = (bf16[6,512]{1,0:T(8,128)(2,1)S(1)}, bf16[6,512]{1,0:T(8,128)(2,1)S(1)}, u32[]{:S(2)}, u32[]{:S(2)}) collective-permute-start(bf16[6,512]{1,0:T(8,128)(2,1)S(1)} %copy-done.2), channel_id=1, source_target_pairs={{0,16},{8,24},{16,0},{24,8},{1,17},{9,25},{17,1},{25,9},{2,18},{10... | collective-permute-start | bytes 18440 | tf_op jit(solution)/shard_map/ppermute | solution.py:28
  3.1 4.1 %collective-permute-start = (bf16[6,512]{1,0:T(8,128)(2,1)S(1)}, bf16[6,512]{1,0:T(8,128)(2,1)S(1)}, u32[]{:S(2)}, u32[]{:S(2)}) collective-permute-start(bf16[6,512]{1,0:T(8,128)(2,1)S(1)} %copy-done.2), channel_id=1, source_target_pairs={{0,8},{8,0},{16,24},{24,16},{1,9},{9,1},{17,25},{25,17},{2,10},{10... | collective-permute-start | bytes 18440 | tf_op jit(solution)/shard_map/ppermute | solution.py:28
  12.4 2.6 %collective-permute-start.3 = (bf16[32,2048]{1,0:T(8,128)(2,1)S(1)}, bf16[32,2048]{1,0:T(8,128)(2,1)S(1)}, u32[]{:S(2)}, u32[]{:S(2)}) collective-permute-start(bf16[32,2048]{1,0:T(8,128)(2,1)S(1)} %get-tuple-element.33), channel_id=1, source_target_pairs={{0,1},{1,0},{2,3},{3,2},{4,5},{5,4},{6,7},{7,6},{8,9},{9,8},{10,11... | collective-permute-start | bytes 393224 | tf_op jit(solution)/shard_map/ppermute | solution.py:28
  13.9 1.3 %collective-permute-start.4 = (bf16[32,2048]{1,0:T(8,128)(2,1)S(1)}, bf16[32,2048]{1,0:T(8,128)(2,1)S(1)}, u32[]{:S(2)}, u32[]{:S(2)}) collective-permute-start(bf16[32,2048]{1,0:T(8,128)(2,1)S(1)} %get-tuple-element.35), channel_id=1, source_target_pairs={{0,1},{1,0},{2,3},{3,2},{4,5},{5,4},{6,7},{7,6},{8,9},{9,8},{10,11... | collective-permute-start | bytes 393224 | tf_op jit(solution)/shard_map/ppermute | solution.py:28
  14.0 3.6 %collective-permute-start.5 = (bf16[32,2048]{1,0:T(8,128)(2,1)S(1)}, bf16[32,2048]{1,0:T(8,128)(2,1)S(1)}, u32[]{:S(2)}, u32[]{:S(2)}) collective-permute-start(bf16[32,2048]{1,0:T(8,128)(2,1)S(1)} %get-tuple-element.37), channel_id=1, source_target_pairs={{0,1},{1,0},{2,3},{3,2},{4,5},{5,4},{6,7},{7,6},{8,9},{9,8},{10,11... | collective-permute-start | bytes 393224 | tf_op jit(solution)/shard_map/ppermute | solution.py:28
  15.0 9.5 %collective-permute-start.6 = (bf16[32,2048]{1,0:T(8,128)(2,1)S(1)}, bf16[32,2048]{1,0:T(8,128)(2,1)S(1)}, u32[]{:S(2)}, u32[]{:S(2)}) collective-permute-start(bf16[32,2048]{1,0:T(8,128)(2,1)S(1)} %add_convert_fusion.2), channel_id=1, source_target_pairs={{0,4},{1,5},{2,6},{3,7},{4,0},{5,1},{6,2},{7,3},{8,12},{9,13},{10,... | collective-permute-start | bytes 393224 | tf_op jit(solution)/shard_map/ppermute | solution.py:28
  15.3 14.5 %collective-permute-start.7 = (bf16[32,2048]{1,0:T(8,128)(2,1)S(1)}, bf16[32,2048]{1,0:T(8,128)(2,1)S(1)}, u32[]{:S(2)}, u32[]{:S(2)}) collective-permute-start(bf16[32,2048]{1,0:T(8,128)(2,1)S(1)} %add_convert_fusion.1), channel_id=1, source_target_pairs={{0,6},{1,7},{2,4},{3,5},{4,2},{5,3},{6,0},{7,1},{8,14},{9,15},{10,... | collective-permute-start | bytes 393224 | tf_op jit(solution)/shard_map/ppermute | solution.py:28
  17.6 12.2 %collective-permute-start.8 = (bf16[32,2048]{1,0:T(8,128)(2,1)S(1)}, bf16[32,2048]{1,0:T(8,128)(2,1)S(1)}, u32[]{:S(2)}, u32[]{:S(2)}) collective-permute-start(bf16[32,2048]{1,0:T(8,128)(2,1)S(1)} %add_convert_fusion), channel_id=1, source_target_pairs={{0,2},{1,3},{2,0},{3,1},{4,6},{5,7},{6,4},{7,5},{8,10},{9,11},{10,... | collective-permute-start | bytes 393224 | tf_op jit(solution)/shard_map/ppermute | solution.py:28
  23.2 6.7 %collective-permute-start.9 = (bf16[32,2048]{1,0:T(8,128)(2,1)S(1)}, bf16[32,2048]{1,0:T(8,128)(2,1)S(1)}, u32[]{:S(2)}, u32[]{:S(2)}) collective-permute-start(bf16[32,2048]{1,0:T(8,128)(2,1)S(1)} %get-tuple-element.46), channel_id=1, source_target_pairs={{0,1},{1,0},{2,3},{3,2},{4,5},{5,4},{6,7},{7,6},{8,9},{9,8},{10,11... | collective-permute-start | bytes 393224 | tf_op jit(solution)/shard_map/ppermute | solution.py:28

commit v5 on v4

--- a/solution.py
+++ b/solution.py
@@ -31,7 +31,7 @@
 def template_kernel(
     shares, stay, raw_ref, avail_ref, usable_ref, token_ref, *refs
 ):
-    out_ref, *factor_refs, flat, rows, avail_cols = refs
+    out_ref, *factor_refs, rows, avail_cols = refs
     channels, width = raw_ref.shape
     stations, count = avail_ref.shape
     tiles = width // LANES
@@ -44,17 +44,32 @@
     groups = len(taken) * chip_rows // PERIOD
     me = lax.axis_index("sta")
     start = me // 2 if stay else me // 2 + 1
-    unroll = next(by for by in (25, 20, 16, 10, 8, 5, 4, 2, 1) if chip_tiles % by == 0)
-
-    def spread(step, carry):
-        source = lax.rem(start * chip_tiles + step * unroll, tiles)
-        for sub in range(unroll):
-            value = raw_ref[:, pl.ds(pl.multiple_of((source + sub) * LANES, LANES), LANES)]
-            there = pl.multiple_of((step * unroll + sub) * SUBLANES, SUBLANES)
-            flat[pl.ds(there, channels), :] = value.astype(jnp.float32)
+    last = TLEN - (DEPTH_TILES - 1) * LANES
+    lane = lax.broadcasted_iota(jnp.int32, (channels, LANES), 1)
+
+    def one_group(group, carry):
+        source = lax.rem(start * chip_tiles + group * PERIOD_TILES, tiles)
+        for which in range(PERIOD):
+            first, offset = divmod(which * TLEN, LANES)
+            pieces = []
+            for part in range(DEPTH_TILES):
+                begin = pl.multiple_of((source + first + part) * LANES, LANES)
+                piece = raw_ref[:, pl.ds(begin, LANES)].astype(jnp.float32)
+                if offset:
+                    piece = pltpu.roll(piece, LANES - offset, 1)
+                pieces.append(piece)
+            row = pl.multiple_of((group * PERIOD + which) * SUBLANES, SUBLANES)
+            for part in range(DEPTH_TILES):
+                value = pieces[part]
+                if part + 1 < DEPTH_TILES:
+                    if offset:
+                        value = jnp.where(lane < LANES - offset, value, pieces[part + 1])
+                else:
+                    value = jnp.where(lane < last, value, 0.0)
+                rows[part, pl.ds(row, channels), :] = value
         return carry
 
-    lax.fori_loop(0, len(taken) * chip_tiles // unroll, spread, 0)
+    lax.fori_loop(0, groups, one_group, 0, unroll=8)
 
     station_row = lax.broadcasted_iota(jnp.int32, (stations, LANES), 0)
     avail = avail_ref[...].astype(jnp.float32)
@@ -75,20 +90,16 @@
         chosen = station_row == me * stations_here + local_station
         avail_cols[local_station] = per_row(chosen.astype(jnp.float32))
 
-    lane = lax.broadcasted_iota(jnp.int32, (groups, LANES), 1)
-    last = TLEN - (DEPTH_TILES - 1) * LANES
     block_lane = lax.broadcasted_iota(jnp.int32, (own, LANES), 1)
 
-    def one_step(step, carry):
-        channel = jnp.maximum(step - 1, 0)
-        ready = 1 - step % 2
+    def one_channel(channel, carry):
         use = usable_ref[me * channels + channel].astype(jnp.float32)
         for place in range(2 * len(taken)):
             core, chip = divmod(place, len(taken))
             owner = me ^ (2 * taken[chip] + core)
             moved = lax.rem(owner // 2 - start + chips, chips) * chip_rows + owner % 2 * own
-            here = pl.ds(pl.multiple_of(moved, own), own)
-            parts = [rows[ready, part, here, :] for part in range(DEPTH_TILES)]
+            here = pl.ds(moved * SUBLANES + channel, own, stride=SUBLANES)
+            parts = [rows[part, here, :] for part in range(DEPTH_TILES)]
             mean = jnp.sum(sum(parts), axis=1, keepdims=True) * (1.0 / TLEN)
             centred = [value - mean for value in parts]
             centred[-1] = jnp.where(block_lane < last, centred[-1], 0.0)
@@ -100,28 +111,9 @@
                 out_ref[
                     channel, place * own : (place + 1) * own, part * LANES : (part + 1) * LANES
                 ] = (centred[part] * factor).astype(jnp.bfloat16)
-        channel = jnp.minimum(step, channels - 1)
-        filled = step % 2
-        for which in range(PERIOD):
-            first, offset = divmod(which * TLEN, LANES)
-            pieces = []
-            for part in range(DEPTH_TILES):
-                begin = (first + part) * SUBLANES + channel
-                piece = flat[pl.ds(begin, groups, stride=PERIOD_TILES * SUBLANES), :]
-                if offset:
-                    piece = pltpu.roll(piece, LANES - offset, 1)
-                pieces.append(piece)
-            for part in range(DEPTH_TILES):
-                value = pieces[part]
-                if part + 1 < DEPTH_TILES:
-                    if offset:
-                        value = jnp.where(lane < LANES - offset, value, pieces[part + 1])
-                else:
-                    value = jnp.where(lane < last, value, 0.0)
-                rows[filled, part, pl.ds(which, groups, stride=PERIOD), :] = value
         return carry
 
-    lax.fori_loop(0, channels + 1, one_step, 0)
+    lax.fori_loop(0, channels, one_channel, 0, unroll=2)
 
 
 def weighted_templates(raw, available, usable, token, shares, stay):
@@ -142,8 +134,7 @@
         ],
         out_specs=[pl.BlockSpec(memory_space=pltpu.VMEM)] * len(outs),
         scratch_shapes=[
-            pltpu.VMEM((taken * TLEN // LANES * SUBLANES, LANES), jnp.float32),
-            pltpu.VMEM((2, DEPTH_TILES, taken, LANES), jnp.float32),
+            pltpu.VMEM((DEPTH_TILES, taken * SUBLANES, LANES), jnp.float32),
             pltpu.VMEM((channels // COMPONENTS + 1, count, LANES), jnp.float32),
         ],
         compiler_params=pltpu.CompilerParams(vmem_limit_bytes=VMEM_LIMIT),

time: 30.9 us -> 30.2 us (0.977)
  Pallas kernels: 14.1 us -> 12.2 us
  waiting for transfers between devices: 6.12 us -> 7.02 us
    pallas_call x2, Pallas kernels: 6.34 us -> 4.41 us  [weighted_templates(): pl.pallas_call(functools.partial(template_kernel, shares, stay), out_shap...]
    ppermute x10, waiting for transfers between devices: 6.12 us -> 7.02 us  [exchanged(): return lax.ppermute(array, axis, [(i, i ^ by) for i in range(length)])]
  transfers between devices with their start and end apart: 10 -> 10, of which waited for: 3 -> 3; matrix products, arithmetic and copies ran while one was open for 0% -> 0% of each run, Pallas kernels for 27% -> 21%
where the time goes in v5:
time: 30.2 us; the launch traced here: 29.9 us
  Pallas kernels  12.2 us (40%)
  starting transfers between devices  9.78 us (32%)
  waiting for transfers between devices  7.02 us (23%)
  local copies, waits for them, and re-layouts  0.68 us (2%)
    ppermute x10, starting transfers between devices, exchanged(): return lax.ppermute(array, axis, [(i, i ^ by) for i in range(length)])  9.78 us
    ppermute x10, waiting for transfers between devices, exchanged(): return lax.ppermute(array, axis, [(i, i ^ by) for i in range(length)])  7.02 us
    pallas_call x2, Pallas kernels, correlations(): pl.pallas_call(correlate_kernel, out_shape=[jax.ShapeDtypeStruct((count /...  4.49 us
    pallas_call x2, Pallas kernels, weighted_templates(): pl.pallas_call(functools.partial(template_kernel, shares, stay), out_shap...  4.41 us
    pallas_call x1, Pallas kernels, all_windows(): pl.pallas_call(functools.partial(windows_kernel, blocks), out_shape=(jax....  2.5 us
    pallas_call x1, Pallas kernels, scaled(): pl.pallas_call(scale_kernel, out_shape=jax.ShapeDtypeStruct(terms[0].shap...  0.73 us
    unnamed x8, local copies, waits for them, and re-layouts  0.68 us
  transfers between devices with their start and end apart: 10, of which 3 were waited for; matrix products, arithmetic and copies ran while one was open for 0% of the time, Pallas kernels for 21%

profile of v5, /device:TPU:17, one launch (start us, length us, event | category | flops | bytes accessed | tf_op | source)
XLA Modules:
  0.0 29.9 jit_solution(14225953901883145115)
XLA Ops:
  0.0 0.0 copy-start
  0.0 0.7 %copy-done.2 = bf16[6,512]{1,0:T(8,128)(2,1)S(1)} copy-done((bf16[6,512]{1,0:T(8,128)(2,1)S(1)}, bf16[6,512]{1,0:T(8,128)(2,1)}, u32[]{:S(2)}) %copy-start.2) | copy-done | bytes 6168
  0.7 2.2 %collective-permute-start.2 = (bf16[6,512]{1,0:T(8,128)(2,1)S(1)}, bf16[6,512]{1,0:T(8,128)(2,1)S(1)}, u32[]{:S(2)}, u32[]{:S(2)}) collective-permute-start(bf16[6,512]{1,0:T(8,128)(2,1)S(1)} %copy-done.2), channel_id=1, source_target_pairs={{0,24},{8,16},{16,8},{24,0},{1,25},{9,17},{17,9},{25,1},{2,26},{10... | collective-permute-start | bytes 18440 | tf_op jit(solution)/shard_map/ppermute | solution.py:28
  2.9 0.2 collective-permute-start.1
  3.1 0.3 collective-permute-start
  3.3 0.0 copy-done.3
  3.4 0.0 copy-done.1
  3.4 0.0 copy-done
  3.4 2.8 %templates_leaving.1.weighted_ref = bf16[6,192,512]{2,1,0:T(8,128)(2,1)S(1)} custom-call(bf16[6,102400]{1,0:T(8,128)(2,1)S(1)} %copy-done, s32[16,256]{1,0:T(8,128)S(1)} %copy-done.1, s32[48]{0:T(128)S(1)} %copy-done.3, f32[8,128]{1,0:T(8,128)S(1)} %first.1.token_ref), custom_call_target="tpu_custom_call" | custom-call | flops 1024 | bytes 1024 | tf_op jit(solution)/shard_map/templates_leaving/pallas_call | solution.py:126
  6.2 0.0 collective-permute-done.2.refs_3_
  6.2 0.0 collective-permute-done.1.refs_2_
  6.2 0.0 collective-permute-done.refs_1_
  6.2 2.5 %windows.1 = (bf16[6,128,2432]{2,1,0:T(8,128)(2,1)S(1)}, f32[8,2048]{1,0:T(8,128)S(1)}) custom-call(bf16[6,512]{1,0:T(8,128)(2,1)S(1)} %copy-done.2, bf16[6,512]{1,0:T(8,128)(2,1)S(1)} %collective-permute-done.refs_1_, bf16[6,512]{1,0:T(8,128)(2,1)S(1)} %collective-permute-done.1.refs_2_, bf16[6,512]{1,0:T(8,128)(2,1)S(1)} %collective-permute-done.2.refs_3_), custom_call_target="tpu_custom_call" | custom-call | flops 1024 | bytes 1024 | tf_op jit(solution)/shard_map/windows/pallas_call | solution.py:195
  8.7 2.6 %correlate_leaving.1 = (f32[32,2048]{1,0:T(8,128)S(1)}, f32[32,2048]{1,0:T(8,128)S(1)}, f32[32,2048]{1,0:T(8,128)S(1)}, bf16[32,2048]{1,0:T(8,128)(2,1)S(1)}, bf...) custom-call(bf16[6,192,512]{2,1,0:T(8,128)(2,1)S(1)} %templates_leaving.1.weighted_ref, ...), custom_call_target="tpu_custom_call" | custom-call | flops 1024 | bytes 1024 | tf_op jit(solution)/shard_map/correlate_leaving/pallas_call | solution.py:253
  11.4 1.8 %collective-permute-start.3 = (bf16[32,2048]{1,0:T(8,128)(2,1)S(1)}, bf16[32,2048]{1,0:T(8,128)(2,1)S(1)}, u32[]{:S(2)}, u32[]{:S(2)}) collective-permute-start(bf16[32,2048]{1,0:T(8,128)(2,1)S(1)} %get-tuple-element.33), channel_id=1, source_target_pairs={{0,1},{1,0},{2,3},{3,2},{4,5},{5,4},{6,7},{7,6},{8,9},{9,8},{10,11... | collective-permute-start | bytes 393224 | tf_op jit(solution)/shard_map/ppermute | solution.py:28
  13.2 0.1 collective-permute-start.4
  13.3 0.4 %collective-permute-start.5 = (bf16[32,2048]{1,0:T(8,128)(2,1)S(1)}, bf16[32,2048]{1,0:T(8,128)(2,1)S(1)}, u32[]{:S(2)}, u32[]{:S(2)}) collective-permute-start(bf16[32,2048]{1,0:T(8,128)(2,1)S(1)} %get-tuple-element.37), channel_id=1, source_target_pairs={{0,1},{1,0},{2,3},{3,2},{4,5},{5,4},{6,7},{7,6},{8,9},{9,8},{10,11... | collective-permute-start | bytes 393224 | tf_op jit(solution)/shard_map/ppermute | solution.py:28
  13.7 0.5 %collective-permute-done.3 = bf16[32,2048]{1,0:T(8,128)(2,1)S(1)} collective-permute-done((bf16[32,2048]{1,0:T(8,128)(2,1)S(1)}, bf16[32,2048]{1,0:T(8,128)(2,1)S(1)}, u32[]{:S(2)}, u32[]{:S(2)}) %collective-permute-start.3) | collective-permute-done | bytes 131104 | tf_op jit(solution)/shard_map/ppermute | solution.py:28
  14.2 0.1 collective-permute-start.6
  14.3 0.2 collective-permute-done.4
  14.6 2.3 %collective-permute-start.7 = (bf16[32,2048]{1,0:T(8,128)(2,1)S(1)}, bf16[32,2048]{1,0:T(8,128)(2,1)S(1)}, u32[]{:S(2)}, u32[]{:S(2)}) collective-permute-start(bf16[32,2048]{1,0:T(8,128)(2,1)S(1)} %add_convert_fusion.1), channel_id=1, source_target_pairs={{0,6},{1,7},{2,4},{3,5},{4,2},{5,3},{6,0},{7,1},{8,14},{9,15},{10,... | collective-permute-start | bytes 393224 | tf_op jit(solution)/shard_map/ppermute | solution.py:28
  16.9 0.0 collective-permute-done.5
  16.9 1.1 %collective-permute-start.8 = (bf16[32,2048]{1,0:T(8,128)(2,1)S(1)}, bf16[32,2048]{1,0:T(8,128)(2,1)S(1)}, u32[]{:S(2)}, u32[]{:S(2)}) collective-permute-start(bf16[32,2048]{1,0:T(8,128)(2,1)S(1)} %add_convert_fusion), channel_id=1, source_target_pairs={{0,2},{1,3},{2,0},{3,1},{4,6},{5,7},{6,4},{7,5},{8,10},{9,11},{10,... | collective-permute-start | bytes 393224 | tf_op jit(solution)/shard_map/ppermute | solution.py:28
  18.0 1.6 %templates_staying.1 = (bf16[6,64,512]{2,1,0:T(8,128)(2,1)S(1)}, f32[32,128]{1,0:T(8,128)S(1)}) custom-call(bf16[6,102400]{1,0:T(8,128)(2,1)S(1)} %copy-done, s32[16,256]{1,0:T(8,128)S(1)} %copy-done.1, s32[48]{0:T(128)S(1)} %copy-done.3, f32[8,128]{1,0:T(8,128)S(1)} %first.1.token_ref), custom_call_target="tpu_custom_call" | custom-call | flops 1024 | bytes 1024 | tf_op jit(solution)/shard_map/templates_staying/pallas_call | solution.py:126
  19.6 1.9 %correlate_staying.1 = (f32[32,2048]{1,0:T(8,128)S(1)}, bf16[32,2048]{1,0:T(8,128)(2,1)S(1)}) custom-call(bf16[6,64,512]{2,1,0:T(8,128)(2,1)S(1)} %get-tuple-element.40.weighted_ref, bf16[6,128,2432]{2,1,0:T(8,128)(2,1)S(1)} %get-tuple-element.28.windows, f32[8,2048]{1,0:T(8,128)S(1)} %get-tuple-element.41.scale), custom_call_target="tpu_custom_call" | custom-call | flops 1024 | bytes 1024 | tf_op jit(solution)/shard_map/correlate_staying/pallas_call | solution.py:253
  21.5 1.3 %collective-permute-start.9 = (bf16[32,2048]{1,0:T(8,128)(2,1)S(1)}, bf16[32,2048]{1,0:T(8,128)(2,1)S(1)}, u32[]{:S(2)}, u32[]{:S(2)}) collective-permute-start(bf16[32,2048]{1,0:T(8,128)(2,1)S(1)} %get-tuple-element.46), channel_id=1, source_target_pairs={{0,1},{1,0},{2,3},{3,2},{4,5},{5,4},{6,7},{7,6},{8,9},{9,8},{10,11... | collective-permute-start | bytes 393224 | tf_op jit(solution)/shard_map/ppermute | solution.py:28
  22.8 0.0 collective-permute-done.6.refs_1_
  22.8 6.3 %collective-permute-done.7.refs_2_ = bf16[32,2048]{1,0:T(8,128)(2,1)S(1)} collective-permute-done((bf16[32,2048]{1,0:T(8,128)(2,1)S(1)}, bf16[32,2048]{1,0:T(8,128)(2,1)S(1)}, u32[]{:S(2)}, u32[]{:S(2)}) %collective-permute-start.7) | collective-permute-done | bytes 131104 | tf_op jit(solution)/shard_map/ppermute | solution.py:28
  29.1 0.0 collective-permute-done.8.refs_3_
  29.1 0.1 added.1.refs_0_
  29.2 0.0 collective-permute-done.9.refs_1_
  29.2 0.7 %scaled.1 = f32[32,2048]{1,0:T(8,128)} custom-call(f32[32,128]{1,0:T(8,128)S(1)} %get-tuple-element.39.factor_ref, f32[32,2048]{1,0:T(8,128)S(1)} %added.1.refs_0_, bf16[32,2048]{1,0:T(8,128)(2,1)S(1)} %collective-permute-done.9.refs_1_), custom_call_target="tpu_custom_call" | custom-call | flops 1024 | bytes 1024 | tf_op jit(solution)/shard_map/scaled/pallas_call | solution.py:309
  (7 shorter events, 0.1 us)
Async XLA Ops:
  0.0 0.7 %copy-start.2 = (bf16[6,512]{1,0:T(8,128)(2,1)S(1)}, bf16[6,512]{1,0:T(8,128)(2,1)}, u32[]{:S(2)}) copy-start(bf16[6,512]{1,0:T(8,128)(2,1)} %refs_0_) | copy-start | bytes 18436
  0.0 3.3 %copy-start.3 = (s32[48]{0:T(128)S(1)}, s32[48]{0:T(128)}, u32[]{:S(2)}) copy-start(s32[48]{0:T(128)} %usable_ref.3) | copy-start | bytes 580
  0.0 3.3 %copy-start.1 = (s32[16,256]{1,0:T(8,128)S(1)}, s32[16,256]{1,0:T(8,128)}, u32[]{:S(2)}) copy-start(s32[16,256]{1,0:T(8,128)} %avail_ref.3) | copy-start | bytes 49156
  0.0 3.3 %copy-start = (bf16[6,102400]{1,0:T(8,128)(2,1)S(1)}, bf16[6,102400]{1,0:T(8,128)(2,1)}, u32[]{:S(2)}) copy-start(bf16[6,102400]{1,0:T(8,128)(2,1)} %raw_ref.3) | copy-start | bytes 3686404
  0.7 5.5 %collective-permute-start.2 = (bf16[6,512]{1,0:T(8,128)(2,1)S(1)}, bf16[6,512]{1,0:T(8,128)(2,1)S(1)}, u32[]{:S(2)}, u32[]{:S(2)}) collective-permute-start(bf16[6,512]{1,0:T(8,128)(2,1)S(1)} %copy-done.2), channel_id=1, source_target_pairs={{0,24},{8,16},{16,8},{24,0},{1,25},{9,17},{17,9},{25,1},{2,26},{10... | collective-permute-start | bytes 18440 | tf_op jit(solution)/shard_map/ppermute | solution.py:28
  2.9 3.3 %collective-permute-start.1 = (bf16[6,512]{1,0:T(8,128)(2,1)S(1)}, bf16[6,512]{1,0:T(8,128)(2,1)S(1)}, u32[]{:S(2)}, u32[]{:S(2)}) collective-permute-start(bf16[6,512]{1,0:T(8,128)(2,1)S(1)} %copy-done.2), channel_id=1, source_target_pairs={{0,16},{8,24},{16,0},{24,8},{1,17},{9,25},{17,1},{25,9},{2,18},{10... | collective-permute-start | bytes 18440 | tf_op jit(solution)/shard_map/ppermute | solution.py:28
  3.1 3.1 %collective-permute-start = (bf16[6,512]{1,0:T(8,128)(2,1)S(1)}, bf16[6,512]{1,0:T(8,128)(2,1)S(1)}, u32[]{:S(2)}, u32[]{:S(2)}) collective-permute-start(bf16[6,512]{1,0:T(8,128)(2,1)S(1)} %copy-done.2), channel_id=1, source_target_pairs={{0,8},{8,0},{16,24},{24,16},{1,9},{9,1},{17,25},{25,17},{2,10},{10... | collective-permute-start | bytes 18440 | tf_op jit(solution)/shard_map/ppermute | solution.py:28
  11.4 2.8 %collective-permute-start.3 = (bf16[32,2048]{1,0:T(8,128)(2,1)S(1)}, bf16[32,2048]{1,0:T(8,128)(2,1)S(1)}, u32[]{:S(2)}, u32[]{:S(2)}) collective-permute-start(bf16[32,2048]{1,0:T(8,128)(2,1)S(1)} %get-tuple-element.33), channel_id=1, source_target_pairs={{0,1},{1,0},{2,3},{3,2},{4,5},{5,4},{6,7},{7,6},{8,9},{9,8},{10,11... | collective-permute-start | bytes 393224 | tf_op jit(solution)/shard_map/ppermute | solution.py:28
  13.2 1.3 %collective-permute-start.4 = (bf16[32,2048]{1,0:T(8,128)(2,1)S(1)}, bf16[32,2048]{1,0:T(8,128)(2,1)S(1)}, u32[]{:S(2)}, u32[]{:S(2)}) collective-permute-start(bf16[32,2048]{1,0:T(8,128)(2,1)S(1)} %get-tuple-element.35), channel_id=1, source_target_pairs={{0,1},{1,0},{2,3},{3,2},{4,5},{5,4},{6,7},{7,6},{8,9},{9,8},{10,11... | collective-permute-start | bytes 393224 | tf_op jit(solution)/shard_map/ppermute | solution.py:28
  13.3 3.6 %collective-permute-start.5 = (bf16[32,2048]{1,0:T(8,128)(2,1)S(1)}, bf16[32,2048]{1,0:T(8,128)(2,1)S(1)}, u32[]{:S(2)}, u32[]{:S(2)}) collective-permute-start(bf16[32,2048]{1,0:T(8,128)(2,1)S(1)} %get-tuple-element.37), channel_id=1, source_target_pairs={{0,1},{1,0},{2,3},{3,2},{4,5},{5,4},{6,7},{7,6},{8,9},{9,8},{10,11... | collective-permute-start | bytes 393224 | tf_op jit(solution)/shard_map/ppermute | solution.py:28
  14.2 8.5 %collective-permute-start.6 = (bf16[32,2048]{1,0:T(8,128)(2,1)S(1)}, bf16[32,2048]{1,0:T(8,128)(2,1)S(1)}, u32[]{:S(2)}, u32[]{:S(2)}) collective-permute-start(bf16[32,2048]{1,0:T(8,128)(2,1)S(1)} %add_convert_fusion.2), channel_id=1, source_target_pairs={{0,4},{1,5},{2,6},{3,7},{4,0},{5,1},{6,2},{7,3},{8,12},{9,13},{10,... | collective-permute-start | bytes 393224 | tf_op jit(solution)/shard_map/ppermute | solution.py:28
  14.6 14.5 %collective-permute-start.7 = (bf16[32,2048]{1,0:T(8,128)(2,1)S(1)}, bf16[32,2048]{1,0:T(8,128)(2,1)S(1)}, u32[]{:S(2)}, u32[]{:S(2)}) collective-permute-start(bf16[32,2048]{1,0:T(8,128)(2,1)S(1)} %add_convert_fusion.1), channel_id=1, source_target_pairs={{0,6},{1,7},{2,4},{3,5},{4,2},{5,3},{6,0},{7,1},{8,14},{9,15},{10,... | collective-permute-start | bytes 393224 | tf_op jit(solution)/shard_map/ppermute | solution.py:28
  16.9 12.2 %collective-permute-start.8 = (bf16[32,2048]{1,0:T(8,128)(2,1)S(1)}, bf16[32,2048]{1,0:T(8,128)(2,1)S(1)}, u32[]{:S(2)}, u32[]{:S(2)}) collective-permute-start(bf16[32,2048]{1,0:T(8,128)(2,1)S(1)} %add_convert_fusion), channel_id=1, source_target_pairs={{0,2},{1,3},{2,0},{3,1},{4,6},{5,7},{6,4},{7,5},{8,10},{9,11},{10,... | collective-permute-start | bytes 393224 | tf_op jit(solution)/shard_map/ppermute | solution.py:28
  21.5 7.7 %collective-permute-start.9 = (bf16[32,2048]{1,0:T(8,128)(2,1)S(1)}, bf16[32,2048]{1,0:T(8,128)(2,1)S(1)}, u32[]{:S(2)}, u32[]{:S(2)}) collective-permute-start(bf16[32,2048]{1,0:T(8,128)(2,1)S(1)} %get-tuple-element.46), channel_id=1, source_target_pairs={{0,1},{1,0},{2,3},{3,2},{4,5},{5,4},{6,7},{7,6},{8,9},{9,8},{10,11... | collective-permute-start | bytes 393224 | tf_op jit(solution)/shard_map/ppermute | solution.py:28

commit v6 on v5

--- a/solution.py
+++ b/solution.py
@@ -149,7 +149,7 @@
 
 def windows_kernel(blocks, *refs):
     segments = refs[:blocks]
-    windows, scale, record = refs[blocks:]
+    windows, scale, record, starts = refs[blocks:]
     channels, segment = segments[0].shape
     lags = blocks * segment
     wide = record.shape[1]
@@ -161,31 +161,36 @@
         start = pl.multiple_of((me ^ by) * segment, LANES)
         record[0:channels, pl.ds(start, segment)] = segments[by][...].astype(jnp.float32)
 
-    power = record[...] * record[...]
-    energy, taken, span = None, 0, 1
-    while True:
-        if TLEN & span:
-            term = ahead(power, taken)
+    sums = {1: record[...] * record[...]}
+    span = 1
+    while 2 * span <= TLEN:
+        sums[2 * span] = sums[span] + ahead(sums[span], span)
+        span *= 2
+    energy, taken = None, 0
+    while taken < TLEN:
+        if taken + span <= TLEN:
+            term = sums[span][:, taken : taken + lags]
             energy = term if energy is None else energy + term
             taken += span
-        if 2 * span > TLEN:
-            break
-        power = power + ahead(power, span)
-        span *= 2
-    scale[...] = lax.rsqrt(jnp.maximum(energy[:, :lags], FLOOR_SHARE * TLEN))
+        span //= 2
+    scale[...] = lax.rsqrt(jnp.maximum(energy, FLOOR_SHARE * TLEN))
 
     sublane = lax.broadcasted_iota(jnp.int32, (SUBLANES, wide), 0)
-
-    def one_record(channel, carry):
-        shifted = jnp.broadcast_to(record[pl.ds(channel, 1), :], (SUBLANES, wide))
+    for channel in range(channels):
+        shifted = jnp.broadcast_to(record[channel : channel + 1, :], (SUBLANES, wide))
         for bit in (1, 2, 4):
             shifted = jnp.where((sublane & bit) != 0, ahead(shifted, bit), shifted)
         pair = jnp.concatenate([shifted, ahead(shifted, SUBLANES)], axis=0).astype(jnp.bfloat16)
-        for row in range(0, LANES, 2 * SUBLANES):
+        starts[channel] = pair
+        windows[channel, : 2 * SUBLANES, :] = pair[:, :base]
+
+    def one_channel(channel, carry):
+        pair = starts[channel]
+        for row in range(2 * SUBLANES, LANES, 2 * SUBLANES):
             windows[channel, row : row + 2 * SUBLANES, :] = pair[:, row : row + base]
         return carry
 
-    lax.fori_loop(0, channels, one_record, 0, unroll=2)
+    lax.fori_loop(0, channels, one_channel, 0, unroll=3)
 
 
 def all_windows(segments, name):
@@ -200,7 +205,10 @@
         ),
         in_specs=[pl.BlockSpec(memory_space=pltpu.VMEM)] * blocks,
         out_specs=(pl.BlockSpec(memory_space=pltpu.VMEM),) * 2,
-        scratch_shapes=[pltpu.VMEM((SUBLANES, lags + DEPTH), jnp.float32)],
+        scratch_shapes=[
+            pltpu.VMEM((SUBLANES, lags + DEPTH), jnp.float32),
+            pltpu.VMEM((channels, 2 * SUBLANES, lags + DEPTH), jnp.bfloat16),
+        ],
         compiler_params=pltpu.CompilerParams(vmem_limit_bytes=VMEM_LIMIT),
         cost_estimate=pl.CostEstimate(flops=1 << 10, transcendentals=0, bytes_accessed=1 << 10),
         name=name,

time: 30.2 us -> 29.8 us (0.987)
  Pallas kernels: 12.2 us -> 11.8 us
    pallas_call x1, Pallas kernels: 2.5 us -> 2.06 us  [all_windows(): pl.pallas_call(functools.partial(windows_kernel, blocks), out_shape=(jax....]
  transfers between devices with their start and end apart: 10 -> 10, of which waited for: 3 -> 3; matrix products, arithmetic and copies ran while one was open for 0% -> 0% of each run, Pallas kernels for 21% -> 22%
where the time goes in v6:
time: 29.8 us; the launch traced here: 29.4 us
  Pallas kernels  11.8 us (40%)
  starting transfers between devices  9.78 us (33%)
  waiting for transfers between devices  7.02 us (24%)
  local copies, waits for them, and re-layouts  0.68 us (2%)
    ppermute x10, starting transfers between devices, exchanged(): return lax.ppermute(array, axis, [(i, i ^ by) for i in range(length)])  9.78 us
    ppermute x10, waiting for transfers between devices, exchanged(): return lax.ppermute(array, axis, [(i, i ^ by) for i in range(length)])  7.02 us
    pallas_call x2, Pallas kernels, correlations(): pl.pallas_call(correlate_kernel, out_shape=[jax.ShapeDtypeStruct((count /...  4.49 us
    pallas_call x2, Pallas kernels, weighted_templates(): pl.pallas_call(functools.partial(template_kernel, shares, stay), out_shap...  4.41 us
    pallas_call x1, Pallas kernels, all_windows(): pl.pallas_call(functools.partial(windows_kernel, blocks), out_shape=(jax....  2.06 us
    pallas_call x1, Pallas kernels, scaled(): pl.pallas_call(scale_kernel, out_shape=jax.ShapeDtypeStruct(terms[0].shap...  0.73 us
    unnamed x8, local copies, waits for them, and re-layouts  0.68 us
  transfers between devices with their start and end apart: 10, of which 3 were waited for; matrix products, arithmetic and copies ran while one was open for 0% of the time, Pallas kernels for 22%

profile of v6, /device:TPU:17, one launch (start us, length us, event | category | flops | bytes accessed | tf_op | source)
XLA Modules:
  0.0 29.4 jit_solution(13973216157377094583)
XLA Ops:
  0.0 0.0 copy-start
  0.0 0.7 %copy-done.2 = bf16[6,512]{1,0:T(8,128)(2,1)S(1)} copy-done((bf16[6,512]{1,0:T(8,128)(2,1)S(1)}, bf16[6,512]{1,0:T(8,128)(2,1)}, u32[]{:S(2)}) %copy-start.2) | copy-done | bytes 6168
  0.7 2.2 %collective-permute-start.2 = (bf16[6,512]{1,0:T(8,128)(2,1)S(1)}, bf16[6,512]{1,0:T(8,128)(2,1)S(1)}, u32[]{:S(2)}, u32[]{:S(2)}) collective-permute-start(bf16[6,512]{1,0:T(8,128)(2,1)S(1)} %copy-done.2), channel_id=1, source_target_pairs={{0,24},{8,16},{16,8},{24,0},{1,25},{9,17},{17,9},{25,1},{2,26},{10... | collective-permute-start | bytes 18440 | tf_op jit(solution)/shard_map/ppermute | solution.py:28
  2.9 0.2 collective-permute-start.1
  3.1 0.3 collective-permute-start
  3.3 0.0 copy-done.3
  3.4 0.0 copy-done.1
  3.4 0.0 copy-done
  3.4 2.8 %templates_leaving.1.weighted_ref = bf16[6,192,512]{2,1,0:T(8,128)(2,1)S(1)} custom-call(bf16[6,102400]{1,0:T(8,128)(2,1)S(1)} %copy-done, s32[16,256]{1,0:T(8,128)S(1)} %copy-done.1, s32[48]{0:T(128)S(1)} %copy-done.3, f32[8,128]{1,0:T(8,128)S(1)} %first.1.token_ref), custom_call_target="tpu_custom_call" | custom-call | flops 1024 | bytes 1024 | tf_op jit(solution)/shard_map/templates_leaving/pallas_call | solution.py:126
  6.2 0.0 collective-permute-done.2.refs_3_
  6.2 0.0 collective-permute-done.1.refs_2_
  6.2 0.0 collective-permute-done.refs_1_
  6.2 2.1 %windows.1 = (bf16[6,128,2432]{2,1,0:T(8,128)(2,1)S(1)}, f32[8,2048]{1,0:T(8,128)S(1)}) custom-call(bf16[6,512]{1,0:T(8,128)(2,1)S(1)} %copy-done.2, bf16[6,512]{1,0:T(8,128)(2,1)S(1)} %collective-permute-done.refs_1_, bf16[6,512]{1,0:T(8,128)(2,1)S(1)} %collective-permute-done.1.refs_2_, bf16[6,512]{1,0:T(8,128)(2,1)S(1)} %collective-permute-done.2.refs_3_), custom_call_target="tpu_custom_call" | custom-call | flops 1024 | bytes 1024 | tf_op jit(solution)/shard_map/windows/pallas_call | solution.py:200
  8.3 2.6 %correlate_leaving.1 = (f32[32,2048]{1,0:T(8,128)S(1)}, f32[32,2048]{1,0:T(8,128)S(1)}, f32[32,2048]{1,0:T(8,128)S(1)}, bf16[32,2048]{1,0:T(8,128)(2,1)S(1)}, bf...) custom-call(bf16[6,192,512]{2,1,0:T(8,128)(2,1)S(1)} %templates_leaving.1.weighted_ref, ...), custom_call_target="tpu_custom_call" | custom-call | flops 1024 | bytes 1024 | tf_op jit(solution)/shard_map/correlate_leaving/pallas_call | solution.py:261
  10.9 1.8 %collective-permute-start.3 = (bf16[32,2048]{1,0:T(8,128)(2,1)S(1)}, bf16[32,2048]{1,0:T(8,128)(2,1)S(1)}, u32[]{:S(2)}, u32[]{:S(2)}) collective-permute-start(bf16[32,2048]{1,0:T(8,128)(2,1)S(1)} %get-tuple-element.33), channel_id=1, source_target_pairs={{0,1},{1,0},{2,3},{3,2},{4,5},{5,4},{6,7},{7,6},{8,9},{9,8},{10,11... | collective-permute-start | bytes 393224 | tf_op jit(solution)/shard_map/ppermute | solution.py:28
  12.7 0.1 collective-permute-start.4
  12.8 0.4 %collective-permute-start.5 = (bf16[32,2048]{1,0:T(8,128)(2,1)S(1)}, bf16[32,2048]{1,0:T(8,128)(2,1)S(1)}, u32[]{:S(2)}, u32[]{:S(2)}) collective-permute-start(bf16[32,2048]{1,0:T(8,128)(2,1)S(1)} %get-tuple-element.37), channel_id=1, source_target_pairs={{0,1},{1,0},{2,3},{3,2},{4,5},{5,4},{6,7},{7,6},{8,9},{9,8},{10,11... | collective-permute-start | bytes 393224 | tf_op jit(solution)/shard_map/ppermute | solution.py:28
  13.2 0.5 %collective-permute-done.3 = bf16[32,2048]{1,0:T(8,128)(2,1)S(1)} collective-permute-done((bf16[32,2048]{1,0:T(8,128)(2,1)S(1)}, bf16[32,2048]{1,0:T(8,128)(2,1)S(1)}, u32[]{:S(2)}, u32[]{:S(2)}) %collective-permute-start.3) | collective-permute-done | bytes 131104 | tf_op jit(solution)/shard_map/ppermute | solution.py:28
  13.8 0.1 collective-permute-start.6
  13.9 0.2 collective-permute-done.4
  14.1 2.3 %collective-permute-start.7 = (bf16[32,2048]{1,0:T(8,128)(2,1)S(1)}, bf16[32,2048]{1,0:T(8,128)(2,1)S(1)}, u32[]{:S(2)}, u32[]{:S(2)}) collective-permute-start(bf16[32,2048]{1,0:T(8,128)(2,1)S(1)} %add_convert_fusion.1), channel_id=1, source_target_pairs={{0,6},{1,7},{2,4},{3,5},{4,2},{5,3},{6,0},{7,1},{8,14},{9,15},{10,... | collective-permute-start | bytes 393224 | tf_op jit(solution)/shard_map/ppermute | solution.py:28
  16.4 0.0 collective-permute-done.5
  16.4 1.1 %collective-permute-start.8 = (bf16[32,2048]{1,0:T(8,128)(2,1)S(1)}, bf16[32,2048]{1,0:T(8,128)(2,1)S(1)}, u32[]{:S(2)}, u32[]{:S(2)}) collective-permute-start(bf16[32,2048]{1,0:T(8,128)(2,1)S(1)} %add_convert_fusion), channel_id=1, source_target_pairs={{0,2},{1,3},{2,0},{3,1},{4,6},{5,7},{6,4},{7,5},{8,10},{9,11},{10,... | collective-permute-start | bytes 393224 | tf_op jit(solution)/shard_map/ppermute | solution.py:28
  17.6 1.6 %templates_staying.1 = (bf16[6,64,512]{2,1,0:T(8,128)(2,1)S(1)}, f32[32,128]{1,0:T(8,128)S(1)}) custom-call(bf16[6,102400]{1,0:T(8,128)(2,1)S(1)} %copy-done, s32[16,256]{1,0:T(8,128)S(1)} %copy-done.1, s32[48]{0:T(128)S(1)} %copy-done.3, f32[8,128]{1,0:T(8,128)S(1)} %first.1.token_ref), custom_call_target="tpu_custom_call" | custom-call | flops 1024 | bytes 1024 | tf_op jit(solution)/shard_map/templates_staying/pallas_call | solution.py:126
  19.2 1.9 %correlate_staying.1 = (f32[32,2048]{1,0:T(8,128)S(1)}, bf16[32,2048]{1,0:T(8,128)(2,1)S(1)}) custom-call(bf16[6,64,512]{2,1,0:T(8,128)(2,1)S(1)} %get-tuple-element.40.weighted_ref, bf16[6,128,2432]{2,1,0:T(8,128)(2,1)S(1)} %get-tuple-element.28.windows, f32[8,2048]{1,0:T(8,128)S(1)} %get-tuple-element.41.scale), custom_call_target="tpu_custom_call" | custom-call | flops 1024 | bytes 1024 | tf_op jit(solution)/shard_map/correlate_staying/pallas_call | solution.py:261
  21.0 1.3 %collective-permute-start.9 = (bf16[32,2048]{1,0:T(8,128)(2,1)S(1)}, bf16[32,2048]{1,0:T(8,128)(2,1)S(1)}, u32[]{:S(2)}, u32[]{:S(2)}) collective-permute-start(bf16[32,2048]{1,0:T(8,128)(2,1)S(1)} %get-tuple-element.46), channel_id=1, source_target_pairs={{0,1},{1,0},{2,3},{3,2},{4,5},{5,4},{6,7},{7,6},{8,9},{9,8},{10,11... | collective-permute-start | bytes 393224 | tf_op jit(solution)/shard_map/ppermute | solution.py:28
  22.3 0.0 collective-permute-done.6.refs_1_
  22.3 6.3 %collective-permute-done.7.refs_2_ = bf16[32,2048]{1,0:T(8,128)(2,1)S(1)} collective-permute-done((bf16[32,2048]{1,0:T(8,128)(2,1)S(1)}, bf16[32,2048]{1,0:T(8,128)(2,1)S(1)}, u32[]{:S(2)}, u32[]{:S(2)}) %collective-permute-start.7) | collective-permute-done | bytes 131104 | tf_op jit(solution)/shard_map/ppermute | solution.py:28
  28.6 0.0 collective-permute-done.8.refs_3_
  28.6 0.1 added.1.refs_0_
  28.7 0.0 collective-permute-done.9.refs_1_
  28.7 0.7 %scaled.1 = f32[32,2048]{1,0:T(8,128)} custom-call(f32[32,128]{1,0:T(8,128)S(1)} %get-tuple-element.39.factor_ref, f32[32,2048]{1,0:T(8,128)S(1)} %added.1.refs_0_, bf16[32,2048]{1,0:T(8,128)(2,1)S(1)} %collective-permute-done.9.refs_1_), custom_call_target="tpu_custom_call" | custom-call | flops 1024 | bytes 1024 | tf_op jit(solution)/shard_map/scaled/pallas_call | solution.py:317
  (7 shorter events, 0.1 us)
Async XLA Ops:
  0.0 0.7 %copy-start.2 = (bf16[6,512]{1,0:T(8,128)(2,1)S(1)}, bf16[6,512]{1,0:T(8,128)(2,1)}, u32[]{:S(2)}) copy-start(bf16[6,512]{1,0:T(8,128)(2,1)} %refs_0_) | copy-start | bytes 18436
  0.0 3.3 %copy-start.3 = (s32[48]{0:T(128)S(1)}, s32[48]{0:T(128)}, u32[]{:S(2)}) copy-start(s32[48]{0:T(128)} %usable_ref.3) | copy-start | bytes 580
  0.0 3.3 %copy-start.1 = (s32[16,256]{1,0:T(8,128)S(1)}, s32[16,256]{1,0:T(8,128)}, u32[]{:S(2)}) copy-start(s32[16,256]{1,0:T(8,128)} %avail_ref.3) | copy-start | bytes 49156
  0.0 3.3 %copy-start = (bf16[6,102400]{1,0:T(8,128)(2,1)S(1)}, bf16[6,102400]{1,0:T(8,128)(2,1)}, u32[]{:S(2)}) copy-start(bf16[6,102400]{1,0:T(8,128)(2,1)} %raw_ref.3) | copy-start | bytes 3686404
  0.7 5.5 %collective-permute-start.2 = (bf16[6,512]{1,0:T(8,128)(2,1)S(1)}, bf16[6,512]{1,0:T(8,128)(2,1)S(1)}, u32[]{:S(2)}, u32[]{:S(2)}) collective-permute-start(bf16[6,512]{1,0:T(8,128)(2,1)S(1)} %copy-done.2), channel_id=1, source_target_pairs={{0,24},{8,16},{16,8},{24,0},{1,25},{9,17},{17,9},{25,1},{2,26},{10... | collective-permute-start | bytes 18440 | tf_op jit(solution)/shard_map/ppermute | solution.py:28
  2.9 3.3 %collective-permute-start.1 = (bf16[6,512]{1,0:T(8,128)(2,1)S(1)}, bf16[6,512]{1,0:T(8,128)(2,1)S(1)}, u32[]{:S(2)}, u32[]{:S(2)}) collective-permute-start(bf16[6,512]{1,0:T(8,128)(2,1)S(1)} %copy-done.2), channel_id=1, source_target_pairs={{0,16},{8,24},{16,0},{24,8},{1,17},{9,25},{17,1},{25,9},{2,18},{10... | collective-permute-start | bytes 18440 | tf_op jit(solution)/shard_map/ppermute | solution.py:28
  3.1 3.1 %collective-permute-start = (bf16[6,512]{1,0:T(8,128)(2,1)S(1)}, bf16[6,512]{1,0:T(8,128)(2,1)S(1)}, u32[]{:S(2)}, u32[]{:S(2)}) collective-permute-start(bf16[6,512]{1,0:T(8,128)(2,1)S(1)} %copy-done.2), channel_id=1, source_target_pairs={{0,8},{8,0},{16,24},{24,16},{1,9},{9,1},{17,25},{25,17},{2,10},{10... | collective-permute-start | bytes 18440 | tf_op jit(solution)/shard_map/ppermute | solution.py:28
  10.9 2.8 %collective-permute-start.3 = (bf16[32,2048]{1,0:T(8,128)(2,1)S(1)}, bf16[32,2048]{1,0:T(8,128)(2,1)S(1)}, u32[]{:S(2)}, u32[]{:S(2)}) collective-permute-start(bf16[32,2048]{1,0:T(8,128)(2,1)S(1)} %get-tuple-element.33), channel_id=1, source_target_pairs={{0,1},{1,0},{2,3},{3,2},{4,5},{5,4},{6,7},{7,6},{8,9},{9,8},{10,11... | collective-permute-start | bytes 393224 | tf_op jit(solution)/shard_map/ppermute | solution.py:28
  12.7 1.3 %collective-permute-start.4 = (bf16[32,2048]{1,0:T(8,128)(2,1)S(1)}, bf16[32,2048]{1,0:T(8,128)(2,1)S(1)}, u32[]{:S(2)}, u32[]{:S(2)}) collective-permute-start(bf16[32,2048]{1,0:T(8,128)(2,1)S(1)} %get-tuple-element.35), channel_id=1, source_target_pairs={{0,1},{1,0},{2,3},{3,2},{4,5},{5,4},{6,7},{7,6},{8,9},{9,8},{10,11... | collective-permute-start | bytes 393224 | tf_op jit(solution)/shard_map/ppermute | solution.py:28
  12.8 3.6 %collective-permute-start.5 = (bf16[32,2048]{1,0:T(8,128)(2,1)S(1)}, bf16[32,2048]{1,0:T(8,128)(2,1)S(1)}, u32[]{:S(2)}, u32[]{:S(2)}) collective-permute-start(bf16[32,2048]{1,0:T(8,128)(2,1)S(1)} %get-tuple-element.37), channel_id=1, source_target_pairs={{0,1},{1,0},{2,3},{3,2},{4,5},{5,4},{6,7},{7,6},{8,9},{9,8},{10,11... | collective-permute-start | bytes 393224 | tf_op jit(solution)/shard_map/ppermute | solution.py:28
  13.8 8.5 %collective-permute-start.6 = (bf16[32,2048]{1,0:T(8,128)(2,1)S(1)}, bf16[32,2048]{1,0:T(8,128)(2,1)S(1)}, u32[]{:S(2)}, u32[]{:S(2)}) collective-permute-start(bf16[32,2048]{1,0:T(8,128)(2,1)S(1)} %add_convert_fusion.2), channel_id=1, source_target_pairs={{0,4},{1,5},{2,6},{3,7},{4,0},{5,1},{6,2},{7,3},{8,12},{9,13},{10,... | collective-permute-start | bytes 393224 | tf_op jit(solution)/shard_map/ppermute | solution.py:28
  14.1 14.5 %collective-permute-start.7 = (bf16[32,2048]{1,0:T(8,128)(2,1)S(1)}, bf16[32,2048]{1,0:T(8,128)(2,1)S(1)}, u32[]{:S(2)}, u32[]{:S(2)}) collective-permute-start(bf16[32,2048]{1,0:T(8,128)(2,1)S(1)} %add_convert_fusion.1), channel_id=1, source_target_pairs={{0,6},{1,7},{2,4},{3,5},{4,2},{5,3},{6,0},{7,1},{8,14},{9,15},{10,... | collective-permute-start | bytes 393224 | tf_op jit(solution)/shard_map/ppermute | solution.py:28
  16.4 12.2 %collective-permute-start.8 = (bf16[32,2048]{1,0:T(8,128)(2,1)S(1)}, bf16[32,2048]{1,0:T(8,128)(2,1)S(1)}, u32[]{:S(2)}, u32[]{:S(2)}) collective-permute-start(bf16[32,2048]{1,0:T(8,128)(2,1)S(1)} %add_convert_fusion), channel_id=1, source_target_pairs={{0,2},{1,3},{2,0},{3,1},{4,6},{5,7},{6,4},{7,5},{8,10},{9,11},{10,... | collective-permute-start | bytes 393224 | tf_op jit(solution)/shard_map/ppermute | solution.py:28
  21.0 7.7 %collective-permute-start.9 = (bf16[32,2048]{1,0:T(8,128)(2,1)S(1)}, bf16[32,2048]{1,0:T(8,128)(2,1)S(1)}, u32[]{:S(2)}, u32[]{:S(2)}) collective-permute-start(bf16[32,2048]{1,0:T(8,128)(2,1)S(1)} %get-tuple-element.46), channel_id=1, source_target_pairs={{0,1},{1,0},{2,3},{3,2},{4,5},{5,4},{6,7},{7,6},{8,9},{9,8},{10,11... | collective-permute-start | bytes 393224 | tf_op jit(solution)/shard_map/ppermute | solution.py:28

commit v7 on v6

--- a/solution.py
+++ b/solution.py
@@ -340,7 +340,7 @@
     (weighted,) = weighted_templates(templates, available, usable, token, shares, False)
     windows, scale = all_windows(segments, "windows")
     sums = correlations(weighted, windows, scale, 2 * (chips - 1), "correlate_leaving")
-    order = sorted(range(1, chips), key=lambda by: -(by ^ (by >> 1)))
+    order = sorted(range(1, chips), key=lambda by: (by != chips // 2, by))
     partner = {by: exchanged(sums[chips - 1 + by - 1], "sta", 1) for by in order}
     sent = []
     for by in order:

time: 29.8 us -> 29.6 us (level)
  starting transfers between devices: 9.78 us -> 8.89 us
  waiting for transfers between devices: 7.02 us -> 7.87 us
    ppermute x10, starting transfers between devices: 9.78 us -> 8.89 us  [exchanged(): return lax.ppermute(array, axis, [(i, i ^ by) for i in range(length)])]
    ppermute x10, waiting for transfers between devices: 7.02 us -> 7.87 us  [exchanged(): return lax.ppermute(array, axis, [(i, i ^ by) for i in range(length)])]
where the time goes in v7:
time: 29.6 us; the launch traced here: 29.4 us
  Pallas kernels  11.8 us (40%)
  starting transfers between devices  8.89 us (30%)
  waiting for transfers between devices  7.87 us (27%)
  local copies, waits for them, and re-layouts  0.68 us (2%)
    ppermute x10, starting transfers between devices, exchanged(): return lax.ppermute(array, axis, [(i, i ^ by) for i in range(length)])  8.89 us
    ppermute x10, waiting for transfers between devices, exchanged(): return lax.ppermute(array, axis, [(i, i ^ by) for i in range(length)])  7.87 us
    pallas_call x2, Pallas kernels, correlations(): pl.pallas_call(correlate_kernel, out_shape=[jax.ShapeDtypeStruct((count /...  4.48 us
    pallas_call x2, Pallas kernels, weighted_templates(): pl.pallas_call(functools.partial(template_kernel, shares, stay), out_shap...  4.41 us
    pallas_call x1, Pallas kernels, all_windows(): pl.pallas_call(functools.partial(windows_kernel, blocks), out_shape=(jax....  2.06 us
    pallas_call x1, Pallas kernels, scaled(): pl.pallas_call(scale_kernel, out_shape=jax.ShapeDtypeStruct(terms[0].shap...  0.73 us
    unnamed x8, local copies, waits for them, and re-layouts  0.68 us
  transfers between devices with their start and end apart: 10, of which 3 were waited for; matrix products, arithmetic and copies ran while one was open for 0% of the time, Pallas kernels for 22%

profile of v7, /device:TPU:17, one launch (start us, length us, event | category | flops | bytes accessed | tf_op | source)
XLA Modules:
  0.0 29.4 jit_solution(1480014301210056858)
XLA Ops:
  0.0 0.0 copy-start
  0.0 0.7 %copy-done.2 = bf16[6,512]{1,0:T(8,128)(2,1)S(1)} copy-done((bf16[6,512]{1,0:T(8,128)(2,1)S(1)}, bf16[6,512]{1,0:T(8,128)(2,1)}, u32[]{:S(2)}) %copy-start.2) | copy-done | bytes 6168
  0.7 2.2 %collective-permute-start.2 = (bf16[6,512]{1,0:T(8,128)(2,1)S(1)}, bf16[6,512]{1,0:T(8,128)(2,1)S(1)}, u32[]{:S(2)}, u32[]{:S(2)}) collective-permute-start(bf16[6,512]{1,0:T(8,128)(2,1)S(1)} %copy-done.2), channel_id=1, source_target_pairs={{0,24},{8,16},{16,8},{24,0},{1,25},{9,17},{17,9},{25,1},{2,26},{10... | collective-permute-start | bytes 18440 | tf_op jit(solution)/shard_map/ppermute | solution.py:28
  2.9 0.2 collective-permute-start.1
  3.1 0.3 collective-permute-start
  3.3 0.0 copy-done.3
  3.4 0.0 copy-done.1
  3.4 0.0 copy-done
  3.4 2.8 %templates_leaving.1.weighted_ref = bf16[6,192,512]{2,1,0:T(8,128)(2,1)S(1)} custom-call(bf16[6,102400]{1,0:T(8,128)(2,1)S(1)} %copy-done, s32[16,256]{1,0:T(8,128)S(1)} %copy-done.1, s32[48]{0:T(128)S(1)} %copy-done.3, f32[8,128]{1,0:T(8,128)S(1)} %first.1.token_ref), custom_call_target="tpu_custom_call" | custom-call | flops 1024 | bytes 1024 | tf_op jit(solution)/shard_map/templates_leaving/pallas_call | solution.py:126
  6.2 0.0 collective-permute-done.2.refs_3_
  6.2 0.0 collective-permute-done.1.refs_2_
  6.2 0.0 collective-permute-done.refs_1_
  6.2 2.1 %windows.1 = (bf16[6,128,2432]{2,1,0:T(8,128)(2,1)S(1)}, f32[8,2048]{1,0:T(8,128)S(1)}) custom-call(bf16[6,512]{1,0:T(8,128)(2,1)S(1)} %copy-done.2, bf16[6,512]{1,0:T(8,128)(2,1)S(1)} %collective-permute-done.refs_1_, bf16[6,512]{1,0:T(8,128)(2,1)S(1)} %collective-permute-done.1.refs_2_, bf16[6,512]{1,0:T(8,128)(2,1)S(1)} %collective-permute-done.2.refs_3_), custom_call_target="tpu_custom_call" | custom-call | flops 1024 | bytes 1024 | tf_op jit(solution)/shard_map/windows/pallas_call | solution.py:200
  8.3 2.6 %correlate_leaving.1 = (f32[32,2048]{1,0:T(8,128)S(1)}, f32[32,2048]{1,0:T(8,128)S(1)}, f32[32,2048]{1,0:T(8,128)S(1)}, bf16[32,2048]{1,0:T(8,128)(2,1)S(1)}, bf...) custom-call(bf16[6,192,512]{2,1,0:T(8,128)(2,1)S(1)} %templates_leaving.1.weighted_ref, ...), custom_call_target="tpu_custom_call" | custom-call | flops 1024 | bytes 1024 | tf_op jit(solution)/shard_map/correlate_leaving/pallas_call | solution.py:261
  10.9 1.8 %collective-permute-start.3 = (bf16[32,2048]{1,0:T(8,128)(2,1)S(1)}, bf16[32,2048]{1,0:T(8,128)(2,1)S(1)}, u32[]{:S(2)}, u32[]{:S(2)}) collective-permute-start(bf16[32,2048]{1,0:T(8,128)(2,1)S(1)} %get-tuple-element.33), channel_id=1, source_target_pairs={{0,1},{1,0},{2,3},{3,2},{4,5},{5,4},{6,7},{7,6},{8,9},{9,8},{10,11... | collective-permute-start | bytes 393224 | tf_op jit(solution)/shard_map/ppermute | solution.py:28
  12.7 0.1 collective-permute-start.4
  12.8 0.4 %collective-permute-start.5 = (bf16[32,2048]{1,0:T(8,128)(2,1)S(1)}, bf16[32,2048]{1,0:T(8,128)(2,1)S(1)}, u32[]{:S(2)}, u32[]{:S(2)}) collective-permute-start(bf16[32,2048]{1,0:T(8,128)(2,1)S(1)} %get-tuple-element.37), channel_id=1, source_target_pairs={{0,1},{1,0},{2,3},{3,2},{4,5},{5,4},{6,7},{7,6},{8,9},{9,8},{10,11... | collective-permute-start | bytes 393224 | tf_op jit(solution)/shard_map/ppermute | solution.py:28
  13.2 0.5 %collective-permute-done.3 = bf16[32,2048]{1,0:T(8,128)(2,1)S(1)} collective-permute-done((bf16[32,2048]{1,0:T(8,128)(2,1)S(1)}, bf16[32,2048]{1,0:T(8,128)(2,1)S(1)}, u32[]{:S(2)}, u32[]{:S(2)}) %collective-permute-start.3) | collective-permute-done | bytes 131104 | tf_op jit(solution)/shard_map/ppermute | solution.py:28
  13.8 0.1 collective-permute-start.6
  13.9 0.2 collective-permute-done.4
  14.1 1.4 %collective-permute-start.7 = (bf16[32,2048]{1,0:T(8,128)(2,1)S(1)}, bf16[32,2048]{1,0:T(8,128)(2,1)S(1)}, u32[]{:S(2)}, u32[]{:S(2)}) collective-permute-start(bf16[32,2048]{1,0:T(8,128)(2,1)S(1)} %add_convert_fusion.1), channel_id=1, source_target_pairs={{0,2},{1,3},{2,0},{3,1},{4,6},{5,7},{6,4},{7,5},{8,10},{9,11},{10,... | collective-permute-start | bytes 393224 | tf_op jit(solution)/shard_map/ppermute | solution.py:28
  15.5 0.0 collective-permute-done.5
  15.5 1.2 %collective-permute-start.8 = (bf16[32,2048]{1,0:T(8,128)(2,1)S(1)}, bf16[32,2048]{1,0:T(8,128)(2,1)S(1)}, u32[]{:S(2)}, u32[]{:S(2)}) collective-permute-start(bf16[32,2048]{1,0:T(8,128)(2,1)S(1)} %add_convert_fusion), channel_id=1, source_target_pairs={{0,6},{1,7},{2,4},{3,5},{4,2},{5,3},{6,0},{7,1},{8,14},{9,15},{10,... | collective-permute-start | bytes 393224 | tf_op jit(solution)/shard_map/ppermute | solution.py:28
  16.7 1.6 %templates_staying.1 = (bf16[6,64,512]{2,1,0:T(8,128)(2,1)S(1)}, f32[32,128]{1,0:T(8,128)S(1)}) custom-call(bf16[6,102400]{1,0:T(8,128)(2,1)S(1)} %copy-done, s32[16,256]{1,0:T(8,128)S(1)} %copy-done.1, s32[48]{0:T(128)S(1)} %copy-done.3, f32[8,128]{1,0:T(8,128)S(1)} %first.1.token_ref), custom_call_target="tpu_custom_call" | custom-call | flops 1024 | bytes 1024 | tf_op jit(solution)/shard_map/templates_staying/pallas_call | solution.py:126
  18.3 1.9 %correlate_staying.1 = (f32[32,2048]{1,0:T(8,128)S(1)}, bf16[32,2048]{1,0:T(8,128)(2,1)S(1)}) custom-call(bf16[6,64,512]{2,1,0:T(8,128)(2,1)S(1)} %get-tuple-element.40.weighted_ref, bf16[6,128,2432]{2,1,0:T(8,128)(2,1)S(1)} %get-tuple-element.28.windows, f32[8,2048]{1,0:T(8,128)S(1)} %get-tuple-element.41.scale), custom_call_target="tpu_custom_call" | custom-call | flops 1024 | bytes 1024 | tf_op jit(solution)/shard_map/correlate_staying/pallas_call | solution.py:261
  20.1 1.3 %collective-permute-start.9 = (bf16[32,2048]{1,0:T(8,128)(2,1)S(1)}, bf16[32,2048]{1,0:T(8,128)(2,1)S(1)}, u32[]{:S(2)}, u32[]{:S(2)}) collective-permute-start(bf16[32,2048]{1,0:T(8,128)(2,1)S(1)} %get-tuple-element.46), channel_id=1, source_target_pairs={{0,1},{1,0},{2,3},{3,2},{4,5},{5,4},{6,7},{7,6},{8,9},{9,8},{10,11... | collective-permute-start | bytes 393224 | tf_op jit(solution)/shard_map/ppermute | solution.py:28
  21.4 0.0 collective-permute-done.6.refs_1_
  21.4 0.0 collective-permute-done.7.refs_2_
  21.4 7.2 %collective-permute-done.8.refs_3_ = bf16[32,2048]{1,0:T(8,128)(2,1)S(1)} collective-permute-done((bf16[32,2048]{1,0:T(8,128)(2,1)S(1)}, bf16[32,2048]{1,0:T(8,128)(2,1)S(1)}, u32[]{:S(2)}, u32[]{:S(2)}) %collective-permute-start.8) | collective-permute-done | bytes 131104 | tf_op jit(solution)/shard_map/ppermute | solution.py:28
  28.6 0.1 added.1.refs_0_
  28.7 0.0 collective-permute-done.9.refs_1_
  28.7 0.7 %scaled.1 = f32[32,2048]{1,0:T(8,128)} custom-call(f32[32,128]{1,0:T(8,128)S(1)} %get-tuple-element.39.factor_ref, f32[32,2048]{1,0:T(8,128)S(1)} %added.1.refs_0_, bf16[32,2048]{1,0:T(8,128)(2,1)S(1)} %collective-permute-done.9.refs_1_), custom_call_target="tpu_custom_call" | custom-call | flops 1024 | bytes 1024 | tf_op jit(solution)/shard_map/scaled/pallas_call | solution.py:317
  (7 shorter events, 0.1 us)
Async XLA Ops:
  0.0 0.7 %copy-start.2 = (bf16[6,512]{1,0:T(8,128)(2,1)S(1)}, bf16[6,512]{1,0:T(8,128)(2,1)}, u32[]{:S(2)}) copy-start(bf16[6,512]{1,0:T(8,128)(2,1)} %refs_0_) | copy-start | bytes 18436
  0.0 3.3 %copy-start.3 = (s32[48]{0:T(128)S(1)}, s32[48]{0:T(128)}, u32[]{:S(2)}) copy-start(s32[48]{0:T(128)} %usable_ref.3) | copy-start | bytes 580
  0.0 3.3 %copy-start.1 = (s32[16,256]{1,0:T(8,128)S(1)}, s32[16,256]{1,0:T(8,128)}, u32[]{:S(2)}) copy-start(s32[16,256]{1,0:T(8,128)} %avail_ref.3) | copy-start | bytes 49156
  0.0 3.3 %copy-start = (bf16[6,102400]{1,0:T(8,128)(2,1)S(1)}, bf16[6,102400]{1,0:T(8,128)(2,1)}, u32[]{:S(2)}) copy-start(bf16[6,102400]{1,0:T(8,128)(2,1)} %raw_ref.3) | copy-start | bytes 3686404
  0.7 5.5 %collective-permute-start.2 = (bf16[6,512]{1,0:T(8,128)(2,1)S(1)}, bf16[6,512]{1,0:T(8,128)(2,1)S(1)}, u32[]{:S(2)}, u32[]{:S(2)}) collective-permute-start(bf16[6,512]{1,0:T(8,128)(2,1)S(1)} %copy-done.2), channel_id=1, source_target_pairs={{0,24},{8,16},{16,8},{24,0},{1,25},{9,17},{17,9},{25,1},{2,26},{10... | collective-permute-start | bytes 18440 | tf_op jit(solution)/shard_map/ppermute | solution.py:28
  2.9 3.3 %collective-permute-start.1 = (bf16[6,512]{1,0:T(8,128)(2,1)S(1)}, bf16[6,512]{1,0:T(8,128)(2,1)S(1)}, u32[]{:S(2)}, u32[]{:S(2)}) collective-permute-start(bf16[6,512]{1,0:T(8,128)(2,1)S(1)} %copy-done.2), channel_id=1, source_target_pairs={{0,16},{8,24},{16,0},{24,8},{1,17},{9,25},{17,1},{25,9},{2,18},{10... | collective-permute-start | bytes 18440 | tf_op jit(solution)/shard_map/ppermute | solution.py:28
  3.1 3.1 %collective-permute-start = (bf16[6,512]{1,0:T(8,128)(2,1)S(1)}, bf16[6,512]{1,0:T(8,128)(2,1)S(1)}, u32[]{:S(2)}, u32[]{:S(2)}) collective-permute-start(bf16[6,512]{1,0:T(8,128)(2,1)S(1)} %copy-done.2), channel_id=1, source_target_pairs={{0,8},{8,0},{16,24},{24,16},{1,9},{9,1},{17,25},{25,17},{2,10},{10... | collective-permute-start | bytes 18440 | tf_op jit(solution)/shard_map/ppermute | solution.py:28
  10.9 2.8 %collective-permute-start.3 = (bf16[32,2048]{1,0:T(8,128)(2,1)S(1)}, bf16[32,2048]{1,0:T(8,128)(2,1)S(1)}, u32[]{:S(2)}, u32[]{:S(2)}) collective-permute-start(bf16[32,2048]{1,0:T(8,128)(2,1)S(1)} %get-tuple-element.33), channel_id=1, source_target_pairs={{0,1},{1,0},{2,3},{3,2},{4,5},{5,4},{6,7},{7,6},{8,9},{9,8},{10,11... | collective-permute-start | bytes 393224 | tf_op jit(solution)/shard_map/ppermute | solution.py:28
  12.7 1.3 %collective-permute-start.4 = (bf16[32,2048]{1,0:T(8,128)(2,1)S(1)}, bf16[32,2048]{1,0:T(8,128)(2,1)S(1)}, u32[]{:S(2)}, u32[]{:S(2)}) collective-permute-start(bf16[32,2048]{1,0:T(8,128)(2,1)S(1)} %get-tuple-element.35), channel_id=1, source_target_pairs={{0,1},{1,0},{2,3},{3,2},{4,5},{5,4},{6,7},{7,6},{8,9},{9,8},{10,11... | collective-permute-start | bytes 393224 | tf_op jit(solution)/shard_map/ppermute | solution.py:28
  12.8 2.7 %collective-permute-start.5 = (bf16[32,2048]{1,0:T(8,128)(2,1)S(1)}, bf16[32,2048]{1,0:T(8,128)(2,1)S(1)}, u32[]{:S(2)}, u32[]{:S(2)}) collective-permute-start(bf16[32,2048]{1,0:T(8,128)(2,1)S(1)} %get-tuple-element.37), channel_id=1, source_target_pairs={{0,1},{1,0},{2,3},{3,2},{4,5},{5,4},{6,7},{7,6},{8,9},{9,8},{10,11... | collective-permute-start | bytes 393224 | tf_op jit(solution)/shard_map/ppermute | solution.py:28
  13.8 7.6 %collective-permute-start.6 = (bf16[32,2048]{1,0:T(8,128)(2,1)S(1)}, bf16[32,2048]{1,0:T(8,128)(2,1)S(1)}, u32[]{:S(2)}, u32[]{:S(2)}) collective-permute-start(bf16[32,2048]{1,0:T(8,128)(2,1)S(1)} %add_convert_fusion.2), channel_id=1, source_target_pairs={{0,4},{1,5},{2,6},{3,7},{4,0},{5,1},{6,2},{7,3},{8,12},{9,13},{10,... | collective-permute-start | bytes 393224 | tf_op jit(solution)/shard_map/ppermute | solution.py:28
  14.1 7.3 %collective-permute-start.7 = (bf16[32,2048]{1,0:T(8,128)(2,1)S(1)}, bf16[32,2048]{1,0:T(8,128)(2,1)S(1)}, u32[]{:S(2)}, u32[]{:S(2)}) collective-permute-start(bf16[32,2048]{1,0:T(8,128)(2,1)S(1)} %add_convert_fusion.1), channel_id=1, source_target_pairs={{0,2},{1,3},{2,0},{3,1},{4,6},{5,7},{6,4},{7,5},{8,10},{9,11},{10,... | collective-permute-start | bytes 393224 | tf_op jit(solution)/shard_map/ppermute | solution.py:28
  15.5 13.1 %collective-permute-start.8 = (bf16[32,2048]{1,0:T(8,128)(2,1)S(1)}, bf16[32,2048]{1,0:T(8,128)(2,1)S(1)}, u32[]{:S(2)}, u32[]{:S(2)}) collective-permute-start(bf16[32,2048]{1,0:T(8,128)(2,1)S(1)} %add_convert_fusion), channel_id=1, source_target_pairs={{0,6},{1,7},{2,4},{3,5},{4,2},{5,3},{6,0},{7,1},{8,14},{9,15},{10,... | collective-permute-start | bytes 393224 | tf_op jit(solution)/shard_map/ppermute | solution.py:28
  20.1 8.5 %collective-permute-start.9 = (bf16[32,2048]{1,0:T(8,128)(2,1)S(1)}, bf16[32,2048]{1,0:T(8,128)(2,1)S(1)}, u32[]{:S(2)}, u32[]{:S(2)}) collective-permute-start(bf16[32,2048]{1,0:T(8,128)(2,1)S(1)} %get-tuple-element.46), channel_id=1, source_target_pairs={{0,1},{1,0},{2,3},{3,2},{4,5},{5,4},{6,7},{7,6},{8,9},{9,8},{10,11... | collective-permute-start | bytes 393224 | tf_op jit(solution)/shard_map/ppermute | solution.py:28

commit v8 on v7

--- a/solution.py
+++ b/solution.py
@@ -134,7 +134,7 @@
         ],
         out_specs=[pl.BlockSpec(memory_space=pltpu.VMEM)] * len(outs),
         scratch_shapes=[
-            pltpu.VMEM((DEPTH_TILES, taken * SUBLANES, LANES), jnp.float32),
+            pltpu.VMEM((DEPTH_TILES, (taken + 1) * SUBLANES, LANES), jnp.float32),
             pltpu.VMEM((channels // COMPONENTS + 1, count, LANES), jnp.float32),
         ],
         compiler_params=pltpu.CompilerParams(vmem_limit_bytes=VMEM_LIMIT),

time: 29.6 us -> 29.6 us (level)
  no operation moved by 1% of the time
where the time goes in v8:
time: 29.6 us; the launch traced here: 29.4 us
  Pallas kernels  11.8 us (40%)
  starting transfers between devices  8.86 us (30%)
  waiting for transfers between devices  7.87 us (27%)
  local copies, waits for them, and re-layouts  0.68 us (2%)
    ppermute x10, starting transfers between devices, exchanged(): return lax.ppermute(array, axis, [(i, i ^ by) for i in range(length)])  8.86 us
    ppermute x10, waiting for transfers between devices, exchanged(): return lax.ppermute(array, axis, [(i, i ^ by) for i in range(length)])  7.87 us
    pallas_call x2, Pallas kernels, correlations(): pl.pallas_call(correlate_kernel, out_shape=[jax.ShapeDtypeStruct((count /...  4.51 us
    pallas_call x2, Pallas kernels, weighted_templates(): pl.pallas_call(functools.partial(template_kernel, shares, stay), out_shap...  4.41 us
    pallas_call x1, Pallas kernels, all_windows(): pl.pallas_call(functools.partial(windows_kernel, blocks), out_shape=(jax....  2.06 us
    pallas_call x1, Pallas kernels, scaled(): pl.pallas_call(scale_kernel, out_shape=jax.ShapeDtypeStruct(terms[0].shap...  0.73 us
    unnamed x8, local copies, waits for them, and re-layouts  0.68 us
  transfers between devices with their start and end apart: 10, of which 3 were waited for; matrix products, arithmetic and copies ran while one was open for 0% of the time, Pallas kernels for 22%

profile of v8, /device:TPU:17, one launch (start us, length us, event | category | flops | bytes accessed | tf_op | source)
XLA Modules:
  0.0 29.4 jit_solution(4222464785019431801)
XLA Ops:
  0.0 0.0 copy-start
  0.0 0.7 %copy-done.2 = bf16[6,512]{1,0:T(8,128)(2,1)S(1)} copy-done((bf16[6,512]{1,0:T(8,128)(2,1)S(1)}, bf16[6,512]{1,0:T(8,128)(2,1)}, u32[]{:S(2)}) %copy-start.2) | copy-done | bytes 6168
  0.7 2.2 %collective-permute-start.2 = (bf16[6,512]{1,0:T(8,128)(2,1)S(1)}, bf16[6,512]{1,0:T(8,128)(2,1)S(1)}, u32[]{:S(2)}, u32[]{:S(2)}) collective-permute-start(bf16[6,512]{1,0:T(8,128)(2,1)S(1)} %copy-done.2), channel_id=1, source_target_pairs={{0,24},{8,16},{16,8},{24,0},{1,25},{9,17},{17,9},{25,1},{2,26},{10... | collective-permute-start | bytes 18440 | tf_op jit(solution)/shard_map/ppermute | solution.py:28
  2.9 0.2 collective-permute-start.1
  3.1 0.3 collective-permute-start
  3.3 0.0 copy-done.3
  3.4 0.0 copy-done.1
  3.4 0.0 copy-done
  3.4 2.8 %templates_leaving.1.weighted_ref = bf16[6,192,512]{2,1,0:T(8,128)(2,1)S(1)} custom-call(bf16[6,102400]{1,0:T(8,128)(2,1)S(1)} %copy-done, s32[16,256]{1,0:T(8,128)S(1)} %copy-done.1, s32[48]{0:T(128)S(1)} %copy-done.3, f32[8,128]{1,0:T(8,128)S(1)} %first.1.token_ref), custom_call_target="tpu_custom_call" | custom-call | flops 1024 | bytes 1024 | tf_op jit(solution)/shard_map/templates_leaving/pallas_call | solution.py:126
  6.2 0.0 collective-permute-done.2.refs_3_
  6.2 0.0 collective-permute-done.1.refs_2_
  6.2 0.0 collective-permute-done.refs_1_
  6.2 2.1 %windows.1 = (bf16[6,128,2432]{2,1,0:T(8,128)(2,1)S(1)}, f32[8,2048]{1,0:T(8,128)S(1)}) custom-call(bf16[6,512]{1,0:T(8,128)(2,1)S(1)} %copy-done.2, bf16[6,512]{1,0:T(8,128)(2,1)S(1)} %collective-permute-done.refs_1_, bf16[6,512]{1,0:T(8,128)(2,1)S(1)} %collective-permute-done.1.refs_2_, bf16[6,512]{1,0:T(8,128)(2,1)S(1)} %collective-permute-done.2.refs_3_), custom_call_target="tpu_custom_call" | custom-call | flops 1024 | bytes 1024 | tf_op jit(solution)/shard_map/windows/pallas_call | solution.py:200
  8.3 2.6 %correlate_leaving.1 = (f32[32,2048]{1,0:T(8,128)S(1)}, f32[32,2048]{1,0:T(8,128)S(1)}, f32[32,2048]{1,0:T(8,128)S(1)}, bf16[32,2048]{1,0:T(8,128)(2,1)S(1)}, bf...) custom-call(bf16[6,192,512]{2,1,0:T(8,128)(2,1)S(1)} %templates_leaving.1.weighted_ref, ...), custom_call_target="tpu_custom_call" | custom-call | flops 1024 | bytes 1024 | tf_op jit(solution)/shard_map/correlate_leaving/pallas_call | solution.py:261
  10.9 1.8 %collective-permute-start.3 = (bf16[32,2048]{1,0:T(8,128)(2,1)S(1)}, bf16[32,2048]{1,0:T(8,128)(2,1)S(1)}, u32[]{:S(2)}, u32[]{:S(2)}) collective-permute-start(bf16[32,2048]{1,0:T(8,128)(2,1)S(1)} %get-tuple-element.33), channel_id=1, source_target_pairs={{0,1},{1,0},{2,3},{3,2},{4,5},{5,4},{6,7},{7,6},{8,9},{9,8},{10,11... | collective-permute-start | bytes 393224 | tf_op jit(solution)/shard_map/ppermute | solution.py:28
  12.7 0.1 collective-permute-start.4
  12.8 0.4 %collective-permute-start.5 = (bf16[32,2048]{1,0:T(8,128)(2,1)S(1)}, bf16[32,2048]{1,0:T(8,128)(2,1)S(1)}, u32[]{:S(2)}, u32[]{:S(2)}) collective-permute-start(bf16[32,2048]{1,0:T(8,128)(2,1)S(1)} %get-tuple-element.37), channel_id=1, source_target_pairs={{0,1},{1,0},{2,3},{3,2},{4,5},{5,4},{6,7},{7,6},{8,9},{9,8},{10,11... | collective-permute-start | bytes 393224 | tf_op jit(solution)/shard_map/ppermute | solution.py:28
  13.2 0.5 %collective-permute-done.3 = bf16[32,2048]{1,0:T(8,128)(2,1)S(1)} collective-permute-done((bf16[32,2048]{1,0:T(8,128)(2,1)S(1)}, bf16[32,2048]{1,0:T(8,128)(2,1)S(1)}, u32[]{:S(2)}, u32[]{:S(2)}) %collective-permute-start.3) | collective-permute-done | bytes 131104 | tf_op jit(solution)/shard_map/ppermute | solution.py:28
  13.8 0.1 collective-permute-start.6
  13.9 0.2 collective-permute-done.4
  14.1 1.4 %collective-permute-start.7 = (bf16[32,2048]{1,0:T(8,128)(2,1)S(1)}, bf16[32,2048]{1,0:T(8,128)(2,1)S(1)}, u32[]{:S(2)}, u32[]{:S(2)}) collective-permute-start(bf16[32,2048]{1,0:T(8,128)(2,1)S(1)} %add_convert_fusion.1), channel_id=1, source_target_pairs={{0,2},{1,3},{2,0},{3,1},{4,6},{5,7},{6,4},{7,5},{8,10},{9,11},{10,... | collective-permute-start | bytes 393224 | tf_op jit(solution)/shard_map/ppermute | solution.py:28
  15.5 0.0 collective-permute-done.5
  15.5 1.2 %collective-permute-start.8 = (bf16[32,2048]{1,0:T(8,128)(2,1)S(1)}, bf16[32,2048]{1,0:T(8,128)(2,1)S(1)}, u32[]{:S(2)}, u32[]{:S(2)}) collective-permute-start(bf16[32,2048]{1,0:T(8,128)(2,1)S(1)} %add_convert_fusion), channel_id=1, source_target_pairs={{0,6},{1,7},{2,4},{3,5},{4,2},{5,3},{6,0},{7,1},{8,14},{9,15},{10,... | collective-permute-start | bytes 393224 | tf_op jit(solution)/shard_map/ppermute | solution.py:28
  16.7 1.6 %templates_staying.1 = (bf16[6,64,512]{2,1,0:T(8,128)(2,1)S(1)}, f32[32,128]{1,0:T(8,128)S(1)}) custom-call(bf16[6,102400]{1,0:T(8,128)(2,1)S(1)} %copy-done, s32[16,256]{1,0:T(8,128)S(1)} %copy-done.1, s32[48]{0:T(128)S(1)} %copy-done.3, f32[8,128]{1,0:T(8,128)S(1)} %first.1.token_ref), custom_call_target="tpu_custom_call" | custom-call | flops 1024 | bytes 1024 | tf_op jit(solution)/shard_map/templates_staying/pallas_call | solution.py:126
  18.3 1.9 %correlate_staying.1 = (f32[32,2048]{1,0:T(8,128)S(1)}, bf16[32,2048]{1,0:T(8,128)(2,1)S(1)}) custom-call(bf16[6,64,512]{2,1,0:T(8,128)(2,1)S(1)} %get-tuple-element.40.weighted_ref, bf16[6,128,2432]{2,1,0:T(8,128)(2,1)S(1)} %get-tuple-element.28.windows, f32[8,2048]{1,0:T(8,128)S(1)} %get-tuple-element.41.scale), custom_call_target="tpu_custom_call" | custom-call | flops 1024 | bytes 1024 | tf_op jit(solution)/shard_map/correlate_staying/pallas_call | solution.py:261
  20.2 1.3 %collective-permute-start.9 = (bf16[32,2048]{1,0:T(8,128)(2,1)S(1)}, bf16[32,2048]{1,0:T(8,128)(2,1)S(1)}, u32[]{:S(2)}, u32[]{:S(2)}) collective-permute-start(bf16[32,2048]{1,0:T(8,128)(2,1)S(1)} %get-tuple-element.46), channel_id=1, source_target_pairs={{0,1},{1,0},{2,3},{3,2},{4,5},{5,4},{6,7},{7,6},{8,9},{9,8},{10,11... | collective-permute-start | bytes 393224 | tf_op jit(solution)/shard_map/ppermute | solution.py:28
  21.4 0.0 collective-permute-done.6.refs_1_
  21.4 0.0 collective-permute-done.7.refs_2_
  21.4 7.2 %collective-permute-done.8.refs_3_ = bf16[32,2048]{1,0:T(8,128)(2,1)S(1)} collective-permute-done((bf16[32,2048]{1,0:T(8,128)(2,1)S(1)}, bf16[32,2048]{1,0:T(8,128)(2,1)S(1)}, u32[]{:S(2)}, u32[]{:S(2)}) %collective-permute-start.8) | collective-permute-done | bytes 131104 | tf_op jit(solution)/shard_map/ppermute | solution.py:28
  28.6 0.1 added.1.refs_0_
  28.7 0.0 collective-permute-done.9.refs_1_
  28.7 0.7 %scaled.1 = f32[32,2048]{1,0:T(8,128)} custom-call(f32[32,128]{1,0:T(8,128)S(1)} %get-tuple-element.39.factor_ref, f32[32,2048]{1,0:T(8,128)S(1)} %added.1.refs_0_, bf16[32,2048]{1,0:T(8,128)(2,1)S(1)} %collective-permute-done.9.refs_1_), custom_call_target="tpu_custom_call" | custom-call | flops 1024 | bytes 1024 | tf_op jit(solution)/shard_map/scaled/pallas_call | solution.py:317
  (7 shorter events, 0.1 us)
Async XLA Ops:
  0.0 0.7 %copy-start.2 = (bf16[6,512]{1,0:T(8,128)(2,1)S(1)}, bf16[6,512]{1,0:T(8,128)(2,1)}, u32[]{:S(2)}) copy-start(bf16[6,512]{1,0:T(8,128)(2,1)} %refs_0_) | copy-start | bytes 18436
  0.0 3.3 %copy-start.3 = (s32[48]{0:T(128)S(1)}, s32[48]{0:T(128)}, u32[]{:S(2)}) copy-start(s32[48]{0:T(128)} %usable_ref.3) | copy-start | bytes 580
  0.0 3.3 %copy-start.1 = (s32[16,256]{1,0:T(8,128)S(1)}, s32[16,256]{1,0:T(8,128)}, u32[]{:S(2)}) copy-start(s32[16,256]{1,0:T(8,128)} %avail_ref.3) | copy-start | bytes 49156
  0.0 3.3 %copy-start = (bf16[6,102400]{1,0:T(8,128)(2,1)S(1)}, bf16[6,102400]{1,0:T(8,128)(2,1)}, u32[]{:S(2)}) copy-start(bf16[6,102400]{1,0:T(8,128)(2,1)} %raw_ref.3) | copy-start | bytes 3686404
  0.7 5.5 %collective-permute-start.2 = (bf16[6,512]{1,0:T(8,128)(2,1)S(1)}, bf16[6,512]{1,0:T(8,128)(2,1)S(1)}, u32[]{:S(2)}, u32[]{:S(2)}) collective-permute-start(bf16[6,512]{1,0:T(8,128)(2,1)S(1)} %copy-done.2), channel_id=1, source_target_pairs={{0,24},{8,16},{16,8},{24,0},{1,25},{9,17},{17,9},{25,1},{2,26},{10... | collective-permute-start | bytes 18440 | tf_op jit(solution)/shard_map/ppermute | solution.py:28
  2.9 3.3 %collective-permute-start.1 = (bf16[6,512]{1,0:T(8,128)(2,1)S(1)}, bf16[6,512]{1,0:T(8,128)(2,1)S(1)}, u32[]{:S(2)}, u32[]{:S(2)}) collective-permute-start(bf16[6,512]{1,0:T(8,128)(2,1)S(1)} %copy-done.2), channel_id=1, source_target_pairs={{0,16},{8,24},{16,0},{24,8},{1,17},{9,25},{17,1},{25,9},{2,18},{10... | collective-permute-start | bytes 18440 | tf_op jit(solution)/shard_map/ppermute | solution.py:28
  3.1 3.1 %collective-permute-start = (bf16[6,512]{1,0:T(8,128)(2,1)S(1)}, bf16[6,512]{1,0:T(8,128)(2,1)S(1)}, u32[]{:S(2)}, u32[]{:S(2)}) collective-permute-start(bf16[6,512]{1,0:T(8,128)(2,1)S(1)} %copy-done.2), channel_id=1, source_target_pairs={{0,8},{8,0},{16,24},{24,16},{1,9},{9,1},{17,25},{25,17},{2,10},{10... | collective-permute-start | bytes 18440 | tf_op jit(solution)/shard_map/ppermute | solution.py:28
  10.9 2.8 %collective-permute-start.3 = (bf16[32,2048]{1,0:T(8,128)(2,1)S(1)}, bf16[32,2048]{1,0:T(8,128)(2,1)S(1)}, u32[]{:S(2)}, u32[]{:S(2)}) collective-permute-start(bf16[32,2048]{1,0:T(8,128)(2,1)S(1)} %get-tuple-element.33), channel_id=1, source_target_pairs={{0,1},{1,0},{2,3},{3,2},{4,5},{5,4},{6,7},{7,6},{8,9},{9,8},{10,11... | collective-permute-start | bytes 393224 | tf_op jit(solution)/shard_map/ppermute | solution.py:28
  12.7 1.3 %collective-permute-start.4 = (bf16[32,2048]{1,0:T(8,128)(2,1)S(1)}, bf16[32,2048]{1,0:T(8,128)(2,1)S(1)}, u32[]{:S(2)}, u32[]{:S(2)}) collective-permute-start(bf16[32,2048]{1,0:T(8,128)(2,1)S(1)} %get-tuple-element.35), channel_id=1, source_target_pairs={{0,1},{1,0},{2,3},{3,2},{4,5},{5,4},{6,7},{7,6},{8,9},{9,8},{10,11... | collective-permute-start | bytes 393224 | tf_op jit(solution)/shard_map/ppermute | solution.py:28
  12.8 2.7 %collective-permute-start.5 = (bf16[32,2048]{1,0:T(8,128)(2,1)S(1)}, bf16[32,2048]{1,0:T(8,128)(2,1)S(1)}, u32[]{:S(2)}, u32[]{:S(2)}) collective-permute-start(bf16[32,2048]{1,0:T(8,128)(2,1)S(1)} %get-tuple-element.37), channel_id=1, source_target_pairs={{0,1},{1,0},{2,3},{3,2},{4,5},{5,4},{6,7},{7,6},{8,9},{9,8},{10,11... | collective-permute-start | bytes 393224 | tf_op jit(solution)/shard_map/ppermute | solution.py:28
  13.8 7.6 %collective-permute-start.6 = (bf16[32,2048]{1,0:T(8,128)(2,1)S(1)}, bf16[32,2048]{1,0:T(8,128)(2,1)S(1)}, u32[]{:S(2)}, u32[]{:S(2)}) collective-permute-start(bf16[32,2048]{1,0:T(8,128)(2,1)S(1)} %add_convert_fusion.2), channel_id=1, source_target_pairs={{0,4},{1,5},{2,6},{3,7},{4,0},{5,1},{6,2},{7,3},{8,12},{9,13},{10,... | collective-permute-start | bytes 393224 | tf_op jit(solution)/shard_map/ppermute | solution.py:28
  14.1 7.3 %collective-permute-start.7 = (bf16[32,2048]{1,0:T(8,128)(2,1)S(1)}, bf16[32,2048]{1,0:T(8,128)(2,1)S(1)}, u32[]{:S(2)}, u32[]{:S(2)}) collective-permute-start(bf16[32,2048]{1,0:T(8,128)(2,1)S(1)} %add_convert_fusion.1), channel_id=1, source_target_pairs={{0,2},{1,3},{2,0},{3,1},{4,6},{5,7},{6,4},{7,5},{8,10},{9,11},{10,... | collective-permute-start | bytes 393224 | tf_op jit(solution)/shard_map/ppermute | solution.py:28
  15.5 13.1 %collective-permute-start.8 = (bf16[32,2048]{1,0:T(8,128)(2,1)S(1)}, bf16[32,2048]{1,0:T(8,128)(2,1)S(1)}, u32[]{:S(2)}, u32[]{:S(2)}) collective-permute-start(bf16[32,2048]{1,0:T(8,128)(2,1)S(1)} %add_convert_fusion), channel_id=1, source_target_pairs={{0,6},{1,7},{2,4},{3,5},{4,2},{5,3},{6,0},{7,1},{8,14},{9,15},{10,... | collective-permute-start | bytes 393224 | tf_op jit(solution)/shard_map/ppermute | solution.py:28
  20.2 8.5 %collective-permute-start.9 = (bf16[32,2048]{1,0:T(8,128)(2,1)S(1)}, bf16[32,2048]{1,0:T(8,128)(2,1)S(1)}, u32[]{:S(2)}, u32[]{:S(2)}) collective-permute-start(bf16[32,2048]{1,0:T(8,128)(2,1)S(1)} %get-tuple-element.46), channel_id=1, source_target_pairs={{0,1},{1,0},{2,3},{3,2},{4,5},{5,4},{6,7},{7,6},{8,9},{9,8},{10,11... | collective-permute-start | bytes 393224 | tf_op jit(solution)/shard_map/ppermute | solution.py:28

commit v9 on v8

--- a/solution.py
+++ b/solution.py
@@ -190,7 +190,7 @@
             windows[channel, row : row + 2 * SUBLANES, :] = pair[:, row : row + base]
         return carry
 
-    lax.fori_loop(0, channels, one_channel, 0, unroll=3)
+    lax.fori_loop(0, channels, one_channel, 0, unroll=6)
 
 
 def all_windows(segments, name):

time: 29.6 us -> 29.7 us (level)
  transfers between devices with their start and end apart: 10 -> 10, of which waited for: 3 -> 3; matrix products, arithmetic and copies ran while one was open for 0% -> 0% of each run, Pallas kernels for 22% -> 21%
where the time goes in v9:
time: 29.7 us; the launch traced here: 29.5 us
  Pallas kernels  11.8 us (40%)
  starting transfers between devices  8.91 us (30%)
  waiting for transfers between devices  7.87 us (26%)
  local copies, waits for them, and re-layouts  0.68 us (2%)
    ppermute x10, starting transfers between devices, exchanged(): return lax.ppermute(array, axis, [(i, i ^ by) for i in range(length)])  8.91 us
    ppermute x10, waiting for transfers between devices, exchanged(): return lax.ppermute(array, axis, [(i, i ^ by) for i in range(length)])  7.87 us
    pallas_call x2, Pallas kernels, correlations(): pl.pallas_call(correlate_kernel, out_shape=[jax.ShapeDtypeStruct((count /...  4.47 us
    pallas_call x2, Pallas kernels, weighted_templates(): pl.pallas_call(functools.partial(template_kernel, shares, stay), out_shap...  4.41 us
    pallas_call x1, Pallas kernels, all_windows(): pl.pallas_call(functools.partial(windows_kernel, blocks), out_shape=(jax....  2.11 us
    pallas_call x1, Pallas kernels, scaled(): pl.pallas_call(scale_kernel, out_shape=jax.ShapeDtypeStruct(terms[0].shap...  0.73 us
    unnamed x8, local copies, waits for them, and re-layouts  0.68 us
  transfers between devices with their start and end apart: 10, of which 3 were waited for; matrix products, arithmetic and copies ran while one was open for 0% of the time, Pallas kernels for 21%

profile of v9, /device:TPU:17, one launch (start us, length us, event | category | flops | bytes accessed | tf_op | source)
XLA Modules:
  0.0 29.5 jit_solution(15231822153247286856)
XLA Ops:
  0.0 0.0 copy-start
  0.0 0.7 %copy-done.2 = bf16[6,512]{1,0:T(8,128)(2,1)S(1)} copy-done((bf16[6,512]{1,0:T(8,128)(2,1)S(1)}, bf16[6,512]{1,0:T(8,128)(2,1)}, u32[]{:S(2)}) %copy-start.2) | copy-done | bytes 6168
  0.7 2.2 %collective-permute-start.2 = (bf16[6,512]{1,0:T(8,128)(2,1)S(1)}, bf16[6,512]{1,0:T(8,128)(2,1)S(1)}, u32[]{:S(2)}, u32[]{:S(2)}) collective-permute-start(bf16[6,512]{1,0:T(8,128)(2,1)S(1)} %copy-done.2), channel_id=1, source_target_pairs={{0,24},{8,16},{16,8},{24,0},{1,25},{9,17},{17,9},{25,1},{2,26},{10... | collective-permute-start | bytes 18440 | tf_op jit(solution)/shard_map/ppermute | solution.py:28
  2.9 0.2 collective-permute-start.1
  3.1 0.3 collective-permute-start
  3.3 0.0 copy-done.3
  3.4 0.0 copy-done.1
  3.4 0.0 copy-done
  3.4 2.8 %templates_leaving.1.weighted_ref = bf16[6,192,512]{2,1,0:T(8,128)(2,1)S(1)} custom-call(bf16[6,102400]{1,0:T(8,128)(2,1)S(1)} %copy-done, s32[16,256]{1,0:T(8,128)S(1)} %copy-done.1, s32[48]{0:T(128)S(1)} %copy-done.3, f32[8,128]{1,0:T(8,128)S(1)} %first.1.token_ref), custom_call_target="tpu_custom_call" | custom-call | flops 1024 | bytes 1024 | tf_op jit(solution)/shard_map/templates_leaving/pallas_call | solution.py:126
  6.2 0.0 collective-permute-done.2.refs_3_
  6.2 0.0 collective-permute-done.1.refs_2_
  6.2 0.0 collective-permute-done.refs_1_
  6.2 2.1 %windows.1 = (bf16[6,128,2432]{2,1,0:T(8,128)(2,1)S(1)}, f32[8,2048]{1,0:T(8,128)S(1)}) custom-call(bf16[6,512]{1,0:T(8,128)(2,1)S(1)} %copy-done.2, bf16[6,512]{1,0:T(8,128)(2,1)S(1)} %collective-permute-done.refs_1_, bf16[6,512]{1,0:T(8,128)(2,1)S(1)} %collective-permute-done.1.refs_2_, bf16[6,512]{1,0:T(8,128)(2,1)S(1)} %collective-permute-done.2.refs_3_), custom_call_target="tpu_custom_call" | custom-call | flops 1024 | bytes 1024 | tf_op jit(solution)/shard_map/windows/pallas_call | solution.py:200
  8.3 2.6 %correlate_leaving.1 = (f32[32,2048]{1,0:T(8,128)S(1)}, f32[32,2048]{1,0:T(8,128)S(1)}, f32[32,2048]{1,0:T(8,128)S(1)}, bf16[32,2048]{1,0:T(8,128)(2,1)S(1)}, bf...) custom-call(bf16[6,192,512]{2,1,0:T(8,128)(2,1)S(1)} %templates_leaving.1.weighted_ref, ...), custom_call_target="tpu_custom_call" | custom-call | flops 1024 | bytes 1024 | tf_op jit(solution)/shard_map/correlate_leaving/pallas_call | solution.py:261
  11.0 1.8 %collective-permute-start.3 = (bf16[32,2048]{1,0:T(8,128)(2,1)S(1)}, bf16[32,2048]{1,0:T(8,128)(2,1)S(1)}, u32[]{:S(2)}, u32[]{:S(2)}) collective-permute-start(bf16[32,2048]{1,0:T(8,128)(2,1)S(1)} %get-tuple-element.33), channel_id=1, source_target_pairs={{0,1},{1,0},{2,3},{3,2},{4,5},{5,4},{6,7},{7,6},{8,9},{9,8},{10,11... | collective-permute-start | bytes 393224 | tf_op jit(solution)/shard_map/ppermute | solution.py:28
  12.8 0.1 collective-permute-start.4
  12.9 0.4 %collective-permute-start.5 = (bf16[32,2048]{1,0:T(8,128)(2,1)S(1)}, bf16[32,2048]{1,0:T(8,128)(2,1)S(1)}, u32[]{:S(2)}, u32[]{:S(2)}) collective-permute-start(bf16[32,2048]{1,0:T(8,128)(2,1)S(1)} %get-tuple-element.37), channel_id=1, source_target_pairs={{0,1},{1,0},{2,3},{3,2},{4,5},{5,4},{6,7},{7,6},{8,9},{9,8},{10,11... | collective-permute-start | bytes 393224 | tf_op jit(solution)/shard_map/ppermute | solution.py:28
  13.3 0.5 %collective-permute-done.3 = bf16[32,2048]{1,0:T(8,128)(2,1)S(1)} collective-permute-done((bf16[32,2048]{1,0:T(8,128)(2,1)S(1)}, bf16[32,2048]{1,0:T(8,128)(2,1)S(1)}, u32[]{:S(2)}, u32[]{:S(2)}) %collective-permute-start.3) | collective-permute-done | bytes 131104 | tf_op jit(solution)/shard_map/ppermute | solution.py:28
  13.8 0.1 collective-permute-start.6
  13.9 0.2 collective-permute-done.4
  14.2 1.4 %collective-permute-start.7 = (bf16[32,2048]{1,0:T(8,128)(2,1)S(1)}, bf16[32,2048]{1,0:T(8,128)(2,1)S(1)}, u32[]{:S(2)}, u32[]{:S(2)}) collective-permute-start(bf16[32,2048]{1,0:T(8,128)(2,1)S(1)} %add_convert_fusion.1), channel_id=1, source_target_pairs={{0,2},{1,3},{2,0},{3,1},{4,6},{5,7},{6,4},{7,5},{8,10},{9,11},{10,... | collective-permute-start | bytes 393224 | tf_op jit(solution)/shard_map/ppermute | solution.py:28
  15.5 0.0 collective-permute-done.5
  15.6 1.2 %collective-permute-start.8 = (bf16[32,2048]{1,0:T(8,128)(2,1)S(1)}, bf16[32,2048]{1,0:T(8,128)(2,1)S(1)}, u32[]{:S(2)}, u32[]{:S(2)}) collective-permute-start(bf16[32,2048]{1,0:T(8,128)(2,1)S(1)} %add_convert_fusion), channel_id=1, source_target_pairs={{0,6},{1,7},{2,4},{3,5},{4,2},{5,3},{6,0},{7,1},{8,14},{9,15},{10,... | collective-permute-start | bytes 393224 | tf_op jit(solution)/shard_map/ppermute | solution.py:28
  16.7 1.6 %templates_staying.1 = (bf16[6,64,512]{2,1,0:T(8,128)(2,1)S(1)}, f32[32,128]{1,0:T(8,128)S(1)}) custom-call(bf16[6,102400]{1,0:T(8,128)(2,1)S(1)} %copy-done, s32[16,256]{1,0:T(8,128)S(1)} %copy-done.1, s32[48]{0:T(128)S(1)} %copy-done.3, f32[8,128]{1,0:T(8,128)S(1)} %first.1.token_ref), custom_call_target="tpu_custom_call" | custom-call | flops 1024 | bytes 1024 | tf_op jit(solution)/shard_map/templates_staying/pallas_call | solution.py:126
  18.3 1.8 %correlate_staying.1 = (f32[32,2048]{1,0:T(8,128)S(1)}, bf16[32,2048]{1,0:T(8,128)(2,1)S(1)}) custom-call(bf16[6,64,512]{2,1,0:T(8,128)(2,1)S(1)} %get-tuple-element.40.weighted_ref, bf16[6,128,2432]{2,1,0:T(8,128)(2,1)S(1)} %get-tuple-element.28.windows, f32[8,2048]{1,0:T(8,128)S(1)} %get-tuple-element.41.scale), custom_call_target="tpu_custom_call" | custom-call | flops 1024 | bytes 1024 | tf_op jit(solution)/shard_map/correlate_staying/pallas_call | solution.py:261
  20.2 1.3 %collective-permute-start.9 = (bf16[32,2048]{1,0:T(8,128)(2,1)S(1)}, bf16[32,2048]{1,0:T(8,128)(2,1)S(1)}, u32[]{:S(2)}, u32[]{:S(2)}) collective-permute-start(bf16[32,2048]{1,0:T(8,128)(2,1)S(1)} %get-tuple-element.46), channel_id=1, source_target_pairs={{0,1},{1,0},{2,3},{3,2},{4,5},{5,4},{6,7},{7,6},{8,9},{9,8},{10,11... | collective-permute-start | bytes 393224 | tf_op jit(solution)/shard_map/ppermute | solution.py:28
  21.5 0.0 collective-permute-done.6.refs_1_
  21.5 0.0 collective-permute-done.7.refs_2_
  21.5 7.2 %collective-permute-done.8.refs_3_ = bf16[32,2048]{1,0:T(8,128)(2,1)S(1)} collective-permute-done((bf16[32,2048]{1,0:T(8,128)(2,1)S(1)}, bf16[32,2048]{1,0:T(8,128)(2,1)S(1)}, u32[]{:S(2)}, u32[]{:S(2)}) %collective-permute-start.8) | collective-permute-done | bytes 131104 | tf_op jit(solution)/shard_map/ppermute | solution.py:28
  28.7 0.1 added.1.refs_0_
  28.7 0.0 collective-permute-done.9.refs_1_
  28.7 0.7 %scaled.1 = f32[32,2048]{1,0:T(8,128)} custom-call(f32[32,128]{1,0:T(8,128)S(1)} %get-tuple-element.39.factor_ref, f32[32,2048]{1,0:T(8,128)S(1)} %added.1.refs_0_, bf16[32,2048]{1,0:T(8,128)(2,1)S(1)} %collective-permute-done.9.refs_1_), custom_call_target="tpu_custom_call" | custom-call | flops 1024 | bytes 1024 | tf_op jit(solution)/shard_map/scaled/pallas_call | solution.py:317
  (7 shorter events, 0.1 us)
Async XLA Ops:
  0.0 0.7 %copy-start.2 = (bf16[6,512]{1,0:T(8,128)(2,1)S(1)}, bf16[6,512]{1,0:T(8,128)(2,1)}, u32[]{:S(2)}) copy-start(bf16[6,512]{1,0:T(8,128)(2,1)} %refs_0_) | copy-start | bytes 18436
  0.0 3.3 %copy-start.3 = (s32[48]{0:T(128)S(1)}, s32[48]{0:T(128)}, u32[]{:S(2)}) copy-start(s32[48]{0:T(128)} %usable_ref.3) | copy-start | bytes 580
  0.0 3.3 %copy-start.1 = (s32[16,256]{1,0:T(8,128)S(1)}, s32[16,256]{1,0:T(8,128)}, u32[]{:S(2)}) copy-start(s32[16,256]{1,0:T(8,128)} %avail_ref.3) | copy-start | bytes 49156
  0.0 3.3 %copy-start = (bf16[6,102400]{1,0:T(8,128)(2,1)S(1)}, bf16[6,102400]{1,0:T(8,128)(2,1)}, u32[]{:S(2)}) copy-start(bf16[6,102400]{1,0:T(8,128)(2,1)} %raw_ref.3) | copy-start | bytes 3686404
  0.7 5.5 %collective-permute-start.2 = (bf16[6,512]{1,0:T(8,128)(2,1)S(1)}, bf16[6,512]{1,0:T(8,128)(2,1)S(1)}, u32[]{:S(2)}, u32[]{:S(2)}) collective-permute-start(bf16[6,512]{1,0:T(8,128)(2,1)S(1)} %copy-done.2), channel_id=1, source_target_pairs={{0,24},{8,16},{16,8},{24,0},{1,25},{9,17},{17,9},{25,1},{2,26},{10... | collective-permute-start | bytes 18440 | tf_op jit(solution)/shard_map/ppermute | solution.py:28
  2.9 3.3 %collective-permute-start.1 = (bf16[6,512]{1,0:T(8,128)(2,1)S(1)}, bf16[6,512]{1,0:T(8,128)(2,1)S(1)}, u32[]{:S(2)}, u32[]{:S(2)}) collective-permute-start(bf16[6,512]{1,0:T(8,128)(2,1)S(1)} %copy-done.2), channel_id=1, source_target_pairs={{0,16},{8,24},{16,0},{24,8},{1,17},{9,25},{17,1},{25,9},{2,18},{10... | collective-permute-start | bytes 18440 | tf_op jit(solution)/shard_map/ppermute | solution.py:28
  3.1 3.1 %collective-permute-start = (bf16[6,512]{1,0:T(8,128)(2,1)S(1)}, bf16[6,512]{1,0:T(8,128)(2,1)S(1)}, u32[]{:S(2)}, u32[]{:S(2)}) collective-permute-start(bf16[6,512]{1,0:T(8,128)(2,1)S(1)} %copy-done.2), channel_id=1, source_target_pairs={{0,8},{8,0},{16,24},{24,16},{1,9},{9,1},{17,25},{25,17},{2,10},{10... | collective-permute-start | bytes 18440 | tf_op jit(solution)/shard_map/ppermute | solution.py:28
  11.0 2.8 %collective-permute-start.3 = (bf16[32,2048]{1,0:T(8,128)(2,1)S(1)}, bf16[32,2048]{1,0:T(8,128)(2,1)S(1)}, u32[]{:S(2)}, u32[]{:S(2)}) collective-permute-start(bf16[32,2048]{1,0:T(8,128)(2,1)S(1)} %get-tuple-element.33), channel_id=1, source_target_pairs={{0,1},{1,0},{2,3},{3,2},{4,5},{5,4},{6,7},{7,6},{8,9},{9,8},{10,11... | collective-permute-start | bytes 393224 | tf_op jit(solution)/shard_map/ppermute | solution.py:28
  12.8 1.3 %collective-permute-start.4 = (bf16[32,2048]{1,0:T(8,128)(2,1)S(1)}, bf16[32,2048]{1,0:T(8,128)(2,1)S(1)}, u32[]{:S(2)}, u32[]{:S(2)}) collective-permute-start(bf16[32,2048]{1,0:T(8,128)(2,1)S(1)} %get-tuple-element.35), channel_id=1, source_target_pairs={{0,1},{1,0},{2,3},{3,2},{4,5},{5,4},{6,7},{7,6},{8,9},{9,8},{10,11... | collective-permute-start | bytes 393224 | tf_op jit(solution)/shard_map/ppermute | solution.py:28
  12.9 2.7 %collective-permute-start.5 = (bf16[32,2048]{1,0:T(8,128)(2,1)S(1)}, bf16[32,2048]{1,0:T(8,128)(2,1)S(1)}, u32[]{:S(2)}, u32[]{:S(2)}) collective-permute-start(bf16[32,2048]{1,0:T(8,128)(2,1)S(1)} %get-tuple-element.37), channel_id=1, source_target_pairs={{0,1},{1,0},{2,3},{3,2},{4,5},{5,4},{6,7},{7,6},{8,9},{9,8},{10,11... | collective-permute-start | bytes 393224 | tf_op jit(solution)/shard_map/ppermute | solution.py:28
  13.8 7.7 %collective-permute-start.6 = (bf16[32,2048]{1,0:T(8,128)(2,1)S(1)}, bf16[32,2048]{1,0:T(8,128)(2,1)S(1)}, u32[]{:S(2)}, u32[]{:S(2)}) collective-permute-start(bf16[32,2048]{1,0:T(8,128)(2,1)S(1)} %add_convert_fusion.2), channel_id=1, source_target_pairs={{0,4},{1,5},{2,6},{3,7},{4,0},{5,1},{6,2},{7,3},{8,12},{9,13},{10,... | collective-permute-start | bytes 393224 | tf_op jit(solution)/shard_map/ppermute | solution.py:28
  14.2 7.3 %collective-permute-start.7 = (bf16[32,2048]{1,0:T(8,128)(2,1)S(1)}, bf16[32,2048]{1,0:T(8,128)(2,1)S(1)}, u32[]{:S(2)}, u32[]{:S(2)}) collective-permute-start(bf16[32,2048]{1,0:T(8,128)(2,1)S(1)} %add_convert_fusion.1), channel_id=1, source_target_pairs={{0,2},{1,3},{2,0},{3,1},{4,6},{5,7},{6,4},{7,5},{8,10},{9,11},{10,... | collective-permute-start | bytes 393224 | tf_op jit(solution)/shard_map/ppermute | solution.py:28
  15.6 13.1 %collective-permute-start.8 = (bf16[32,2048]{1,0:T(8,128)(2,1)S(1)}, bf16[32,2048]{1,0:T(8,128)(2,1)S(1)}, u32[]{:S(2)}, u32[]{:S(2)}) collective-permute-start(bf16[32,2048]{1,0:T(8,128)(2,1)S(1)} %add_convert_fusion), channel_id=1, source_target_pairs={{0,6},{1,7},{2,4},{3,5},{4,2},{5,3},{6,0},{7,1},{8,14},{9,15},{10,... | collective-permute-start | bytes 393224 | tf_op jit(solution)/shard_map/ppermute | solution.py:28
  20.2 8.5 %collective-permute-start.9 = (bf16[32,2048]{1,0:T(8,128)(2,1)S(1)}, bf16[32,2048]{1,0:T(8,128)(2,1)S(1)}, u32[]{:S(2)}, u32[]{:S(2)}) collective-permute-start(bf16[32,2048]{1,0:T(8,128)(2,1)S(1)} %get-tuple-element.46), channel_id=1, source_target_pairs={{0,1},{1,0},{2,3},{3,2},{4,5},{5,4},{6,7},{7,6},{8,9},{9,8},{10,11... | collective-permute-start | bytes 393224 | tf_op jit(solution)/shard_map/ppermute | solution.py:28
